TPU v7x, 32 devices: a whole 2x2x4 slice. The times are simulated.
32 devices in a mesh: layer: 4 (over y, x), dp: 8 (over z, core).
Axes of the slice: x: 2, y: 2, z: 4, core: 2. Of those that a mesh axis runs over, the one named last changes fastest.
Arguments:
- states: bfloat16 [8, 16, 32, 32, 256], P('layer', 'dp'), may hold values from -6 to 6
- slopes: bfloat16 [8, 16, 32, 32, 256], P('layer', 'dp'), may hold values from 0.099609375 to 1
- kernels: bfloat16 [8, 9, 256, 256], P('layer'), may hold values from -0.125 to 0.125
- guess: float32 [8, 16, 32, 32, 256], P('layer', 'dp'), may hold values from -6 to 6
Outputs:
- lower_adjoint: float32 [4, 16, 32, 32, 256], P('layer', 'dp')
- kernel_grad: float32 [8, 9, 256, 256], P('layer', None, 'dp')
All inputs are finite; a program needn't handle non-finite values.
Results may differ from a plain program's by a relative error of at most 0.005.
Values sent between devices are 32-bit elements; how exact they have to be, the bound alone decides.
No kernel may reach another device: no remote copies, remote signals or barrier semaphores. Data moves between devices by JAX's collectives and lax.ppermute only.
A program may use at most 64 MiB of HBM per device.

v0:
```python
import functools

import jax
import jax.numpy as jnp
from jax import lax
from jax.experimental import pallas as pl
from jax.experimental.pallas import tpu as pltpu
from jax.sharding import PartitionSpec as P


PIECES = 4

step_size = 0.5

f32 = jnp.float32
bf16 = jnp.bfloat16


def tile_of(size):
    for tile in (256, 128, 64, 32):
        if size % tile == 0:
            return tile
    return size


def fill(zs, first, z, width):
    count = z.shape[0]
    column = lax.broadcasted_iota(jnp.int32, z.shape, 0) % width
    after = jnp.where(column == width - 1, 0.0, pltpu.roll(z, count - 1, 0))
    before = jnp.where(column == 0, 0.0, pltpu.roll(z, 1, 0))
    rows = pl.ds(first, count)
    zs[0, rows, :] = after.astype(bf16)
    zs[1, rows, :] = z.astype(bf16)
    zs[2, rows, :] = before.astype(bf16)


def blank(zs, first, count):
    zs[:, pl.ds(first, count), :] = jnp.zeros((3, count, zs.shape[2]), bf16)


def taps_at(zs, kernel_ref, start, size, width):
    total = None
    for a in range(3):
        for b in range(3):
            rows = zs[b, pl.ds(start + (2 - a) * width, size), :]
            term = lax.dot_general(
                rows, kernel_ref[3 * a + b], (((1,), (1,)), ((), ())), preferred_element_type=f32
            )
            total = term if total is None else total + term
    return total


def conv_into(out, zs, kernel_ref, width, finish):
    count = out.shape[0]
    tile = tile_of(count)
    for start in range(0, count, tile):
        out[pl.ds(start, tile), :] = finish(start, tile, taps_at(zs, kernel_ref, start, tile, width))


def window(shape, lead, first):
    spec = (None,) * len(lead) + (pl.Element(shape[0]), pl.Element(shape[1]))
    return pl.BlockSpec(spec, lambda *_: (*lead, first, 0))


def cost(rows, channels, taps, moved):
    return pl.CostEstimate(
        flops=2 * rows * channels * channels * taps, bytes_accessed=moved, transcendentals=0
    )


def whole(shape):
    return pl.BlockSpec(shape, lambda *_: (0,) * len(shape))


def end_kernel(width, guess, slope, kernel, out, zs):
    count = guess.shape[0]
    blank(zs, 0, width)
    blank(zs, count + width, width)
    fill(zs, width, slope[...].astype(f32) * guess[...], width)
    conv_into(
        out, zs, kernel, width,
        lambda s, n, moved: guess[pl.ds(s, n), :] + step_size * moved,
    )


def section_end_of(guess, slopes, kernels, image, width):
    pixels, channels = guess.shape[2:]
    return pl.pallas_call(
        functools.partial(end_kernel, width),
        out_shape=jax.ShapeDtypeStruct((pixels, channels), f32),
        grid=(1,),
        in_specs=[
            window((pixels, channels), (0, image), 0),
            window((pixels, channels), (0, image), 0),
            pl.BlockSpec((None, *kernels.shape[1:]), lambda *_: (0, 0, 0, 0)),
        ],
        out_specs=whole((pixels, channels)),
        scratch_shapes=[pltpu.VMEM((3, pixels + 2 * width, channels), bf16)],
        cost_estimate=cost(pixels, channels, 9, pixels * channels * 12),
        name="section_end",
    )(guess, slopes, kernels)


def stage_kernel(width, factor, first_row, low_row, has_tail, gives_tail, *refs):
    refs = list(refs)
    tail = refs.pop(0) if has_tail else None
    arrived, guess, slope, end, kernel = refs[:5]
    out = refs[5]
    tail_out = refs[6] if gives_tail else None
    field, zs = refs[-2:]
    above = max(first_row - 1, 0)
    kept = (low_row - above) * width
    new = arrived.shape[0]
    if has_tail:
        field[pl.ds(0, kept), :] = tail[...]
    field[pl.ds(kept, new), :] = arrived[...] - guess[...]
    lead = (above - (first_row - 1)) * width
    count = kept + new
    if lead:
        blank(zs, 0, lead)
    fill(zs, lead, slope[...].astype(f32) * field[...], width)
    rest = zs.shape[1] - lead - count
    if rest:
        blank(zs, lead + count, rest)
    base = (first_row - above) * width
    conv_into(
        out, zs, kernel, width,
        lambda s, n, moved: field[pl.ds(base + s, n), :] + factor * moved + end[pl.ds(s, n), :],
    )
    if gives_tail:
        tail_out[...] = field[pl.ds(count - 2 * width, 2 * width), :]


def stage(arrived, tail, guess, slopes, kernels, end, image, factor, rows, width):
    first, low, last, high, height = rows
    layers, _, _, channels = guess.shape
    above = max(first - 1, 0)
    gives_tail = high < height
    count = (last - first) * width
    in_specs = [] if tail is None else [whole(tail.shape)]
    in_specs += [
        whole(arrived.shape),
        window(arrived.shape, (layers - 1, image), low * width),
        window(((high - above) * width, channels), (0, image), above * width),
        window((count, channels), (), first * width),
        pl.BlockSpec((None, *kernels.shape[1:]), lambda *_: (0, 0, 0, 0)),
    ]
    out_shape = [jax.ShapeDtypeStruct((count, channels), f32)]
    if gives_tail:
        out_shape.append(jax.ShapeDtypeStruct((2 * width, channels), f32))
    results = pl.pallas_call(
        functools.partial(stage_kernel, width, factor, first, low, tail is not None, gives_tail),
        out_shape=out_shape,
        grid=(1,),
        in_specs=in_specs,
        out_specs=[whole(s.shape) for s in out_shape],
        scratch_shapes=[
            pltpu.VMEM(((high - above) * width, channels), f32),
            pltpu.VMEM((3, count + 2 * width, channels), bf16),
        ],
        cost_estimate=cost(count, channels, 9, count * channels * 20),
        name="stage",
    )(*(() if tail is None else (tail,)), arrived, guess, slopes, end, kernels)
    return results[0], (results[1] if gives_tail else None)


def grads_into(acc, zs, states, width, scale, before):
    pixels = states.shape[0]
    turned = states[...].T
    for a in range(3):
        for b in range(3):
            rows = zs[b, pl.ds((2 - a) * width, pixels), :]
            term = lax.dot_general(
                turned, rows, (((1,), (0,)), ((), ())), preferred_element_type=f32
            )
            if before is not None:
                term = term + before[3 * a + b]
            acc[3 * a + b] = term * scale if scale != 1.0 else term


def hand_out(acc, side, mine, away, share):
    for node in range(mine.shape[0]):
        base = 2 * node * share
        kept = pl.multiple_of(base + side * share, share)
        sent = pl.multiple_of(base + (1 - side) * share, share)
        mine[node] = acc[:, pl.ds(kept, share), :]
        away[node] = acc[:, pl.ds(sent, share), :]


def top_kernel(width, pieces, final, scale, share, *refs):
    place, *refs = refs
    arrived, refs = refs[:pieces], list(refs[pieces:])
    guess, slope, states = refs[:3]
    del refs[:3]
    before = refs.pop(0) if final else None
    if final:
        adjoint, mine, away, acc, zs = refs
    else:
        adjoint, acc, zs = refs
    pixels = guess.shape[0]
    top = place[0] == 1
    adjoint[...] = jnp.where(top, guess[...], 0.0)
    row = 0
    for ref in arrived:
        count = ref.shape[0]
        spot = pl.ds(row, count)
        adjoint[spot, :] = adjoint[spot, :] + ref[...]
        row = (row + count) % pixels
    blank(zs, 0, width)
    blank(zs, pixels + width, width)
    fill(zs, width, slope[...].astype(f32) * adjoint[...], width)
    grads_into(acc, zs, states, width, scale, before)
    if final:
        hand_out(acc, place[1], mine, away, share)


def top_of(place, arrived, guess, slopes, states, before, image, width, scale, share):
    layers, _, pixels, channels = guess.shape
    final = before is not None
    grad = (9, channels, channels)
    split = (channels // share // 2, 9, share, channels)
    tile = window((pixels, channels), (layers - 1, image), 0)
    in_specs = [pl.BlockSpec(memory_space=pltpu.SMEM)]
    in_specs += [whole(p.shape) for p in arrived] + [tile, tile, tile]
    out_shape = [jax.ShapeDtypeStruct((pixels, channels), f32)]
    scratch = [pltpu.VMEM((3, pixels + 2 * width, channels), bf16)]
    if final:
        in_specs.append(whole(grad))
        out_shape += [jax.ShapeDtypeStruct(split, f32)] * 2
        scratch.insert(0, pltpu.VMEM(grad, f32))
    else:
        out_shape.append(jax.ShapeDtypeStruct(grad, f32))
    return pl.pallas_call(
        functools.partial(top_kernel, width, len(arrived), final, scale, share),
        out_shape=out_shape,
        grid=(1,),
        in_specs=in_specs,
        out_specs=[whole(s.shape) for s in out_shape],
        scratch_shapes=scratch,
        cost_estimate=cost(pixels, channels, 9, pixels * channels * 20),
        name="top",
    )(place, *arrived, guess, slopes, states, *((before,) if final else ()))


def inner_kernel(width, final, scale, share, *refs):
    place, adjoint, slope_above, slope, states, kernel = refs[:6]
    refs = list(refs[6:])
    before = refs.pop(0) if final else None
    if final:
        below, mine, away, acc, zs, zs2 = refs
    else:
        below, acc, zs, zs2 = refs
    pixels = adjoint.shape[0]
    for z in (zs, zs2):
        blank(z, 0, width)
        blank(z, pixels + width, width)
    fill(zs, width, slope_above[...].astype(f32) * adjoint[...], width)
    conv_into(
        below, zs, kernel, width,
        lambda s, n, moved: adjoint[pl.ds(s, n), :] + step_size * moved,
    )
    fill(zs2, width, slope[...].astype(f32) * below[...], width)
    grads_into(acc, zs2, states, width, scale, before)
    if final:
        hand_out(acc, place[1], mine, away, share)


def inner_of(place, adjoint, slopes, states, kernels, before, layer, image, width, scale, share):
    pixels, channels = adjoint.shape
    final = before is not None
    grad = (9, channels, channels)
    split = (channels // share // 2, 9, share, channels)
    in_specs = [
        pl.BlockSpec(memory_space=pltpu.SMEM),
        whole((pixels, channels)),
        window((pixels, channels), (layer + 1, image), 0),
        window((pixels, channels), (layer, image), 0),
        window((pixels, channels), (layer, image), 0),
        pl.BlockSpec((None, *kernels.shape[1:]), lambda *_: (layer + 1, 0, 0, 0)),
    ]
    out_shape = [jax.ShapeDtypeStruct((pixels, channels), f32)]
    scratch = [pltpu.VMEM((3, pixels + 2 * width, channels), bf16)] * 2
    if final:
        in_specs.append(whole(grad))
        out_shape += [jax.ShapeDtypeStruct(split, f32)] * 2
        scratch.insert(0, pltpu.VMEM(grad, f32))
    else:
        out_shape.append(jax.ShapeDtypeStruct(grad, f32))
    return pl.pallas_call(
        functools.partial(inner_kernel, width, final, scale, share),
        out_shape=out_shape,
        grid=(1,),
        in_specs=in_specs,
        out_specs=[whole(s.shape) for s in out_shape],
        scratch_shapes=scratch,
        cost_estimate=cost(pixels, channels, 18, pixels * channels * 20),
        name="inner",
    )(place, adjoint, slopes, slopes, states, kernels, *((before,) if final else ()))


def lower_kernel(width, *refs):
    first, second, slope, kernel, out, zs = refs
    pixels = first.shape[0]
    for image, adjoint in enumerate((first, second)):
        blank(zs, 0, width)
        blank(zs, pixels + width, width)
        fill(zs, width, slope[image].astype(f32) * adjoint[...], width)
        conv_into(
            out.at[image], zs, kernel, width,
            lambda s, n, moved, adjoint=adjoint: adjoint[pl.ds(s, n), :] + step_size * moved,
        )


def lower_of(adjoints, slopes, kernels, width):
    images = len(adjoints)
    pixels, channels = adjoints[0].shape
    return pl.pallas_call(
        functools.partial(lower_kernel, width),
        out_shape=jax.ShapeDtypeStruct((images, pixels, channels), f32),
        grid=(1,),
        in_specs=[whole((pixels, channels))] * images
        + [
            pl.BlockSpec((None, images, pixels, channels), lambda *_: (0, 0, 0, 0)),
            pl.BlockSpec((None, *kernels.shape[1:]), lambda *_: (0, 0, 0, 0)),
        ],
        out_specs=whole((images, pixels, channels)),
        scratch_shapes=[pltpu.VMEM((3, pixels + 2 * width, channels), bf16)],
        cost_estimate=cost(images * pixels, channels, 9, images * pixels * channels * 12),
        name="lower",
    )(*adjoints, slopes, kernels)


def cuts_of(height, hops):
    piece = height // PIECES
    return [
        [0] + [min(height, piece * (k + 1) + hops - 1 - hop) for k in range(PIECES - 1)] + [height]
        for hop in range(hops)
    ]


def chain(ends, guess, slopes, kernels, factor, width):
    sections = lax.axis_size("layer")
    images, pixels, channels = len(ends), *ends[0].shape
    height = pixels // width
    hops = sections - 1
    cuts = cuts_of(height, hops)
    payload = [
        [ends[i][low * width : high * width] for low, high in zip(cuts[0], cuts[0][1:])]
        for i in range(images)
    ]
    arrivals = []
    for hop in range(hops):
        pairs = [(sections - 1 - hop, sections - 2 - hop)]
        following, here = [], []
        for i in range(images):
            sent, got, tail = [], [], None
            for k, rows in enumerate(payload[i]):
                arrived = lax.ppermute(rows, "layer", pairs)
                got.append(arrived)
                if hop + 1 < hops:
                    low, high = cuts[hop][k : k + 2]
                    first, last = cuts[hop + 1][k : k + 2]
                    passed, tail = stage(
                        arrived, tail, guess, slopes, kernels, ends[i], i, factor,
                        (first, low, last, high, height), width,
                    )
                    sent.append(passed)
            following.append(sent)
            here.append(got)
        arrivals.append(here)
        payload = following
    return arrivals


def scatter_sum(mine, away):
    replicas = lax.axis_size("dp")
    node = lax.axis_index("dp") // 2
    nodes = replicas // 2
    got = lax.ppermute(away, "dp", [(i, i ^ 1) for i in range(replicas)])
    held = mine + got

    def block(index):
        return lax.dynamic_index_in_dim(held, jnp.clip(index, 0, nodes - 1), 0, keepdims=False)

    total = block(node)
    up = down = None
    for tick in range(1, nodes):
        up_out, down_out = block(node + nodes - tick), block(node - nodes + tick)
        if up is not None:
            up_out, down_out = up_out + up, down_out + down
        up_pairs = [(2 * n + s, 2 * n + 2 + s) for n in range(tick) for s in range(2)]
        down_pairs = [
            (2 * n + s, 2 * n - 2 + s) for n in range(nodes - tick, nodes) for s in range(2)
        ]
        up = lax.ppermute(up_out, "dp", up_pairs)
        down = lax.ppermute(down_out, "dp", down_pairs)
    return total + up + down


def on_device(states, slopes, kernels, guess):
    layers, images, height, width, channels = states.shape
    flat = (layers, images, height * width, channels)
    states, slopes, guess = (x.reshape(flat) for x in (states, slopes, guess))
    replicas = lax.axis_size("dp")
    sections = lax.axis_size("layer")
    share = channels // replicas
    place = jnp.stack(
        [
            (lax.axis_index("layer") == sections - 1).astype(jnp.int32),
            (lax.axis_index("dp") % 2).astype(jnp.int32),
        ]
    )
    ends = [section_end_of(guess, slopes, kernels, i, width) for i in range(images)]
    arrivals = chain(ends, guess, slopes, kernels, step_size * layers, width)
    scale = step_size / (images * replicas)
    adjoints = [None] * images
    partial = None
    for i in range(images):
        final = i == images - 1
        pieces = [p for hop in arrivals for p in hop[i]]
        adjoints[i], *partial = top_of(
            place, pieces, guess, slopes, states, partial[0] if final else None, i, width,
            scale if final else 1.0, share,
        )
    gradients = [None] * layers
    gradients[layers - 1] = scatter_sum(*partial)
    for layer in range(layers - 2, -1, -1):
        partial = None
        for i in range(images):
            final = i == images - 1
            adjoints[i], *partial = inner_of(
                place, adjoints[i], slopes, states, kernels, partial[0] if final else None,
                layer, i, width, scale if final else 1.0, share,
            )
        gradients[layer] = scatter_sum(*partial)
    lower = lower_of(adjoints, slopes, kernels, width)
    return lower.reshape(1, images, height, width, channels), jnp.stack(gradients)


def solution(mesh):
    return jax.shard_map(
        on_device,
        mesh=mesh,
        in_specs=(
            P("layer", "dp", None, None, None),
            P("layer", "dp", None, None, None),
            P("layer", None, None, None),
            P("layer", "dp", None, None, None),
        ),
        out_specs=(P("layer", "dp", None, None, None), P("layer", None, "dp", None)),
        check_vma=False,
    )
```

profile of v0, /device:TPU:0, one launch (start us, length us, event | category | flops | bytes accessed | tf_op | source)
XLA Modules:
  0.0 205.6 jit_solution(17400723136683727947)
XLA Ops:
  0.6 4.2 %section_end.3.refs_3_.refs_4_ = f32[1024,256]{1,0:T(8,128)} custom-call(f32[2,2,1024,256]{3,2,1,0:T(8,128)} %bitcast.46, bf16[2,2,1024,256]{3,2,1,0:T(8,128)(2,1)} %bitcast.66, bf16[2,9,256,256]{3,2,1,0:T(8,128)(2,1)} %refs_3_.1), custom_call_target="tpu_custom_call" | custom-call | flops 1207959552 | bytes 3145728 | tf_op jit(solution)/shard_map/section_end/pallas_call | solution.py:88
  6.5 4.2 %section_end.2.refs_3_.refs_4_ = f32[1024,256]{1,0:T(8,128)} custom-call(f32[2,2,1024,256]{3,2,1,0:T(8,128)} %bitcast.47, bf16[2,2,1024,256]{3,2,1,0:T(8,128)(2,1)} %bitcast.67, bf16[2,9,256,256]{3,2,1,0:T(8,128)(2,1)} %refs_3_.1), custom_call_target="tpu_custom_call" | custom-call | flops 1207959552 | bytes 3145728 | tf_op jit(solution)/shard_map/section_end/pallas_call | solution.py:88
  16.3 5.5 %stage.16 = (f32[288,256]{1,0:T(8,128)}, f32[64,256]{1,0:T(8,128)}) custom-call(f32[320,256]{1,0:T(8,128)} %copy-done.2, f32[2,2,1024,256]{3,2,1,0:T(8,128)} %bitcast.48, bf16[2,2,1024,256]{3,2,1,0:T(8,128)(2,1)} %bitcast.68, f32[1024,256]{1,0:T(8,128)} %section_end.2.refs_3_.refs_4_, bf16[2,9,256,256]{3,2,1,0:T(8,128)(2,1)} %refs_3_.1), custom_call_target="tpu_custom_call" | custom-call | flops 339738624 | bytes 1474560 | tf_op jit(solution)/shard_map/stage/pallas_call | solution.py:151
  22.6 2.9 %stage.17 = (f32[256,256]{1,0:T(8,128)}, f32[64,256]{1,0:T(8,128)}) custom-call(f32[64,256]{1,0:T(8,128)} %get-tuple-element.37.refs_0_, f32[256,256]{1,0:T(8,128)} %copy-done.10, f32[2,2,1024,256]{3,2,1,0:T(8,128)} %bitcast.49, bf16[2,2,1024,256]{3,2,1,0:T(8,128)(2,1)} %bitcast.69, f32[1024,256]{1,0:T(8,128)} %section_end.2.refs_3_.refs_4_, ...), custom_call_target="tpu_custom_call" | custom-call | flops 301989888 | bytes 1310720 | tf_op jit(solution)/shard_map/stage/pallas_call | solution.py:151
  27.8 2.9 %stage.18 = (f32[256,256]{1,0:T(8,128)}, f32[64,256]{1,0:T(8,128)}) custom-call(f32[64,256]{1,0:T(8,128)} %get-tuple-element.39.refs_0_, f32[256,256]{1,0:T(8,128)} %copy-done.9, f32[2,2,1024,256]{3,2,1,0:T(8,128)} %bitcast.50, bf16[2,2,1024,256]{3,2,1,0:T(8,128)(2,1)} %bitcast.70, f32[1024,256]{1,0:T(8,128)} %section_end.2.refs_3_.refs_4_, ...), custom_call_target="tpu_custom_call" | custom-call | flops 301989888 | bytes 1310720 | tf_op jit(solution)/shard_map/stage/pallas_call | solution.py:151
  32.0 5.6 %stage.24 = (f32[288,256]{1,0:T(8,128)}, f32[64,256]{1,0:T(8,128)}) custom-call(f32[320,256]{1,0:T(8,128)} %copy-done.1, f32[2,2,1024,256]{3,2,1,0:T(8,128)} %bitcast.51, bf16[2,2,1024,256]{3,2,1,0:T(8,128)(2,1)} %bitcast.71, f32[1024,256]{1,0:T(8,128)} %section_end.3.refs_3_.refs_4_, bf16[2,9,256,256]{3,2,1,0:T(8,128)(2,1)} %refs_3_.1), custom_call_target="tpu_custom_call" | custom-call | flops 339738624 | bytes 1474560 | tf_op jit(solution)/shard_map/stage/pallas_call | solution.py:151
  41.2 4.9 %stage.19 = f32[224,256]{1,0:T(8,128)} custom-call(f32[64,256]{1,0:T(8,128)} %get-tuple-element.41.refs_0_, f32[192,256]{1,0:T(8,128)} %copy-done.17, f32[2,2,1024,256]{3,2,1,0:T(8,128)} %bitcast.53, bf16[2,2,1024,256]{3,2,1,0:T(8,128)(2,1)} %bitcast.73, f32[1024,256]{1,0:T(8,128)} %section_end.2.refs_3_.refs_4_, bf16[2,9,256,256]{3,2,1,0:T(8,128)(2,1)} %refs_3_.1), custom_call_target="tpu_custom_call" | custom-call | flops 264241152 | bytes 1146880 | tf_op jit(solution)/shard_map/stage/pallas_call | solution.py:151
  46.7 2.9 %stage.26 = (f32[256,256]{1,0:T(8,128)}, f32[64,256]{1,0:T(8,128)}) custom-call(f32[64,256]{1,0:T(8,128)} %get-tuple-element.53.refs_0_, f32[256,256]{1,0:T(8,128)} %copy-done.8, f32[2,2,1024,256]{3,2,1,0:T(8,128)} %bitcast.54, bf16[2,2,1024,256]{3,2,1,0:T(8,128)(2,1)} %bitcast.74, f32[1024,256]{1,0:T(8,128)} %section_end.3.refs_3_.refs_4_, ...), custom_call_target="tpu_custom_call" | custom-call | flops 301989888 | bytes 1310720 | tf_op jit(solution)/shard_map/stage/pallas_call | solution.py:151
  55.5 2.8 %stage.21 = (f32[256,256]{1,0:T(8,128)}, f32[64,256]{1,0:T(8,128)}) custom-call(f32[64,256]{1,0:T(8,128)} %get-tuple-element.43.refs_0_, f32[256,256]{1,0:T(8,128)} %copy-done.11, f32[2,2,1024,256]{3,2,1,0:T(8,128)} %bitcast.56, bf16[2,2,1024,256]{3,2,1,0:T(8,128)(2,1)} %bitcast.76, f32[1024,256]{1,0:T(8,128)} %section_end.2.refs_3_.refs_4_, ...), custom_call_target="tpu_custom_call" | custom-call | flops 301989888 | bytes 1310720 | tf_op jit(solution)/shard_map/stage/pallas_call | solution.py:151
  58.4 2.9 %stage.22 = (f32[256,256]{1,0:T(8,128)}, f32[64,256]{1,0:T(8,128)}) custom-call(f32[64,256]{1,0:T(8,128)} %get-tuple-element.45.refs_0_, f32[256,256]{1,0:T(8,128)} %copy-done.13, f32[2,2,1024,256]{3,2,1,0:T(8,128)} %bitcast.57, bf16[2,2,1024,256]{3,2,1,0:T(8,128)(2,1)} %bitcast.77, f32[1024,256]{1,0:T(8,128)} %section_end.2.refs_3_.refs_4_, ...), custom_call_target="tpu_custom_call" | custom-call | flops 301989888 | bytes 1310720 | tf_op jit(solution)/shard_map/stage/pallas_call | solution.py:151
  62.5 2.9 %stage.23 = f32[256,256]{1,0:T(8,128)} custom-call(f32[64,256]{1,0:T(8,128)} %get-tuple-element.47.refs_0_, f32[224,256]{1,0:T(8,128)} %copy-done.15, f32[2,2,1024,256]{3,2,1,0:T(8,128)} %bitcast.58, bf16[2,2,1024,256]{3,2,1,0:T(8,128)(2,1)} %bitcast.78, f32[1024,256]{1,0:T(8,128)} %section_end.2.refs_3_.refs_4_, bf16[2,9,256,256]{3,2,1,0:T(8,128)(2,1)} %refs_3_.1), custom_call_target="tpu_custom_call" | custom-call | flops 301989888 | bytes 1310720 | tf_op jit(solution)/shard_map/stage/pallas_call | solution.py:151
  68.3 4.9 %stage.27 = f32[224,256]{1,0:T(8,128)} custom-call(f32[64,256]{1,0:T(8,128)} %get-tuple-element.55.refs_0_, f32[192,256]{1,0:T(8,128)} %copy-done.18, f32[2,2,1024,256]{3,2,1,0:T(8,128)} %bitcast.59, bf16[2,2,1024,256]{3,2,1,0:T(8,128)(2,1)} %bitcast.79, f32[1024,256]{1,0:T(8,128)} %section_end.3.refs_3_.refs_4_, bf16[2,9,256,256]{3,2,1,0:T(8,128)(2,1)} %refs_3_.1), custom_call_target="tpu_custom_call" | custom-call | flops 264241152 | bytes 1146880 | tf_op jit(solution)/shard_map/stage/pallas_call | solution.py:151
  78.0 2.9 %stage.29 = (f32[256,256]{1,0:T(8,128)}, f32[64,256]{1,0:T(8,128)}) custom-call(f32[64,256]{1,0:T(8,128)} %get-tuple-element.57.refs_0_, f32[256,256]{1,0:T(8,128)} %copy-done.12, f32[2,2,1024,256]{3,2,1,0:T(8,128)} %bitcast.61, bf16[2,2,1024,256]{3,2,1,0:T(8,128)(2,1)} %bitcast.81, f32[1024,256]{1,0:T(8,128)} %section_end.3.refs_3_.refs_4_, ...), custom_call_target="tpu_custom_call" | custom-call | flops 301989888 | bytes 1310720 | tf_op jit(solution)/shard_map/stage/pallas_call | solution.py:151
  80.9 2.9 %stage.30 = (f32[256,256]{1,0:T(8,128)}, f32[64,256]{1,0:T(8,128)}) custom-call(f32[64,256]{1,0:T(8,128)} %get-tuple-element.59.refs_0_, f32[256,256]{1,0:T(8,128)} %copy-done.14, f32[2,2,1024,256]{3,2,1,0:T(8,128)} %bitcast.62, bf16[2,2,1024,256]{3,2,1,0:T(8,128)(2,1)} %bitcast.82, f32[1024,256]{1,0:T(8,128)} %section_end.3.refs_3_.refs_4_, ...), custom_call_target="tpu_custom_call" | custom-call | flops 301989888 | bytes 1310720 | tf_op jit(solution)/shard_map/stage/pallas_call | solution.py:151
  85.1 2.9 %stage.31 = f32[256,256]{1,0:T(8,128)} custom-call(f32[64,256]{1,0:T(8,128)} %get-tuple-element.61.refs_0_, f32[224,256]{1,0:T(8,128)} %copy-done.16, f32[2,2,1024,256]{3,2,1,0:T(8,128)} %bitcast.63, bf16[2,2,1024,256]{3,2,1,0:T(8,128)(2,1)} %bitcast.83, f32[1024,256]{1,0:T(8,128)} %section_end.3.refs_3_.refs_4_, bf16[2,9,256,256]{3,2,1,0:T(8,128)(2,1)} %refs_3_.1), custom_call_target="tpu_custom_call" | custom-call | flops 301989888 | bytes 1310720 | tf_op jit(solution)/shard_map/stage/pallas_call | solution.py:151
  90.7 3.2 %collective-permute-done.11.refs_12_ = f32[256,256]{1,0:T(8,128)S(1)} collective-permute-done((f32[256,256]{1,0:T(8,128)}, f32[256,256]{1,0:T(8,128)S(1)}, u32[]{:S(2)}, u32[]{:S(2)}) %collective-permute-start.11) | collective-permute-done | bytes 262176 | tf_op jit(solution)/shard_map/ppermute | solution.py:358
  98.4 5.5 %top.2 = (f32[1024,256]{1,0:T(8,128)}, f32[9,256,256]{2,1,0:T(8,128)}) custom-call(s32[2]{0:T(128)} %pad_add_fusion.refs_0_, f32[320,256]{1,0:T(8,128)} %copy-done.2, f32[256,256]{1,0:T(8,128)} %copy-done.10, f32[256,256]{1,0:T(8,128)} %copy-done.9, f32[192,256]{1,0:T(8,128)} %copy-done.17, f32[288,256]{1,0:T(8,128)} %copy-done.3, f32[256,256]{1,0:T(8,128)} %copy-done.11, ...), custom_call_target="tpu_custom_call" | custom-call | flops 1207959552 | bytes 5242880 | tf_op jit(solution)/shard_map/top/pallas_call | solution.py:233
  104.0 4.9 %collective-permute-done.20.refs_9_ = f32[256,256]{1,0:T(8,128)S(1)} collective-permute-done((f32[256,256]{1,0:T(8,128)S(1)}, f32[256,256]{1,0:T(8,128)S(1)}, u32[]{:S(2)}, u32[]{:S(2)}) %collective-permute-start.20) | collective-permute-done | bytes 262176 | tf_op jit(solution)/shard_map/ppermute | solution.py:358
  108.8 5.6 %collective-permute-done.22.refs_11_ = f32[256,256]{1,0:T(8,128)S(1)} collective-permute-done((f32[256,256]{1,0:T(8,128)S(1)}, f32[256,256]{1,0:T(8,128)S(1)}, u32[]{:S(2)}, u32[]{:S(2)}) %collective-permute-start.22) | collective-permute-done | bytes 262176 | tf_op jit(solution)/shard_map/ppermute | solution.py:358
  114.5 5.6 %collective-permute-done.23.refs_12_ = f32[256,256]{1,0:T(8,128)S(1)} collective-permute-done((f32[256,256]{1,0:T(8,128)}, f32[256,256]{1,0:T(8,128)S(1)}, u32[]{:S(2)}, u32[]{:S(2)}) %collective-permute-start.23) | collective-permute-done | bytes 262176 | tf_op jit(solution)/shard_map/ppermute | solution.py:358
  120.1 4.3 %collective-permute-done.21.refs_10_ = f32[256,256]{1,0:T(8,128)S(1)} collective-permute-done((f32[256,256]{1,0:T(8,128)S(1)}, f32[256,256]{1,0:T(8,128)S(1)}, u32[]{:S(2)}, u32[]{:S(2)}) %collective-permute-start.21) | collective-permute-done | bytes 262176 | tf_op jit(solution)/shard_map/ppermute | solution.py:358
  125.1 6.5 %top.3 = (f32[1024,256]{1,0:T(8,128)}, f32[4,9,32,256]{3,2,1,0:T(8,128)}, f32[4,9,32,256]{3,2,1,0:T(8,128)}) custom-call(s32[2]{0:T(128)} %pad_add_fusion.refs_0_, f32[320,256]{1,0:T(8,128)} %copy-done.1, f32[256,256]{1,0:T(8,128)} %copy-done.7, f32[256,256]{1,0:T(8,128)} %copy-done.8, f32[192,256]{1,0:T(8,128)} %copy-done.18, f32[288,256]{1,0:T(8,128)} %copy-done.4, ...), custom_call_target="tpu_custom_call" | custom-call | flops 1207959552 | bytes 5242880 | tf_op jit(solution)/shard_map/top/pallas_call | solution.py:233
  131.5 6.4 %inner.2 = (f32[1024,256]{1,0:T(8,128)}, f32[9,256,256]{2,1,0:T(8,128)}) custom-call(s32[2]{0:T(128)} %pad_add_fusion.refs_0_, f32[1024,256]{1,0:T(8,128)} %get-tuple-element.48.refs_1_, bf16[2,2,1024,256]{3,2,1,0:T(8,128)(2,1)} %bitcast.86, bf16[2,2,1024,256]{3,2,1,0:T(8,128)(2,1)} %bitcast.87, bf16[2,2,1024,256]{3,2,1,0:T(8,128)(2,1)} %bitcast.93, ...), custom_call_target="tpu_custom_call" | custom-call | flops 2415919104 | bytes 5242880 | tf_op jit(solution)/shard_map/inner/pallas_call | solution.py:289
  137.9 7.3 %inner.3 = (f32[1024,256]{1,0:T(8,128)}, f32[4,9,32,256]{3,2,1,0:T(8,128)}, f32[4,9,32,256]{3,2,1,0:T(8,128)}) custom-call(s32[2]{0:T(128)} %pad_add_fusion.refs_0_, f32[1024,256]{1,0:T(8,128)} %get-tuple-element.63.refs_1_, bf16[2,2,1024,256]{3,2,1,0:T(8,128)(2,1)} %bitcast.88, bf16[2,2,1024,256]{3,2,1,0:T(8,128)(2,1)} %bitcast.89, ...), custom_call_target="tpu_custom_call" | custom-call | flops 2415919104 | bytes 5242880 | tf_op jit(solution)/shard_map/inner/pallas_call | solution.py:289
  146.0 3.8 %collective-permute-start.32 = (f32[9,32,256]{2,1,0:T(8,128)S(1)}, f32[9,32,256]{2,1,0:T(8,128)S(1)}, u32[]{:S(2)}, u32[]{:S(2)}) collective-permute-start(f32[9,32,256]{2,1,0:T(8,128)S(1)} %get-tuple-element.76), channel_id=1, source_target_pairs={{0,2},{1,3},{8,10},{9,11},{16,18},{17,19},{24,26},{25,27}} | collective-permute-start | bytes 884744 | tf_op jit(solution)/shard_map/ppermute | solution.py:395
  157.2 5.1 %collective-permute-start.33 = (f32[9,32,256]{2,1,0:T(8,128)S(1)}, f32[9,32,256]{2,1,0:T(8,128)}, u32[]{:S(2)}, u32[]{:S(2)}) collective-permute-start(f32[9,32,256]{2,1,0:T(8,128)S(1)} %bitcast_add_fusion.2), channel_id=1, source_target_pairs={{0,2},{1,3},{2,4},{3,5},{8,10},{9,11},{10,12},{11,13},{16,18},{17,... | collective-permute-start | bytes 884744 | tf_op jit(solution)/shard_map/ppermute | solution.py:395
  163.8 4.9 %collective-permute-start.26 = (f32[9,32,256]{2,1,0:T(8,128)S(1)}, f32[9,32,256]{2,1,0:T(8,128)}, u32[]{:S(2)}, u32[]{:S(2)}) collective-permute-start(f32[9,32,256]{2,1,0:T(8,128)S(1)} %bitcast_add_fusion.7), channel_id=1, source_target_pairs={{0,2},{1,3},{2,4},{3,5},{8,10},{9,11},{10,12},{11,13},{16,18},{17,... | collective-permute-start | bytes 884744 | tf_op jit(solution)/shard_map/ppermute | solution.py:395
  171.7 3.5 %collective-permute-done.26 = f32[9,32,256]{2,1,0:T(8,128)} collective-permute-done((f32[9,32,256]{2,1,0:T(8,128)S(1)}, f32[9,32,256]{2,1,0:T(8,128)}, u32[]{:S(2)}, u32[]{:S(2)}) %collective-permute-start.26) | collective-permute-done | bytes 294944 | tf_op jit(solution)/shard_map/ppermute | solution.py:395
  177.8 5.8 %collective-permute-start.34 = (f32[9,32,256]{2,1,0:T(8,128)S(1)}, f32[9,32,256]{2,1,0:T(8,128)}, u32[]{:S(2)}, u32[]{:S(2)}) collective-permute-start(f32[9,32,256]{2,1,0:T(8,128)S(1)} %get-tuple-element.74), channel_id=1, source_target_pairs={{0,2},{1,3},{2,4},{3,5},{4,6},{5,7},{8,10},{9,11},{10,12},{11,13},... | collective-permute-start | bytes 884744 | tf_op jit(solution)/shard_map/ppermute | solution.py:395
  183.7 4.6 %collective-permute-start.27 = (f32[9,32,256]{2,1,0:T(8,128)}, f32[9,32,256]{2,1,0:T(8,128)}, u32[]{:S(2)}, u32[]{:S(2)}) collective-permute-start(f32[9,32,256]{2,1,0:T(8,128)} %get-tuple-element.70), channel_id=1, source_target_pairs={{0,2},{1,3},{2,4},{3,5},{4,6},{5,7},{8,10},{9,11},{10,12},{11,13},... | collective-permute-start | bytes 884744 | tf_op jit(solution)/shard_map/ppermute | solution.py:395
  191.0 6.2 %lower.1 = f32[2,1024,256]{2,1,0:T(8,128)} custom-call(f32[1024,256]{1,0:T(8,128)} %get-tuple-element.49.refs_0_, f32[1024,256]{1,0:T(8,128)} %get-tuple-element.65.refs_1_, bf16[2,2,1024,256]{3,2,1,0:T(8,128)(2,1)} %bitcast.90, bf16[2,9,256,256]{3,2,1,0:T(8,128)(2,1)} %refs_3_.1), custom_call_target="tpu_custom_call" | custom-call | flops 2415919104 | bytes 6291456 | tf_op jit(solution)/shard_map/lower/pallas_call | solution.py:317
  197.2 3.0 %collective-permute-done.37 = f32[9,32,256]{2,1,0:T(8,128)} collective-permute-done((f32[9,32,256]{2,1,0:T(8,128)S(1)}, f32[9,32,256]{2,1,0:T(8,128)}, u32[]{:S(2)}, u32[]{:S(2)}) %collective-permute-start.37) | collective-permute-done | bytes 294944 | tf_op jit(solution)/shard_map/ppermute | solution.py:396
  (151 shorter events, 62.9 us)
Async XLA Ops:
  5.8 25.5 %collective-permute-start.12 = (f32[320,256]{1,0:T(8,128)S(1)}, f32[320,256]{1,0:T(8,128)S(1)}, u32[]{:S(2)}, u32[]{:S(2)}) collective-permute-start(f32[320,256]{1,0:T(8,128)S(1)} %slice.36), channel_id=1, source_target_pairs={{24,16},{25,17},{26,18},{27,19},{28,20},{29,21},{30,22},{31,23}} | collective-permute-start | bytes 983048 | tf_op jit(solution)/shard_map/ppermute | solution.py:358
  13.5 13.6 %collective-permute-start.2 = (f32[256,256]{1,0:T(8,128)S(1)}, f32[256,256]{1,0:T(8,128)S(1)}, u32[]{:S(2)}, u32[]{:S(2)}) collective-permute-start(f32[256,256]{1,0:T(8,128)S(1)} %get-tuple-element.80), channel_id=1, source_target_pairs={{24,16},{25,17},{26,18},{27,19},{28,20},{29,21},{30,22},{31,23}} | collective-permute-start | bytes 786440 | tf_op jit(solution)/shard_map/ppermute | solution.py:358
  14.9 15.7 %collective-permute-start.13 = (f32[256,256]{1,0:T(8,128)S(1)}, f32[256,256]{1,0:T(8,128)S(1)}, u32[]{:S(2)}, u32[]{:S(2)}) collective-permute-start(f32[256,256]{1,0:T(8,128)S(1)} %get-tuple-element.79), channel_id=1, source_target_pairs={{24,16},{25,17},{26,18},{27,19},{28,20},{29,21},{30,22},{31,23}} | collective-permute-start | bytes 786440 | tf_op jit(solution)/shard_map/ppermute | solution.py:358
  15.6 30.4 %collective-permute-start.14 = (f32[256,256]{1,0:T(8,128)S(1)}, f32[256,256]{1,0:T(8,128)S(1)}, u32[]{:S(2)}, u32[]{:S(2)}) collective-permute-start(f32[256,256]{1,0:T(8,128)S(1)} %get-tuple-element.78), channel_id=1, source_target_pairs={{24,16},{25,17},{26,18},{27,19},{28,20},{29,21},{30,22},{31,23}} | collective-permute-start | bytes 786440 | tf_op jit(solution)/shard_map/ppermute | solution.py:358
  25.4 24.2 %collective-permute-start.5 = (f32[256,256]{1,0:T(8,128)}, f32[256,256]{1,0:T(8,128)S(1)}, u32[]{:S(2)}, u32[]{:S(2)}) collective-permute-start(f32[256,256]{1,0:T(8,128)} %get-tuple-element.38), channel_id=1, source_target_pairs={{16,8},{17,9},{18,10},{19,11},{20,12},{21,13},{22,14},{23,15}} | collective-permute-start | bytes 786440 | tf_op jit(solution)/shard_map/ppermute | solution.py:358
  27.1 13.4 %collective-permute-start.3 = (f32[192,256]{1,0:T(8,128)S(1)}, f32[192,256]{1,0:T(8,128)S(1)}, u32[]{:S(2)}, u32[]{:S(2)}) collective-permute-start(f32[192,256]{1,0:T(8,128)S(1)} %slice.35), channel_id=1, source_target_pairs={{24,16},{25,17},{26,18},{27,19},{28,20},{29,21},{30,22},{31,23}} | collective-permute-start | bytes 589832 | tf_op jit(solution)/shard_map/ppermute | solution.py:358
  30.6 20.6 %collective-permute-start.6 = (f32[256,256]{1,0:T(8,128)}, f32[256,256]{1,0:T(8,128)S(1)}, u32[]{:S(2)}, u32[]{:S(2)}) collective-permute-start(f32[256,256]{1,0:T(8,128)} %get-tuple-element.40), channel_id=1, source_target_pairs={{16,8},{17,9},{18,10},{19,11},{20,12},{21,13},{22,14},{23,15}} | collective-permute-start | bytes 786440 | tf_op jit(solution)/shard_map/ppermute | solution.py:358
  31.3 20.6 %collective-permute-start.4 = (f32[288,256]{1,0:T(8,128)}, f32[288,256]{1,0:T(8,128)S(1)}, u32[]{:S(2)}, u32[]{:S(2)}) collective-permute-start(f32[288,256]{1,0:T(8,128)} %get-tuple-element.36), channel_id=1, source_target_pairs={{16,8},{17,9},{18,10},{19,11},{20,12},{21,13},{22,14},{23,15}} | collective-permute-start | bytes 884744 | tf_op jit(solution)/shard_map/ppermute | solution.py:358
  40.5 26.3 %collective-permute-start.17 = (f32[256,256]{1,0:T(8,128)}, f32[256,256]{1,0:T(8,128)S(1)}, u32[]{:S(2)}, u32[]{:S(2)}) collective-permute-start(f32[256,256]{1,0:T(8,128)} %get-tuple-element.52), channel_id=1, source_target_pairs={{16,8},{17,9},{18,10},{19,11},{20,12},{21,13},{22,14},{23,15}} | collective-permute-start | bytes 786440 | tf_op jit(solution)/shard_map/ppermute | solution.py:358
  46.0 15.2 %collective-permute-start.7 = (f32[224,256]{1,0:T(8,128)}, f32[224,256]{1,0:T(8,128)S(1)}, u32[]{:S(2)}, u32[]{:S(2)}) collective-permute-start(f32[224,256]{1,0:T(8,128)} %stage.19), channel_id=1, source_target_pairs={{16,8},{17,9},{18,10},{19,11},{20,12},{21,13},{22,14},{23,15}} | collective-permute-start | bytes 688136 | tf_op jit(solution)/shard_map/ppermute | solution.py:358
  49.6 23.6 %collective-permute-start.18 = (f32[256,256]{1,0:T(8,128)}, f32[256,256]{1,0:T(8,128)S(1)}, u32[]{:S(2)}, u32[]{:S(2)}) collective-permute-start(f32[256,256]{1,0:T(8,128)} %get-tuple-element.54), channel_id=1, source_target_pairs={{16,8},{17,9},{18,10},{19,11},{20,12},{21,13},{22,14},{23,15}} | collective-permute-start | bytes 786440 | tf_op jit(solution)/shard_map/ppermute | solution.py:358
  51.3 14.2 %collective-permute-start.15 = (f32[192,256]{1,0:T(8,128)S(1)}, f32[192,256]{1,0:T(8,128)S(1)}, u32[]{:S(2)}, u32[]{:S(2)}) collective-permute-start(f32[192,256]{1,0:T(8,128)S(1)} %slice.39), channel_id=1, source_target_pairs={{24,16},{25,17},{26,18},{27,19},{28,20},{29,21},{30,22},{31,23}} | collective-permute-start | bytes 589832 | tf_op jit(solution)/shard_map/ppermute | solution.py:358
  52.0 21.9 %collective-permute-start.16 = (f32[288,256]{1,0:T(8,128)S(1)}, f32[288,256]{1,0:T(8,128)S(1)}, u32[]{:S(2)}, u32[]{:S(2)}) collective-permute-start(f32[288,256]{1,0:T(8,128)S(1)} %copy-done.27), channel_id=1, source_target_pairs={{16,8},{17,9},{18,10},{19,11},{20,12},{21,13},{22,14},{23,15}} | collective-permute-start | bytes 884744 | tf_op jit(solution)/shard_map/ppermute | solution.py:358
  61.2 26.8 %collective-permute-start.8 = (f32[256,256]{1,0:T(8,128)}, f32[256,256]{1,0:T(8,128)S(1)}, u32[]{:S(2)}, u32[]{:S(2)}) collective-permute-start(f32[256,256]{1,0:T(8,128)} %get-tuple-element.42), channel_id=1, source_target_pairs={{8,0},{9,1},{10,2},{11,3},{12,4},{13,5},{14,6},{15,7}} | collective-permute-start | bytes 786440 | tf_op jit(solution)/shard_map/ppermute | solution.py:358
  65.5 23.9 %collective-permute-start.10 = (f32[256,256]{1,0:T(8,128)}, f32[256,256]{1,0:T(8,128)S(1)}, u32[]{:S(2)}, u32[]{:S(2)}) collective-permute-start(f32[256,256]{1,0:T(8,128)} %get-tuple-element.46), channel_id=1, source_target_pairs={{8,0},{9,1},{10,2},{11,3},{12,4},{13,5},{14,6},{15,7}} | collective-permute-start | bytes 786440 | tf_op jit(solution)/shard_map/ppermute | solution.py:358
  66.8 27.1 %collective-permute-start.11 = (f32[256,256]{1,0:T(8,128)}, f32[256,256]{1,0:T(8,128)S(1)}, u32[]{:S(2)}, u32[]{:S(2)}) collective-permute-start(f32[256,256]{1,0:T(8,128)} %stage.23), channel_id=1, source_target_pairs={{8,0},{9,1},{10,2},{11,3},{12,4},{13,5},{14,6},{15,7}} | collective-permute-start | bytes 786440 | tf_op jit(solution)/shard_map/ppermute | solution.py:358
  73.9 23.8 %collective-permute-start.9 = (f32[256,256]{1,0:T(8,128)S(1)}, f32[256,256]{1,0:T(8,128)S(1)}, u32[]{:S(2)}, u32[]{:S(2)}) collective-permute-start(f32[256,256]{1,0:T(8,128)S(1)} %copy-done.28), channel_id=1, source_target_pairs={{8,0},{9,1},{10,2},{11,3},{12,4},{13,5},{14,6},{15,7}} | collective-permute-start | bytes 786440 | tf_op jit(solution)/shard_map/ppermute | solution.py:358
  83.8 25.0 %collective-permute-start.20 = (f32[256,256]{1,0:T(8,128)S(1)}, f32[256,256]{1,0:T(8,128)S(1)}, u32[]{:S(2)}, u32[]{:S(2)}) collective-permute-start(f32[256,256]{1,0:T(8,128)S(1)} %copy-done.30), channel_id=1, source_target_pairs={{8,0},{9,1},{10,2},{11,3},{12,4},{13,5},{14,6},{15,7}} | collective-permute-start | bytes 786440 | tf_op jit(solution)/shard_map/ppermute | solution.py:358
  88.1 26.4 %collective-permute-start.22 = (f32[256,256]{1,0:T(8,128)S(1)}, f32[256,256]{1,0:T(8,128)S(1)}, u32[]{:S(2)}, u32[]{:S(2)}) collective-permute-start(f32[256,256]{1,0:T(8,128)S(1)} %copy-done.31), channel_id=1, source_target_pairs={{8,0},{9,1},{10,2},{11,3},{12,4},{13,5},{14,6},{15,7}} | collective-permute-start | bytes 786440 | tf_op jit(solution)/shard_map/ppermute | solution.py:358
  89.4 30.7 %collective-permute-start.23 = (f32[256,256]{1,0:T(8,128)}, f32[256,256]{1,0:T(8,128)S(1)}, u32[]{:S(2)}, u32[]{:S(2)}) collective-permute-start(f32[256,256]{1,0:T(8,128)} %stage.31), channel_id=1, source_target_pairs={{8,0},{9,1},{10,2},{11,3},{12,4},{13,5},{14,6},{15,7}} | collective-permute-start | bytes 786440 | tf_op jit(solution)/shard_map/ppermute | solution.py:358
  93.9 30.5 %collective-permute-start.21 = (f32[256,256]{1,0:T(8,128)S(1)}, f32[256,256]{1,0:T(8,128)S(1)}, u32[]{:S(2)}, u32[]{:S(2)}) collective-permute-start(f32[256,256]{1,0:T(8,128)S(1)} %copy-done.29), channel_id=1, source_target_pairs={{8,0},{9,1},{10,2},{11,3},{12,4},{13,5},{14,6},{15,7}} | collective-permute-start | bytes 786440 | tf_op jit(solution)/shard_map/ppermute | solution.py:358
  131.5 14.2 %collective-permute-start.31 = (f32[4,9,32,256]{3,2,1,0:T(8,128)}, f32[4,9,32,256]{3,2,1,0:T(8,128)S(1)}, u32[]{:S(2)}, u32[]{:S(2)}) collective-permute-start(f32[4,9,32,256]{3,2,1,0:T(8,128)} %get-tuple-element.69), channel_id=1, source_target_pairs={{0,1},{1,0},{2,3},{3,2},{4,5},{5,4},{6,7},{7,6},{8,9},{9,8},{10,11... | collective-permute-start | bytes 3538952 | tf_op jit(solution)/shard_map/ppermute | solution.py:379
  152.2 11.6 %collective-permute-start.25 = (f32[9,32,256]{2,1,0:T(8,128)}, f32[9,32,256]{2,1,0:T(8,128)S(1)}, u32[]{:S(2)}, u32[]{:S(2)}) collective-permute-start(f32[9,32,256]{2,1,0:T(8,128)} %get-tuple-element.72), channel_id=1, source_target_pairs={{0,2},{1,3},{8,10},{9,11},{16,18},{17,19},{24,26},{25,27}} | collective-permute-start | bytes 884744 | tf_op jit(solution)/shard_map/ppermute | solution.py:395
  154.3 14.4 %collective-permute-start.35 = (f32[9,32,256]{2,1,0:T(8,128)S(1)}, f32[9,32,256]{2,1,0:T(8,128)}, u32[]{:S(2)}, u32[]{:S(2)}) collective-permute-start(f32[9,32,256]{2,1,0:T(8,128)S(1)} %get-tuple-element.77), channel_id=1, source_target_pairs={{6,4},{7,5},{14,12},{15,13},{22,20},{23,21},{30,28},{31,29}} | collective-permute-start | bytes 884744 | tf_op jit(solution)/shard_map/ppermute | solution.py:396
  157.2 12.6 %collective-permute-start.33 = (f32[9,32,256]{2,1,0:T(8,128)S(1)}, f32[9,32,256]{2,1,0:T(8,128)}, u32[]{:S(2)}, u32[]{:S(2)}) collective-permute-start(f32[9,32,256]{2,1,0:T(8,128)S(1)} %bitcast_add_fusion.2), channel_id=1, source_target_pairs={{0,2},{1,3},{2,4},{3,5},{8,10},{9,11},{10,12},{11,13},{16,18},{17,... | collective-permute-start | bytes 884744 | tf_op jit(solution)/shard_map/ppermute | solution.py:395
  163.8 11.4 %collective-permute-start.26 = (f32[9,32,256]{2,1,0:T(8,128)S(1)}, f32[9,32,256]{2,1,0:T(8,128)}, u32[]{:S(2)}, u32[]{:S(2)}) collective-permute-start(f32[9,32,256]{2,1,0:T(8,128)S(1)} %bitcast_add_fusion.7), channel_id=1, source_target_pairs={{0,2},{1,3},{2,4},{3,5},{8,10},{9,11},{10,12},{11,13},{16,18},{17,... | collective-permute-start | bytes 884744 | tf_op jit(solution)/shard_map/ppermute | solution.py:395
  171.0 17.3 %collective-permute-start.36 = (f32[9,32,256]{2,1,0:T(8,128)S(1)}, f32[9,32,256]{2,1,0:T(8,128)S(1)}, u32[]{:S(2)}, u32[]{:S(2)}) collective-permute-start(f32[9,32,256]{2,1,0:T(8,128)S(1)} %get-tuple-element.75), channel_id=1, source_target_pairs={{4,2},{5,3},{6,4},{7,5},{12,10},{13,11},{14,12},{15,13},{20,18},{2... | collective-permute-start | bytes 884744 | tf_op jit(solution)/shard_map/ppermute | solution.py:396
  177.2 12.4 %collective-permute-start.29 = (f32[9,32,256]{2,1,0:T(8,128)}, f32[9,32,256]{2,1,0:T(8,128)S(1)}, u32[]{:S(2)}, u32[]{:S(2)}) collective-permute-start(f32[9,32,256]{2,1,0:T(8,128)} %get-tuple-element.71), channel_id=1, source_target_pairs={{4,2},{5,3},{6,4},{7,5},{12,10},{13,11},{14,12},{15,13},{20,18},{2... | collective-permute-start | bytes 884744 | tf_op jit(solution)/shard_map/ppermute | solution.py:396
  177.8 19.4 %collective-permute-start.34 = (f32[9,32,256]{2,1,0:T(8,128)S(1)}, f32[9,32,256]{2,1,0:T(8,128)}, u32[]{:S(2)}, u32[]{:S(2)}) collective-permute-start(f32[9,32,256]{2,1,0:T(8,128)S(1)} %get-tuple-element.74), channel_id=1, source_target_pairs={{0,2},{1,3},{2,4},{3,5},{4,6},{5,7},{8,10},{9,11},{10,12},{11,13},... | collective-permute-start | bytes 884744 | tf_op jit(solution)/shard_map/ppermute | solution.py:395
  183.7 17.6 %collective-permute-start.27 = (f32[9,32,256]{2,1,0:T(8,128)}, f32[9,32,256]{2,1,0:T(8,128)}, u32[]{:S(2)}, u32[]{:S(2)}) collective-permute-start(f32[9,32,256]{2,1,0:T(8,128)} %get-tuple-element.70), channel_id=1, source_target_pairs={{0,2},{1,3},{2,4},{3,5},{4,6},{5,7},{8,10},{9,11},{10,12},{11,13},... | collective-permute-start | bytes 884744 | tf_op jit(solution)/shard_map/ppermute | solution.py:395
  188.3 11.9 %collective-permute-start.37 = (f32[9,32,256]{2,1,0:T(8,128)S(1)}, f32[9,32,256]{2,1,0:T(8,128)}, u32[]{:S(2)}, u32[]{:S(2)}) collective-permute-start(f32[9,32,256]{2,1,0:T(8,128)S(1)} %bitcast_add_fusion.1), channel_id=1, source_target_pairs={{2,0},{3,1},{4,2},{5,3},{6,4},{7,5},{10,8},{11,9},{12,10},{13,11},... | collective-permute-start | bytes 884744 | tf_op jit(solution)/shard_map/ppermute | solution.py:396
  189.7 14.1 %collective-permute-start.30 = (f32[9,32,256]{2,1,0:T(8,128)S(1)}, f32[9,32,256]{2,1,0:T(8,128)S(1)}, u32[]{:S(2)}, u32[]{:S(2)}) collective-permute-start(f32[9,32,256]{2,1,0:T(8,128)S(1)} %bitcast_add_fusion.6), channel_id=1, source_target_pairs={{2,0},{3,1},{4,2},{5,3},{6,4},{7,5},{10,8},{11,9},{12,10},{13,11},... | collective-permute-start | bytes 884744 | tf_op jit(solution)/shard_map/ppermute | solution.py:396
  (38 other events, 181.8 us)
where the time goes:
time: 207 us; the launch traced here: 206 us
  Pallas kernels  95.5 us (46%)
  starting transfers between devices  54.9 us (27%)
  waiting for transfers between devices  37.2 us (18%)
  other arithmetic  8.49 us (4%)
  local copies, waits for them, and re-layouts  8.26 us (4%)
    pallas_call x16, Pallas kernels, stage(): pl.pallas_call(functools.partial(stage_kernel, width, factor, first, low,...  55.2 us
    ppermute x6, starting transfers between devices, scatter_sum(): up = lax.ppermute(up_out, 'dp', up_pairs)  26.4 us
    ppermute x24, waiting for transfers between devices, chain(): arrived = lax.ppermute(rows, 'layer', pairs)  25.5 us
    ppermute x24, starting transfers between devices, chain(): arrived = lax.ppermute(rows, 'layer', pairs)  21.3 us
    pallas_call x2, Pallas kernels, inner_of(): pl.pallas_call(functools.partial(inner_kernel, width, final, scale, share...  13.7 us
    pallas_call x2, Pallas kernels, top_of(): pl.pallas_call(functools.partial(top_kernel, width, len(arrived), final,...  12 us
    pallas_call x2, Pallas kernels, section_end_of(): pl.pallas_call(functools.partial(end_kernel, width), out_shape=jax.ShapeD...  8.33 us
    ppermute x6, starting transfers between devices, scatter_sum(): down = lax.ppermute(down_out, 'dp', down_pairs)  6.69 us
  transfers between devices with their start and end apart: 38, of which 11 were waited for; matrix products, arithmetic and copies ran while one was open for 6% of the time, Pallas kernels for 41%

commit v1 on v0

v1 whole, which is shorter than its diff:
```python
import functools

import jax
import jax.numpy as jnp
from jax import lax
from jax.experimental import pallas as pl
from jax.experimental.pallas import tpu as pltpu
from jax.sharding import PartitionSpec as P


PIECES = 4

step_size = 0.5

f32 = jnp.float32
bf16 = jnp.bfloat16


def tile_of(size):
    if size <= 384:
        return size
    for tile in (256, 128, 64, 32):
        if size % tile == 0:
            return tile
    return size


def limits(megabytes):
    return pltpu.CompilerParams(vmem_limit_bytes=megabytes << 20)


def fill(zs, first, z, width):
    count = z.shape[0]
    column = lax.broadcasted_iota(jnp.int32, z.shape, 0) % width
    after = jnp.where(column == width - 1, 0.0, pltpu.roll(z, count - 1, 0))
    before = jnp.where(column == 0, 0.0, pltpu.roll(z, 1, 0))
    rows = pl.ds(first, count)
    zs[0, rows, :] = after.astype(bf16)
    zs[1, rows, :] = z.astype(bf16)
    zs[2, rows, :] = before.astype(bf16)


def blank(zs, first, count):
    zs[:, pl.ds(first, count), :] = jnp.zeros((3, count, zs.shape[2]), bf16)


def taps_at(zs, kernel_ref, start, size, width):
    total = None
    for a in range(3):
        for b in range(3):
            rows = zs[b, pl.ds(start + (2 - a) * width, size), :]
            term = lax.dot_general(
                rows, kernel_ref[3 * a + b], (((1,), (1,)), ((), ())), preferred_element_type=f32
            )
            total = term if total is None else total + term
    return total


def conv_into(out, zs, kernel_ref, width, finish):
    for start, tile in tiles_of(out.shape[0]):
        out[pl.ds(start, tile), :] = finish(start, tile, taps_at(zs, kernel_ref, start, tile, width))


def window(shape, lead, first):
    spec = (None,) * len(lead) + (pl.Element(shape[0]), pl.Element(shape[1]))
    return pl.BlockSpec(spec, lambda *_: (*lead, first, 0))


def cost(rows, channels, taps, moved):
    return pl.CostEstimate(
        flops=2 * rows * channels * channels * taps, bytes_accessed=moved, transcendentals=0
    )


def whole(shape):
    return pl.BlockSpec(shape, lambda *_: (0,) * len(shape))


def end_kernel(width, first_row, low_row, counts, *refs):
    guess, slope, kernel = refs[:3]
    outs, (zs,) = refs[-1 - len(counts) : -1], refs[-1:]
    lead = (first_row - (low_row - 1)) * width
    count = guess.shape[0]
    if lead:
        blank(zs, 0, lead)
    fill(zs, lead, slope[...].astype(f32) * guess[...], width)
    rest = zs.shape[1] - lead - count
    if rest:
        blank(zs, lead + count, rest)
    base = 0
    inside = (low_row - first_row) * width
    for out in outs:
        for start, size in tiles_of(out.shape[0]):
            moved = taps_at(zs, kernel, base + start, size, width)
            rows = pl.ds(inside + base + start, size)
            out[pl.ds(start, size), :] = guess[rows, :] + step_size * moved
        base += out.shape[0]


def tiles_of(count):
    tile = tile_of(count)
    return [(start, tile) for start in range(0, count, tile)]


def section_end_of(guess, slopes, kernels, image, cuts, width, after):
    pixels, channels = guess.shape[2:]
    height = pixels // width
    low, high = cuts[0], cuts[-1]
    first, last = max(low - 1, 0), min(high + 1, height)
    rows = window(((last - first) * width, channels), (0, image), first * width)
    shapes = [((b - a) * width, channels) for a, b in zip(cuts, cuts[1:])]
    anywhere = [pl.BlockSpec(memory_space=pl.ANY)] * len(after)
    return pl.pallas_call(
        functools.partial(end_kernel, width, first, low, shapes),
        out_shape=[jax.ShapeDtypeStruct(s, f32) for s in shapes],
        grid=(1,),
        in_specs=[rows, rows, pl.BlockSpec((None, *kernels.shape[1:]), lambda *_: (0, 0, 0, 0))]
        + anywhere,
        out_specs=[whole(s) for s in shapes],
        scratch_shapes=[pltpu.VMEM((3, (high - low + 2) * width, channels), bf16)],
        cost_estimate=cost((high - low) * width, channels, 9, (high - low) * width * channels * 12),
        compiler_params=limits(16) if after else None,
        name="section_end",
    )(guess, slopes, kernels, *after)


def stage_kernel(width, factor, first_row, low_row, has_tail, gives_tail, spans, owner, *refs):
    place, *refs = refs
    tail = refs.pop(0) if has_tail else None
    arrived, guess, slope, kernel = refs[:4]
    ends = refs[4 : 4 + len(spans)]
    out = refs[4 + len(spans)]
    tail_out = refs[5 + len(spans)] if gives_tail else None
    field, zs = refs[-2:]
    above = max(first_row - 1, 0)
    kept = (low_row - above) * width
    new = arrived.shape[0]

    @pl.when(place[0] == owner)
    def _():
        if has_tail:
            field[pl.ds(0, kept), :] = tail[...]
        field[pl.ds(kept, new), :] = arrived[...] - guess[...]
        lead = (above - (first_row - 1)) * width
        count = kept + new
        if lead:
            blank(zs, 0, lead)
        fill(zs, lead, slope[...].astype(f32) * field[...], width)
        rest = zs.shape[1] - lead - count
        if rest:
            blank(zs, lead + count, rest)
        if gives_tail:
            tail_out[...] = field[pl.ds(count - 2 * width, 2 * width), :]
        base = (first_row - above) * width
        for start, size in tiles_of(out.shape[0]):
            moved = taps_at(zs, kernel, start, size, width)
            out[pl.ds(start, size), :] = field[pl.ds(base + start, size), :] + factor * moved
        for (top, begin, size), end in zip(spans, ends):
            rows = pl.ds(top, size)
            out[rows, :] = out[rows, :] + end[pl.ds(begin, size), :]


def stage(place, owner, arrived, tail, guess, slopes, kernels, ends, image, factor, rows, width):
    first, low, last, high, height = rows
    layers, _, _, channels = guess.shape
    above = max(first - 1, 0)
    gives_tail = high < height
    count = (last - first) * width
    used, spans = [], []
    for begin, piece in ends:
        stop = begin + piece.shape[0] // width
        a, b = max(begin, first), min(stop, last)
        if a < b:
            used.append(piece)
            spans.append(((a - first) * width, (a - begin) * width, (b - a) * width))
    in_specs = [pl.BlockSpec(memory_space=pltpu.SMEM)]
    in_specs += [] if tail is None else [whole(tail.shape)]
    in_specs += [
        whole(arrived.shape),
        window(arrived.shape, (layers - 1, image), low * width),
        window(((high - above) * width, channels), (0, image), above * width),
        pl.BlockSpec((None, *kernels.shape[1:]), lambda *_: (0, 0, 0, 0)),
    ] + [whole(piece.shape) for piece in used]
    out_shape = [jax.ShapeDtypeStruct((count, channels), f32)]
    if gives_tail:
        out_shape.append(jax.ShapeDtypeStruct((2 * width, channels), f32))
    results = pl.pallas_call(
        functools.partial(
            stage_kernel, width, factor, first, low, tail is not None, gives_tail,
            spans, owner,
        ),
        out_shape=out_shape,
        grid=(1,),
        in_specs=in_specs,
        out_specs=[whole(s.shape) for s in out_shape],
        scratch_shapes=[
            pltpu.VMEM(((high - above) * width, channels), f32),
            pltpu.VMEM((3, count + 2 * width, channels), bf16),
        ],
        cost_estimate=cost(count, channels, 9, count * channels * 20),
        compiler_params=limits(12),
        name="stage",
    )(place, *(() if tail is None else (tail,)), arrived, guess, slopes, kernels, *used)
    return results[0], (results[1] if gives_tail else None)


def grads_into(acc, zs, states, width, scale, before):
    pixels = states.shape[0]
    turned = states[...].T
    for a in range(3):
        for b in range(3):
            rows = zs[b, pl.ds((2 - a) * width, pixels), :]
            term = lax.dot_general(
                turned, rows, (((1,), (0,)), ((), ())), preferred_element_type=f32
            )
            if before is not None:
                term = term + before[3 * a + b]
            acc[3 * a + b] = term * scale if scale != 1.0 else term


def hand_out(acc, side, mine, away, share):
    for node in range(mine.shape[0]):
        base = 2 * node * share
        kept = pl.multiple_of(base + side * share, share)
        sent = pl.multiple_of(base + (1 - side) * share, share)
        mine[node] = acc[:, pl.ds(kept, share), :]
        away[node] = acc[:, pl.ds(sent, share), :]


def top_kernel(width, hops, final, scale, share, *refs):
    place, *refs = refs
    arrived = []
    for pieces in hops:
        arrived.append(refs[:pieces])
        refs = refs[pieces:]
    guess, slope, states = refs[:3]
    refs = refs[3:]
    if final:
        before, _, adjoint, mine, away, acc, zs = refs
    else:
        before = None
        adjoint, acc, zs = refs
    pixels = guess.shape[0]

    @pl.when(place[0] == len(hops))
    def _():
        adjoint[...] = guess[...]

    for hop, pieces in enumerate(arrived):

        @pl.when(place[0] == len(hops) - 1 - hop)
        def _(pieces=pieces):
            row = 0
            for piece in pieces:
                adjoint[pl.ds(row, piece.shape[0]), :] = piece[...]
                row += piece.shape[0]

    blank(zs, 0, width)
    blank(zs, pixels + width, width)
    fill(zs, width, slope[...].astype(f32) * adjoint[...], width)
    grads_into(acc, zs, states, width, scale, before)
    if final:
        hand_out(acc, place[1], mine, away, share)


def top_of(place, arrived, guess, slopes, states, before, after, image, width, scale, share):
    layers, _, pixels, channels = guess.shape
    final = before is not None
    grad = (9, channels, channels)
    split = (channels // share // 2, 9, share, channels)
    tile = window((pixels, channels), (layers - 1, image), 0)
    pieces = [p for hop in arrived for p in hop]
    in_specs = [pl.BlockSpec(memory_space=pltpu.SMEM)]
    in_specs += [whole(p.shape) for p in pieces] + [tile, tile, tile]
    out_shape = [jax.ShapeDtypeStruct((pixels, channels), f32)]
    scratch = [pltpu.VMEM((3, pixels + 2 * width, channels), bf16)]
    if final:
        in_specs += [whole(grad), pl.BlockSpec(memory_space=pl.ANY)]
        out_shape += [jax.ShapeDtypeStruct(split, f32)] * 2
        scratch.insert(0, pltpu.VMEM(grad, f32))
    else:
        out_shape.append(jax.ShapeDtypeStruct(grad, f32))
    return pl.pallas_call(
        functools.partial(top_kernel, width, [len(hop) for hop in arrived], final, scale, share),
        out_shape=out_shape,
        grid=(1,),
        in_specs=in_specs,
        out_specs=[whole(s.shape) for s in out_shape],
        scratch_shapes=scratch,
        cost_estimate=cost(pixels, channels, 9, pixels * channels * 20),
        compiler_params=limits(36),
        name="top",
    )(place, *pieces, guess, slopes, states, *((before, after) if final else ()))


def inner_kernel(width, final, scale, share, *refs):
    place, adjoint, slope_above, slope, states, kernel = refs[:6]
    refs = list(refs[6:])
    before = refs.pop(0) if final else None
    if final:
        below, mine, away, acc, zs, zs2 = refs
    else:
        below, acc, zs, zs2 = refs
    pixels = adjoint.shape[0]
    for z in (zs, zs2):
        blank(z, 0, width)
        blank(z, pixels + width, width)
    fill(zs, width, slope_above[...].astype(f32) * adjoint[...], width)
    conv_into(
        below, zs, kernel, width,
        lambda s, n, moved: adjoint[pl.ds(s, n), :] + step_size * moved,
    )
    fill(zs2, width, slope[...].astype(f32) * below[...], width)
    grads_into(acc, zs2, states, width, scale, before)
    if final:
        hand_out(acc, place[1], mine, away, share)


def inner_of(place, adjoint, slopes, states, kernels, before, layer, image, width, scale, share):
    pixels, channels = adjoint.shape
    final = before is not None
    grad = (9, channels, channels)
    split = (channels // share // 2, 9, share, channels)
    in_specs = [
        pl.BlockSpec(memory_space=pltpu.SMEM),
        whole((pixels, channels)),
        window((pixels, channels), (layer + 1, image), 0),
        window((pixels, channels), (layer, image), 0),
        window((pixels, channels), (layer, image), 0),
        pl.BlockSpec((None, *kernels.shape[1:]), lambda *_: (layer + 1, 0, 0, 0)),
    ]
    out_shape = [jax.ShapeDtypeStruct((pixels, channels), f32)]
    scratch = [pltpu.VMEM((3, pixels + 2 * width, channels), bf16)] * 2
    if final:
        in_specs.append(whole(grad))
        out_shape += [jax.ShapeDtypeStruct(split, f32)] * 2
        scratch.insert(0, pltpu.VMEM(grad, f32))
    else:
        out_shape.append(jax.ShapeDtypeStruct(grad, f32))
    return pl.pallas_call(
        functools.partial(inner_kernel, width, final, scale, share),
        out_shape=out_shape,
        grid=(1,),
        in_specs=in_specs,
        out_specs=[whole(s.shape) for s in out_shape],
        scratch_shapes=scratch,
        cost_estimate=cost(pixels, channels, 18, pixels * channels * 20),
        compiler_params=limits(36),
        name="inner",
    )(place, adjoint, slopes, slopes, states, kernels, *((before,) if final else ()))


def lower_kernel(width, adjoint, slope, kernel, *refs):
    out, zs = refs[-2:]
    pixels = adjoint.shape[0]
    blank(zs, 0, width)
    blank(zs, pixels + width, width)
    fill(zs, width, slope[...].astype(f32) * adjoint[...], width)
    conv_into(
        out, zs, kernel, width,
        lambda s, n, moved: adjoint[pl.ds(s, n), :] + step_size * moved,
    )


def lower_of(adjoint, slopes, kernels, image, images, into, width):
    pixels, channels = adjoint.shape
    return pl.pallas_call(
        functools.partial(lower_kernel, width),
        out_shape=jax.ShapeDtypeStruct((images, pixels, channels), f32),
        grid=(1,),
        in_specs=[
            whole((pixels, channels)),
            window((pixels, channels), (0, image), 0),
            pl.BlockSpec((None, *kernels.shape[1:]), lambda *_: (0, 0, 0, 0)),
        ]
        + [pl.BlockSpec(memory_space=pl.ANY)] * len(into),
        out_specs=pl.BlockSpec((None, pixels, channels), lambda *_: (image, 0, 0)),
        scratch_shapes=[pltpu.VMEM((3, pixels + 2 * width, channels), bf16)],
        input_output_aliases={3: 0} if into else {},
        cost_estimate=cost(pixels, channels, 9, pixels * channels * 12),
        compiler_params=limits(16),
        name="lower",
    )(adjoint, slopes, kernels, *into)


def cuts_of(height, hops):
    piece = height // PIECES
    return [
        [0] + [min(height, piece * (k + 1) + hops - 1 - hop) for k in range(PIECES - 1)] + [height]
        for hop in range(hops)
    ]


def chain(place, ends, cuts, guess, slopes, kernels, factor, width):
    sections = lax.axis_size("layer")
    images, pixels = guess.shape[1:3]
    height = pixels // width
    hops = sections - 1
    payload = ends
    arrivals = [[] for _ in range(images)]
    for hop in range(hops):
        pairs = [(sections - 1 - hop, sections - 2 - hop)]
        following = []
        for i in range(images):
            sent, got, tail = [], [], None
            for k, rows in enumerate(payload[i]):
                arrived = lax.ppermute(rows, "layer", pairs)
                got.append(arrived)
                if hop + 1 < hops:
                    low, high = cuts[hop][k : k + 2]
                    first, last = cuts[hop + 1][k : k + 2]
                    passed, tail = stage(
                        place, sections - 2 - hop, arrived, tail, guess, slopes, kernels,
                        list(zip(cuts[0], ends[i])), i, factor,
                        (first, low, last, high, height), width,
                    )
                    sent.append(passed)
            following.append(sent)
            arrivals[i].append(got)
        payload = following
    return arrivals


def both_sides(pairs):
    return [(2 * a + side, 2 * b + side) for a, b in pairs for side in range(2)]


def join_kernel(place, mine, got, held, *outs):
    held[...] = mine[...] + got[...]
    last = held.shape[0] - 1
    for item, out in enumerate(outs):
        out[...] = held[jnp.where(place[2] == 0, last - item, item)]


def join(place, mine, got):
    nodes, *block = mine.shape
    shapes = [mine.shape] + [tuple(block)] * (nodes - 1)
    return pl.pallas_call(
        join_kernel,
        out_shape=[jax.ShapeDtypeStruct(x, f32) for x in shapes],
        grid=(1,),
        in_specs=[pl.BlockSpec(memory_space=pltpu.SMEM)] + [whole(mine.shape)] * 2,
        out_specs=[whole(x) for x in shapes],
        cost_estimate=pl.CostEstimate(flops=mine.size, bytes_accessed=16 * mine.size, transcendentals=0),
        compiler_params=limits(16),
        name="join",
    )(place, mine, got)


def relay_kernel(place, held, arrived, out):
    out[...] = held[...] + arrived[...]


def relay(place, held, arrived, wave, item):
    last = held.shape[0] - 1
    block = held.shape[1:]

    def which(_, place):
        return (jnp.where(place[2] == wave - 1, last - item, item), 0, 0, 0)

    return pl.pallas_call(
        relay_kernel,
        out_shape=jax.ShapeDtypeStruct(block, f32),
        grid_spec=pltpu.PrefetchScalarGridSpec(
            num_scalar_prefetch=1,
            grid=(1,),
            in_specs=[pl.BlockSpec((None, *block), which), whole(block)],
            out_specs=whole(block),
        ),
        cost_estimate=pl.CostEstimate(
            flops=arrived.size, bytes_accessed=12 * arrived.size, transcendentals=0
        ),
        compiler_params=limits(12),
        name="relay",
    )(place, held, arrived)


def total_kernel(nodes, place, held, *refs):
    arrived, out = refs[: nodes - 1], refs[-1]
    out[...] = held[...]
    for wave, piece in enumerate(arrived, 1):

        @pl.when((place[2] == wave) | (place[2] == nodes - 1 - wave))
        def _(piece=piece):
            out[...] = out[...] + piece[...]


def total(place, held, arrived, layer, layers, into):
    nodes, *block = held.shape
    return pl.pallas_call(
        functools.partial(total_kernel, nodes),
        out_shape=jax.ShapeDtypeStruct((layers, *block), f32),
        grid_spec=pltpu.PrefetchScalarGridSpec(
            num_scalar_prefetch=1,
            grid=(1,),
            in_specs=[pl.BlockSpec((None, *block), lambda _, place: (place[2], 0, 0, 0))]
            + [whole(tuple(block))] * len(arrived)
            + [pl.BlockSpec(memory_space=pl.ANY)] * len(into),
            out_specs=pl.BlockSpec((None, *block), lambda *_: (layer, 0, 0, 0)),
        ),
        input_output_aliases={2 + len(arrived): 0} if into else {},
        cost_estimate=pl.CostEstimate(
            flops=held.size, bytes_accessed=4 * held.size, transcendentals=0
        ),
        compiler_params=limits(12),
        name="total",
    )(place, held, *arrived, *into)


def line_sum(place, mine, away, layer, layers, into):
    replicas = lax.axis_size("dp")
    nodes = replicas // 2
    got = lax.ppermute(away, "dp", [(i, i ^ 1) for i in range(replicas)])
    held, *sends = join(place, mine, got)
    arrived = {}
    for wave in range(1, nodes):
        pairs = both_sides([(wave - 1, wave), (nodes - wave, nodes - 1 - wave)])
        for item in range(nodes - wave):
            out = sends[item]
            if wave > 1:
                out = relay(place, held, arrived[wave - 1, item], wave, item)
            arrived[wave, item] = lax.ppermute(out, "dp", pairs)
    last = [arrived[wave, nodes - 1 - wave] for wave in range(1, nodes)]
    return total(place, held, last, layer, layers, into)


def plain_sum(mine, away):
    nodes, taps, share, channels = mine.shape
    side = lax.axis_index("dp") % 2
    first, second = jnp.where(side == 0, mine, away), jnp.where(side == 0, away, mine)
    terms = jnp.stack([first, second], axis=1).reshape(2 * nodes, taps, share, channels)
    return lax.psum_scatter(terms, "dp", scatter_dimension=0, tiled=False)


def on_device(states, slopes, kernels, guess):
    layers, images, height, width, channels = states.shape
    flat = (layers, images, height * width, channels)
    states, slopes, guess = (x.reshape(flat) for x in (states, slopes, guess))
    replicas = lax.axis_size("dp")
    sections = lax.axis_size("layer")
    share = channels // replicas
    device = lax.axis_index("dp")
    place = jnp.stack([lax.axis_index("layer"), device % 2, device // 2]).astype(jnp.int32)
    cuts = cuts_of(height, sections - 1)
    ends = [section_end_of(guess, slopes, kernels, 0, cuts[0][:2], width, ())]
    ends[0] += section_end_of(guess, slopes, kernels, 0, cuts[0][1:], width, ends[0])
    for i in range(1, images):
        ends.append(section_end_of(guess, slopes, kernels, i, cuts[0], width, ends[i - 1][-1:]))
    arrivals = chain(place, ends, cuts, guess, slopes, kernels, step_size * layers, width)
    scale = step_size / (images * replicas)
    adjoints = [None] * images
    grads = [None] * layers
    for i in range(images):
        final = i == images - 1
        for layer in range(layers - 1, -1, -1):
            if layer == layers - 1:
                adjoints[i], *grads[layer] = top_of(
                    place, arrivals[i], guess, slopes, states,
                    grads[layer][0] if final else None, adjoints[i - 1] if final else None, i,
                    width, scale if final else 1.0, share,
                )
            else:
                adjoints[i], *grads[layer] = inner_of(
                    place, adjoints[i], slopes, states, kernels,
                    grads[layer][0] if final else None, layer, i, width,
                    scale if final else 1.0, share,
                )
    lower = ()
    for i in range(images):
        lower = (lower_of(adjoints[i], slopes, kernels, i, images, lower, width),)
    if replicas in (4, 8):
        gradients = ()
        for layer in range(layers - 1, -1, -1):
            gradients = (line_sum(place, *grads[layer], layer, layers, gradients),)
        gradients = gradients[0]
    else:
        gradients = jnp.stack([plain_sum(*grads[layer]) for layer in range(layers)])
    return lower[0].reshape(1, images, height, width, channels), gradients


def solution(mesh):
    return jax.shard_map(
        on_device,
        mesh=mesh,
        in_specs=(
            P("layer", "dp", None, None, None),
            P("layer", "dp", None, None, None),
            P("layer", None, None, None),
            P("layer", "dp", None, None, None),
        ),
        out_specs=(P("layer", "dp", None, None, None), P("layer", None, "dp", None)),
        check_vma=False,
    )
```

time: 207 us -> 181 us (0.87)
  Pallas kernels: 95.5 us -> 43.2 us
  waiting for transfers between devices: 37.2 us -> 75.1 us
  other arithmetic: 8.49 us -> 0.08 us
  starting transfers between devices: 54.9 us -> 47.8 us
  local copies, waits for them, and re-layouts: 8.26 us -> 12.4 us
    pallas_call x16, Pallas kernels: 55.2 us -> 12 us  [stage(): pl.pallas_call(functools.partial(stage_kernel, width, factor, first, low,...]
    ppermute x24, waiting for transfers between devices: 25.5 us -> 58.6 us  [chain(): arrived = lax.ppermute(rows, 'layer', pairs)]
    ppermute x14, starting transfers between devices: 33.6 us -> 23.2 us  [the longest x12 22.5 us: line_sum(): arrived[wave, item] = lax.ppermute(out, 'dp', pairs)]
    unnamed x64 -> x32, local copies, waits for them, and re-layouts: 2.28 us -> 12.4 us
    pallas_call x2, Pallas kernels: 13.7 us -> 7.11 us  [inner_of(): pl.pallas_call(functools.partial(inner_kernel, width, final, scale, share...]
    slice x6 -> x0, local copies, waits for them, and re-layouts: 5.07 us -> none  [chain(): ends[i][low * width:high * width]]
    add x8 -> x0, other arithmetic: 4.89 us -> none  [the longest x6 3.23 us: scatter_sum(): up_out, down_out = (up_out + up, down_out + down)]
    ppermute x14, waiting for transfers between devices: 11.6 us -> 16.5 us  [the longest x12 16.5 us: line_sum(): arrived[wave, item] = lax.ppermute(out, 'dp', pairs)]
  transfers between devices with their start and end apart: 38 -> 38, of which waited for: 11 -> 13; matrix products, arithmetic and copies ran while one was open for 6% -> 0% of each run, Pallas kernels for 41% -> 20%
where the time goes in v1:
time: 181 us; the launch traced here: 180 us
  waiting for transfers between devices  75.1 us (41%)
  starting transfers between devices  47.8 us (26%)
  Pallas kernels  43.2 us (24%)
  local copies, waits for them, and re-layouts  12.4 us (7%)
    ppermute x24, waiting for transfers between devices, chain(): arrived = lax.ppermute(rows, 'layer', pairs)  58.6 us
    ppermute x24, starting transfers between devices, chain(): arrived = lax.ppermute(rows, 'layer', pairs)  24.6 us
    ppermute x12, starting transfers between devices, line_sum(): arrived[wave, item] = lax.ppermute(out, 'dp', pairs)  22.5 us
    ppermute x12, waiting for transfers between devices, line_sum(): arrived[wave, item] = lax.ppermute(out, 'dp', pairs)  16.5 us
    unnamed x32, local copies, waits for them, and re-layouts  12.4 us
    pallas_call x16, Pallas kernels, stage(): pl.pallas_call(functools.partial(stage_kernel, width, factor, first, low,...  12 us
    pallas_call x2, Pallas kernels, inner_of(): pl.pallas_call(functools.partial(inner_kernel, width, final, scale, share...  7.11 us
    pallas_call x2, Pallas kernels, top_of(): pl.pallas_call(functools.partial(top_kernel, width, [len(hop) for hop in...  5.94 us
  transfers between devices with their start and end apart: 38, of which 13 were waited for; matrix products, arithmetic and copies ran while one was open for 0% of the time, Pallas kernels for 20%

profile of v1, /device:TPU:0, one launch (start us, length us, event | category | flops | bytes accessed | tf_op | source)
XLA Modules:
  0.0 180.0 jit_solution(18076983698069272949)
XLA Ops:
  0.6 2.9 %section_end.3.refs_3_.refs_5_.refs_6_ = f32[320,256]{1,0:T(8,128)} custom-call(f32[2,2,1024,256]{3,2,1,0:T(8,128)} %bitcast.7, bf16[2,2,1024,256]{3,2,1,0:T(8,128)(2,1)} %bitcast.28, bf16[2,9,256,256]{3,2,1,0:T(8,128)(2,1)} %kernel.3), custom_call_target="tpu_custom_call" | custom-call | flops 377487360 | bytes 983040 | tf_op jit(solution)/shard_map/section_end/pallas_call | solution.py:113
  3.6 1.4 collective-permute-start.12
  5.0 2.2 %copy-done = f32[2,2,32,32,256]{4,3,2,1,0:T(8,128)S(1)} copy-done((f32[2,2,32,32,256]{4,3,2,1,0:T(8,128)S(1)}, f32[2,2,32,32,256]{4,3,2,1,0:T(8,128)}, u32[]{:S(2)}) %copy-start) | copy-done | bytes 4194328
  7.2 1.7 copy-done.4
  13.8 1.5 section_end.5
  16.0 1.4 collective-permute-start
  19.5 2.2 %copy-done.1 = f32[2,2,32,32,256]{4,3,2,1,0:T(8,128)S(1)} copy-done((f32[2,2,32,32,256]{4,3,2,1,0:T(8,128)S(1)}, f32[2,2,32,32,256]{4,3,2,1,0:T(8,128)}, u32[]{:S(2)}) %copy-start.1) | copy-done | bytes 4194328
  21.7 1.7 copy-done.5
  49.1 33.9 %collective-permute-done.20.refs_9_ = f32[256,256]{1,0:T(8,128)S(1)} collective-permute-done((f32[256,256]{1,0:T(8,128)S(1)}, f32[256,256]{1,0:T(8,128)S(1)}, u32[]{:S(2)}, u32[]{:S(2)}) %collective-permute-start.20) | collective-permute-done | bytes 262176 | tf_op jit(solution)/shard_map/ppermute | solution.py:407
  84.3 4.3 %collective-permute-done.21.refs_10_ = f32[256,256]{1,0:T(8,128)S(1)} collective-permute-done((f32[256,256]{1,0:T(8,128)S(1)}, f32[256,256]{1,0:T(8,128)S(1)}, u32[]{:S(2)}, u32[]{:S(2)}) %collective-permute-start.21) | collective-permute-done | bytes 262176 | tf_op jit(solution)/shard_map/ppermute | solution.py:407
  89.9 4.3 %collective-permute-done.23.refs_12_ = f32[256,256]{1,0:T(8,128)S(1)} collective-permute-done((f32[256,256]{1,0:T(8,128)S(1)}, f32[256,256]{1,0:T(8,128)S(1)}, u32[]{:S(2)}, u32[]{:S(2)}) %collective-permute-start.23) | collective-permute-done | bytes 262176 | tf_op jit(solution)/shard_map/ppermute | solution.py:407
  95.5 4.3 %collective-permute-done.22.refs_11_ = f32[256,256]{1,0:T(8,128)S(1)} collective-permute-done((f32[256,256]{1,0:T(8,128)S(1)}, f32[256,256]{1,0:T(8,128)S(1)}, u32[]{:S(2)}, u32[]{:S(2)}) %collective-permute-start.22) | collective-permute-done | bytes 262176 | tf_op jit(solution)/shard_map/ppermute | solution.py:407
  99.8 3.1 %top.2 = (f32[1024,256]{1,0:T(8,128)S(1)}, f32[9,256,256]{2,1,0:T(8,128)S(1)}) custom-call(s32[3]{0:T(128)S(1)} %pad_add_fusion.refs_0_.place, f32[320,256]{1,0:T(8,128)} %collective-permute-done.12.refs_1_, f32[256,256]{1,0:T(8,128)} %collective-permute-done.13.refs_2_, f32[256,256]{1,0:T(8,128)} %collective-permute-done.14.refs_2_.refs_3_, ...), custom_call_target="tpu_custom_call" | custom-call | flops 1207959552 | bytes 5242880 | tf_op jit(solution)/shard_map/top/pallas_call | solution.py:283
  102.9 3.5 %inner.2 = (f32[1024,256]{1,0:T(8,128)S(1)}, f32[9,256,256]{2,1,0:T(8,128)S(1)}) custom-call(s32[3]{0:T(128)S(1)} %pad_add_fusion.refs_0_.place, f32[1024,256]{1,0:T(8,128)S(1)} %get-tuple-element.83.refs_1_, bf16[2,2,1024,256]{3,2,1,0:T(8,128)(2,1)S(1)} %bitcast.48, bf16[2,2,1024,256]{3,2,1,0:T(8,128)(2,1)S(1)} %bitcast.49, ...), custom_call_target="tpu_custom_call" | custom-call | flops 2415919104 | bytes 5242880 | tf_op jit(solution)/shard_map/inner/pallas_call | solution.py:340
  106.4 1.4 copy-done.10
  107.8 3.2 %collective-permute-done.11.refs_12_ = f32[256,256]{1,0:T(8,128)S(1)} collective-permute-done((f32[256,256]{1,0:T(8,128)S(1)}, f32[256,256]{1,0:T(8,128)S(1)}, u32[]{:S(2)}, u32[]{:S(2)}) %collective-permute-start.11) | collective-permute-done | bytes 262176 | tf_op jit(solution)/shard_map/ppermute | solution.py:407
  111.1 5.6 %collective-permute-done.9.refs_10_ = f32[256,256]{1,0:T(8,128)S(1)} collective-permute-done((f32[256,256]{1,0:T(8,128)S(1)}, f32[256,256]{1,0:T(8,128)S(1)}, u32[]{:S(2)}, u32[]{:S(2)}) %collective-permute-start.9) | collective-permute-done | bytes 262176 | tf_op jit(solution)/shard_map/ppermute | solution.py:407
  116.7 2.8 %collective-permute-done.8.refs_9_ = f32[256,256]{1,0:T(8,128)S(1)} collective-permute-done((f32[256,256]{1,0:T(8,128)S(1)}, f32[256,256]{1,0:T(8,128)S(1)}, u32[]{:S(2)}, u32[]{:S(2)}) %collective-permute-start.8) | collective-permute-done | bytes 262176 | tf_op jit(solution)/shard_map/ppermute | solution.py:407
  119.5 2.8 %top.3 = (f32[1024,256]{1,0:T(8,128)S(1)}, f32[4,9,32,256]{3,2,1,0:T(8,128)S(1)}, f32[4,9,32,256]{3,2,1,0:T(8,128)S(1)}) custom-call(s32[3]{0:T(128)S(1)} %pad_add_fusion.refs_0_.place, f32[320,256]{1,0:T(8,128)} %collective-permute-done.refs_1_, f32[256,256]{1,0:T(8,128)} %collective-permute-done.1.refs_2_, ...), custom_call_target="tpu_custom_call" | custom-call | flops 1207959552 | bytes 5242880 | tf_op jit(solution)/shard_map/top/pallas_call | solution.py:283
  122.5 1.7 copy-done.11
  124.1 3.6 %inner.3 = (f32[1024,256]{1,0:T(8,128)S(1)}, f32[4,9,32,256]{3,2,1,0:T(8,128)S(1)}, f32[4,9,32,256]{3,2,1,0:T(8,128)S(1)}) custom-call(s32[3]{0:T(128)S(1)} %pad_add_fusion.refs_0_.place, f32[1024,256]{1,0:T(8,128)S(1)} %get-tuple-element.85.refs_1_, bf16[2,2,1024,256]{3,2,1,0:T(8,128)(2,1)S(1)} %bitcast.51, bf16[2,2,1024,256]{3,2,1,0:T(8,128)(2,1)S(1)} %bitcast.52, ...), custom_call_target="tpu_custom_call" | custom-call | flops 2415919104 | bytes 5242880 | tf_op jit(solution)/shard_map/inner/pallas_call | solution.py:340
  129.1 3.5 %collective-permute-start.35 = (f32[9,32,256]{2,1,0:T(8,128)S(1)}, f32[9,32,256]{2,1,0:T(8,128)S(1)}, u32[]{:S(2)}, u32[]{:S(2)}) collective-permute-start(f32[9,32,256]{2,1,0:T(8,128)S(1)} %get-tuple-element.99), channel_id=1, source_target_pairs={{0,2},{1,3},{6,4},{7,5},{8,10},{9,11},{14,12},{15,13},{16,18},{17,... | collective-permute-start | bytes 884744 | tf_op jit(solution)/shard_map/ppermute | solution.py:522
  133.3 1.7 collective-permute-start.28
  137.6 2.3 %collective-permute-done.35.arrived = f32[9,32,256]{2,1,0:T(8,128)S(1)} collective-permute-done((f32[9,32,256]{2,1,0:T(8,128)S(1)}, f32[9,32,256]{2,1,0:T(8,128)S(1)}, u32[]{:S(2)}, u32[]{:S(2)}) %collective-permute-start.35) | collective-permute-done | bytes 294944 | tf_op jit(solution)/shard_map/ppermute | solution.py:522
  141.2 5.1 %collective-permute-done.28.arrived = f32[9,32,256]{2,1,0:T(8,128)S(1)} collective-permute-done((f32[9,32,256]{2,1,0:T(8,128)S(1)}, f32[9,32,256]{2,1,0:T(8,128)S(1)}, u32[]{:S(2)}, u32[]{:S(2)}) %collective-permute-start.28) | collective-permute-done | bytes 294944 | tf_op jit(solution)/shard_map/ppermute | solution.py:522
  147.5 7.2 %collective-permute-start.32 = (f32[9,32,256]{2,1,0:T(8,128)S(1)}, f32[9,32,256]{2,1,0:T(8,128)S(1)}, u32[]{:S(2)}, u32[]{:S(2)}) collective-permute-start(f32[9,32,256]{2,1,0:T(8,128)S(1)} %get-tuple-element.97), channel_id=1, source_target_pairs={{0,2},{1,3},{6,4},{7,5},{8,10},{9,11},{14,12},{15,13},{16,18},{17,... | collective-permute-start | bytes 884744 | tf_op jit(solution)/shard_map/ppermute | solution.py:522
  154.7 2.2 %collective-permute-start.25 = (f32[9,32,256]{2,1,0:T(8,128)S(1)}, f32[9,32,256]{2,1,0:T(8,128)S(1)}, u32[]{:S(2)}, u32[]{:S(2)}) collective-permute-start(f32[9,32,256]{2,1,0:T(8,128)S(1)} %get-tuple-element.91), channel_id=1, source_target_pairs={{0,2},{1,3},{6,4},{7,5},{8,10},{9,11},{14,12},{15,13},{16,18},{17,... | collective-permute-start | bytes 884744 | tf_op jit(solution)/shard_map/ppermute | solution.py:522
  163.3 1.9 %collective-permute-done.32.refs_0_ = f32[9,32,256]{2,1,0:T(8,128)S(1)} collective-permute-done((f32[9,32,256]{2,1,0:T(8,128)S(1)}, f32[9,32,256]{2,1,0:T(8,128)S(1)}, u32[]{:S(2)}, u32[]{:S(2)}) %collective-permute-start.32) | collective-permute-done | bytes 294944 | tf_op jit(solution)/shard_map/ppermute | solution.py:522
  166.5 2.5 %lower.2.refs_0_ = f32[2,1024,256]{2,1,0:T(8,128)} custom-call(f32[1024,256]{1,0:T(8,128)S(1)} %get-tuple-element.84.refs_17_.adjoint, bf16[2,2,1024,256]{3,2,1,0:T(8,128)(2,1)S(1)} %bitcast.53, bf16[2,9,256,256]{3,2,1,0:T(8,128)(2,1)S(1)} %copy-done.6), custom_call_target="tpu_custom_call" | custom-call | flops 1207959552 | bytes 3145728 | tf_op jit(solution)/shard_map/lower/pallas_call | solution.py:367
  168.9 2.5 %lower.3 = f32[2,1024,256]{2,1,0:T(8,128)} custom-call(f32[1024,256]{1,0:T(8,128)S(1)} %get-tuple-element.87.adjoint, bf16[2,2,1024,256]{3,2,1,0:T(8,128)(2,1)S(1)} %bitcast.54, bf16[2,9,256,256]{3,2,1,0:T(8,128)(2,1)S(1)} %copy-done.6, f32[2,1024,256]{2,1,0:T(8,128)} %lower.2.refs_0_), custom_call_target="tpu_custom_call", output_to_operand_aliasing={{}: (3, {})} | custom-call | flops 1207959552 | bytes 3145728 | tf_op jit(solution)/shard_map/lower/pallas_call | solution.py:367
  171.4 3.2 %collective-permute-done.37.refs_2_ = f32[9,32,256]{2,1,0:T(8,128)S(1)} collective-permute-done((f32[9,32,256]{2,1,0:T(8,128)S(1)}, f32[9,32,256]{2,1,0:T(8,128)S(1)}, u32[]{:S(2)}, u32[]{:S(2)}) %collective-permute-start.37) | collective-permute-done | bytes 294944 | tf_op jit(solution)/shard_map/ppermute | solution.py:522
  176.0 2.7 %collective-permute-done.30.refs_2_ = f32[9,32,256]{2,1,0:T(8,128)S(1)} collective-permute-done((f32[9,32,256]{2,1,0:T(8,128)S(1)}, f32[9,32,256]{2,1,0:T(8,128)S(1)}, u32[]{:S(2)}, u32[]{:S(2)}) %collective-permute-start.30) | collective-permute-done | bytes 294944 | tf_op jit(solution)/shard_map/ppermute | solution.py:522
  (112 shorter events, 54.3 us)
Async XLA Ops:
  3.6 15.3 %collective-permute-start.12 = (f32[320,256]{1,0:T(8,128)}, f32[320,256]{1,0:T(8,128)}, u32[]{:S(2)}, u32[]{:S(2)}) collective-permute-start(f32[320,256]{1,0:T(8,128)} %section_end.3.refs_3_.refs_5_.refs_6_), channel_id=1, source_target_pairs={{24,16},{25,17},{26,18},{27,19},{28,20},{29,21},{30,22},{31,23}} | collective-permute-start | bytes 983048 | tf_op jit(solution)/shard_map/ppermute | solution.py:407
  11.1 13.3 %collective-permute-start.13 = (f32[256,256]{1,0:T(8,128)}, f32[256,256]{1,0:T(8,128)}, u32[]{:S(2)}, u32[]{:S(2)}) collective-permute-start(f32[256,256]{1,0:T(8,128)} %get-tuple-element.68.refs_7_.refs_6_), channel_id=1, source_target_pairs={{24,16},{25,17},{26,18},{27,19},{28,20},{29,21},{30,22},{31,23}} | collective-permute-start | bytes 786440 | tf_op jit(solution)/shard_map/ppermute | solution.py:407
  12.4 13.7 %collective-permute-start.14 = (f32[256,256]{1,0:T(8,128)S(1)}, f32[256,256]{1,0:T(8,128)}, u32[]{:S(2)}, u32[]{:S(2)}) collective-permute-start(f32[256,256]{1,0:T(8,128)S(1)} %get-tuple-element.69.refs_7_.refs_6_), channel_id=1, source_target_pairs={{24,16},{25,17},{26,18},{27,19},{28,20},{29,21},{30,22},{31,23}} | collective-permute-start | bytes 786440 | tf_op jit(solution)/shard_map/ppermute | solution.py:407
  16.0 12.6 %collective-permute-start = (f32[320,256]{1,0:T(8,128)S(1)}, f32[320,256]{1,0:T(8,128)}, u32[]{:S(2)}, u32[]{:S(2)}) collective-permute-start(f32[320,256]{1,0:T(8,128)S(1)} %get-tuple-element.52.refs_5_.refs_6_), channel_id=1, source_target_pairs={{24,16},{25,17},{26,18},{27,19},{28,20},{29,21},{30,22},{31,23}} | collective-permute-start | bytes 983048 | tf_op jit(solution)/shard_map/ppermute | solution.py:407
  17.4 10.6 %collective-permute-start.1 = (f32[256,256]{1,0:T(8,128)S(1)}, f32[256,256]{1,0:T(8,128)}, u32[]{:S(2)}, u32[]{:S(2)}) collective-permute-start(f32[256,256]{1,0:T(8,128)S(1)} %get-tuple-element.53.refs_7_.refs_6_), channel_id=1, source_target_pairs={{24,16},{25,17},{26,18},{27,19},{28,20},{29,21},{30,22},{31,23}} | collective-permute-start | bytes 786440 | tf_op jit(solution)/shard_map/ppermute | solution.py:407
  18.8 12.5 %collective-permute-start.2 = (f32[256,256]{1,0:T(8,128)S(1)}, f32[256,256]{1,0:T(8,128)S(1)}, u32[]{:S(2)}, u32[]{:S(2)}) collective-permute-start(f32[256,256]{1,0:T(8,128)S(1)} %get-tuple-element.54.refs_7_.refs_6_), channel_id=1, source_target_pairs={{24,16},{25,17},{26,18},{27,19},{28,20},{29,21},{30,22},{31,23}} | collective-permute-start | bytes 786440 | tf_op jit(solution)/shard_map/ppermute | solution.py:407
  25.5 7.8 %collective-permute-start.17 = (f32[256,256]{1,0:T(8,128)S(1)}, f32[256,256]{1,0:T(8,128)S(1)}, u32[]{:S(2)}, u32[]{:S(2)}) collective-permute-start(f32[256,256]{1,0:T(8,128)S(1)} %get-tuple-element.72), channel_id=1, source_target_pairs={{16,8},{17,9},{18,10},{19,11},{20,12},{21,13},{22,14},{23,15}} | collective-permute-start | bytes 786440 | tf_op jit(solution)/shard_map/ppermute | solution.py:407
  27.3 7.3 %collective-permute-start.18 = (f32[256,256]{1,0:T(8,128)S(1)}, f32[256,256]{1,0:T(8,128)S(1)}, u32[]{:S(2)}, u32[]{:S(2)}) collective-permute-start(f32[256,256]{1,0:T(8,128)S(1)} %get-tuple-element.74), channel_id=1, source_target_pairs={{16,8},{17,9},{18,10},{19,11},{20,12},{21,13},{22,14},{23,15}} | collective-permute-start | bytes 786440 | tf_op jit(solution)/shard_map/ppermute | solution.py:407
  28.0 7.3 %collective-permute-start.16 = (f32[288,256]{1,0:T(8,128)S(1)}, f32[288,256]{1,0:T(8,128)S(1)}, u32[]{:S(2)}, u32[]{:S(2)}) collective-permute-start(f32[288,256]{1,0:T(8,128)S(1)} %get-tuple-element.70), channel_id=1, source_target_pairs={{16,8},{17,9},{18,10},{19,11},{20,12},{21,13},{22,14},{23,15}} | collective-permute-start | bytes 884744 | tf_op jit(solution)/shard_map/ppermute | solution.py:407
  31.3 13.5 %collective-permute-start.4 = (f32[288,256]{1,0:T(8,128)S(1)}, f32[288,256]{1,0:T(8,128)S(1)}, u32[]{:S(2)}, u32[]{:S(2)}) collective-permute-start(f32[288,256]{1,0:T(8,128)S(1)} %get-tuple-element.56), channel_id=1, source_target_pairs={{16,8},{17,9},{18,10},{19,11},{20,12},{21,13},{22,14},{23,15}} | collective-permute-start | bytes 884744 | tf_op jit(solution)/shard_map/ppermute | solution.py:407
  32.6 9.0 %collective-permute-start.5 = (f32[256,256]{1,0:T(8,128)S(1)}, f32[256,256]{1,0:T(8,128)S(1)}, u32[]{:S(2)}, u32[]{:S(2)}) collective-permute-start(f32[256,256]{1,0:T(8,128)S(1)} %get-tuple-element.58), channel_id=1, source_target_pairs={{16,8},{17,9},{18,10},{19,11},{20,12},{21,13},{22,14},{23,15}} | collective-permute-start | bytes 786440 | tf_op jit(solution)/shard_map/ppermute | solution.py:407
  33.3 9.7 %collective-permute-start.6 = (f32[256,256]{1,0:T(8,128)S(1)}, f32[256,256]{1,0:T(8,128)S(1)}, u32[]{:S(2)}, u32[]{:S(2)}) collective-permute-start(f32[256,256]{1,0:T(8,128)S(1)} %get-tuple-element.60), channel_id=1, source_target_pairs={{16,8},{17,9},{18,10},{19,11},{20,12},{21,13},{22,14},{23,15}} | collective-permute-start | bytes 786440 | tf_op jit(solution)/shard_map/ppermute | solution.py:407
  38.5 44.5 %collective-permute-start.20 = (f32[256,256]{1,0:T(8,128)S(1)}, f32[256,256]{1,0:T(8,128)S(1)}, u32[]{:S(2)}, u32[]{:S(2)}) collective-permute-start(f32[256,256]{1,0:T(8,128)S(1)} %get-tuple-element.76), channel_id=1, source_target_pairs={{8,0},{9,1},{10,2},{11,3},{12,4},{13,5},{14,6},{15,7}} | collective-permute-start | bytes 786440 | tf_op jit(solution)/shard_map/ppermute | solution.py:407
  40.3 48.3 %collective-permute-start.21 = (f32[256,256]{1,0:T(8,128)S(1)}, f32[256,256]{1,0:T(8,128)S(1)}, u32[]{:S(2)}, u32[]{:S(2)}) collective-permute-start(f32[256,256]{1,0:T(8,128)S(1)} %get-tuple-element.78), channel_id=1, source_target_pairs={{8,0},{9,1},{10,2},{11,3},{12,4},{13,5},{14,6},{15,7}} | collective-permute-start | bytes 786440 | tf_op jit(solution)/shard_map/ppermute | solution.py:407
  41.6 52.6 %collective-permute-start.23 = (f32[256,256]{1,0:T(8,128)S(1)}, f32[256,256]{1,0:T(8,128)S(1)}, u32[]{:S(2)}, u32[]{:S(2)}) collective-permute-start(f32[256,256]{1,0:T(8,128)S(1)} %stage.31), channel_id=1, source_target_pairs={{8,0},{9,1},{10,2},{11,3},{12,4},{13,5},{14,6},{15,7}} | collective-permute-start | bytes 786440 | tf_op jit(solution)/shard_map/ppermute | solution.py:407
  42.9 56.9 %collective-permute-start.22 = (f32[256,256]{1,0:T(8,128)S(1)}, f32[256,256]{1,0:T(8,128)S(1)}, u32[]{:S(2)}, u32[]{:S(2)}) collective-permute-start(f32[256,256]{1,0:T(8,128)S(1)} %get-tuple-element.80), channel_id=1, source_target_pairs={{8,0},{9,1},{10,2},{11,3},{12,4},{13,5},{14,6},{15,7}} | collective-permute-start | bytes 786440 | tf_op jit(solution)/shard_map/ppermute | solution.py:407
  47.2 60.6 %collective-permute-start.10 = (f32[256,256]{1,0:T(8,128)S(1)}, f32[256,256]{1,0:T(8,128)S(1)}, u32[]{:S(2)}, u32[]{:S(2)}) collective-permute-start(f32[256,256]{1,0:T(8,128)S(1)} %get-tuple-element.66), channel_id=1, source_target_pairs={{8,0},{9,1},{10,2},{11,3},{12,4},{13,5},{14,6},{15,7}} | collective-permute-start | bytes 786440 | tf_op jit(solution)/shard_map/ppermute | solution.py:407
  83.0 28.1 %collective-permute-start.11 = (f32[256,256]{1,0:T(8,128)S(1)}, f32[256,256]{1,0:T(8,128)S(1)}, u32[]{:S(2)}, u32[]{:S(2)}) collective-permute-start(f32[256,256]{1,0:T(8,128)S(1)} %stage.23), channel_id=1, source_target_pairs={{8,0},{9,1},{10,2},{11,3},{12,4},{13,5},{14,6},{15,7}} | collective-permute-start | bytes 786440 | tf_op jit(solution)/shard_map/ppermute | solution.py:407
  88.6 28.1 %collective-permute-start.9 = (f32[256,256]{1,0:T(8,128)S(1)}, f32[256,256]{1,0:T(8,128)S(1)}, u32[]{:S(2)}, u32[]{:S(2)}) collective-permute-start(f32[256,256]{1,0:T(8,128)S(1)} %get-tuple-element.64), channel_id=1, source_target_pairs={{8,0},{9,1},{10,2},{11,3},{12,4},{13,5},{14,6},{15,7}} | collective-permute-start | bytes 786440 | tf_op jit(solution)/shard_map/ppermute | solution.py:407
  94.2 25.3 %collective-permute-start.8 = (f32[256,256]{1,0:T(8,128)S(1)}, f32[256,256]{1,0:T(8,128)S(1)}, u32[]{:S(2)}, u32[]{:S(2)}) collective-permute-start(f32[256,256]{1,0:T(8,128)S(1)} %get-tuple-element.62), channel_id=1, source_target_pairs={{8,0},{9,1},{10,2},{11,3},{12,4},{13,5},{14,6},{15,7}} | collective-permute-start | bytes 786440 | tf_op jit(solution)/shard_map/ppermute | solution.py:407
  129.1 10.9 %collective-permute-start.35 = (f32[9,32,256]{2,1,0:T(8,128)S(1)}, f32[9,32,256]{2,1,0:T(8,128)S(1)}, u32[]{:S(2)}, u32[]{:S(2)}) collective-permute-start(f32[9,32,256]{2,1,0:T(8,128)S(1)} %get-tuple-element.99), channel_id=1, source_target_pairs={{0,2},{1,3},{6,4},{7,5},{8,10},{9,11},{14,12},{15,13},{16,18},{17,... | collective-permute-start | bytes 884744 | tf_op jit(solution)/shard_map/ppermute | solution.py:522
  133.3 12.9 %collective-permute-start.28 = (f32[9,32,256]{2,1,0:T(8,128)S(1)}, f32[9,32,256]{2,1,0:T(8,128)S(1)}, u32[]{:S(2)}, u32[]{:S(2)}) collective-permute-start(f32[9,32,256]{2,1,0:T(8,128)S(1)} %get-tuple-element.93), channel_id=1, source_target_pairs={{0,2},{1,3},{6,4},{7,5},{8,10},{9,11},{14,12},{15,13},{16,18},{17,... | collective-permute-start | bytes 884744 | tf_op jit(solution)/shard_map/ppermute | solution.py:522
  135.0 19.7 %collective-permute-start.33 = (f32[9,32,256]{2,1,0:T(8,128)S(1)}, f32[9,32,256]{2,1,0:T(8,128)S(1)}, u32[]{:S(2)}, u32[]{:S(2)}) collective-permute-start(f32[9,32,256]{2,1,0:T(8,128)S(1)} %get-tuple-element.98), channel_id=1, source_target_pairs={{0,2},{1,3},{6,4},{7,5},{8,10},{9,11},{14,12},{15,13},{16,18},{17,... | collective-permute-start | bytes 884744 | tf_op jit(solution)/shard_map/ppermute | solution.py:522
  136.3 22.5 %collective-permute-start.26 = (f32[9,32,256]{2,1,0:T(8,128)S(1)}, f32[9,32,256]{2,1,0:T(8,128)S(1)}, u32[]{:S(2)}, u32[]{:S(2)}) collective-permute-start(f32[9,32,256]{2,1,0:T(8,128)S(1)} %get-tuple-element.92), channel_id=1, source_target_pairs={{0,2},{1,3},{6,4},{7,5},{8,10},{9,11},{14,12},{15,13},{16,18},{17,... | collective-permute-start | bytes 884744 | tf_op jit(solution)/shard_map/ppermute | solution.py:522
  140.5 19.6 %collective-permute-start.36 = (f32[9,32,256]{2,1,0:T(8,128)S(1)}, f32[9,32,256]{2,1,0:T(8,128)S(1)}, u32[]{:S(2)}, u32[]{:S(2)}) collective-permute-start(f32[9,32,256]{2,1,0:T(8,128)S(1)} %relay.10), channel_id=1, source_target_pairs={{2,4},{3,5},{4,2},{5,3},{10,12},{11,13},{12,10},{13,11},{18,20},{1... | collective-permute-start | bytes 884744 | tf_op jit(solution)/shard_map/ppermute | solution.py:522
  146.8 15.2 %collective-permute-start.29 = (f32[9,32,256]{2,1,0:T(8,128)S(1)}, f32[9,32,256]{2,1,0:T(8,128)S(1)}, u32[]{:S(2)}, u32[]{:S(2)}) collective-permute-start(f32[9,32,256]{2,1,0:T(8,128)S(1)} %relay.7), channel_id=1, source_target_pairs={{2,4},{3,5},{4,2},{5,3},{10,12},{11,13},{12,10},{13,11},{18,20},{1... | collective-permute-start | bytes 884744 | tf_op jit(solution)/shard_map/ppermute | solution.py:522
  147.5 17.7 %collective-permute-start.32 = (f32[9,32,256]{2,1,0:T(8,128)S(1)}, f32[9,32,256]{2,1,0:T(8,128)S(1)}, u32[]{:S(2)}, u32[]{:S(2)}) collective-permute-start(f32[9,32,256]{2,1,0:T(8,128)S(1)} %get-tuple-element.97), channel_id=1, source_target_pairs={{0,2},{1,3},{6,4},{7,5},{8,10},{9,11},{14,12},{15,13},{16,18},{17,... | collective-permute-start | bytes 884744 | tf_op jit(solution)/shard_map/ppermute | solution.py:522
  154.7 21.3 %collective-permute-start.25 = (f32[9,32,256]{2,1,0:T(8,128)S(1)}, f32[9,32,256]{2,1,0:T(8,128)S(1)}, u32[]{:S(2)}, u32[]{:S(2)}) collective-permute-start(f32[9,32,256]{2,1,0:T(8,128)S(1)} %get-tuple-element.91), channel_id=1, source_target_pairs={{0,2},{1,3},{6,4},{7,5},{8,10},{9,11},{14,12},{15,13},{16,18},{17,... | collective-permute-start | bytes 884744 | tf_op jit(solution)/shard_map/ppermute | solution.py:522
  158.9 12.5 %collective-permute-start.34 = (f32[9,32,256]{2,1,0:T(8,128)S(1)}, f32[9,32,256]{2,1,0:T(8,128)S(1)}, u32[]{:S(2)}, u32[]{:S(2)}) collective-permute-start(f32[9,32,256]{2,1,0:T(8,128)S(1)} %relay.9), channel_id=1, source_target_pairs={{2,4},{3,5},{4,2},{5,3},{10,12},{11,13},{12,10},{13,11},{18,20},{1... | collective-permute-start | bytes 884744 | tf_op jit(solution)/shard_map/ppermute | solution.py:522
  160.7 13.9 %collective-permute-start.37 = (f32[9,32,256]{2,1,0:T(8,128)S(1)}, f32[9,32,256]{2,1,0:T(8,128)S(1)}, u32[]{:S(2)}, u32[]{:S(2)}) collective-permute-start(f32[9,32,256]{2,1,0:T(8,128)S(1)} %relay.11), channel_id=1, source_target_pairs={{4,6},{5,7},{2,0},{3,1},{12,14},{13,15},{10,8},{11,9},{20,22},{21,... | collective-permute-start | bytes 884744 | tf_op jit(solution)/shard_map/ppermute | solution.py:522
  162.0 13.9 %collective-permute-start.27 = (f32[9,32,256]{2,1,0:T(8,128)S(1)}, f32[9,32,256]{2,1,0:T(8,128)S(1)}, u32[]{:S(2)}, u32[]{:S(2)}) collective-permute-start(f32[9,32,256]{2,1,0:T(8,128)S(1)} %relay.6), channel_id=1, source_target_pairs={{2,4},{3,5},{4,2},{5,3},{10,12},{11,13},{12,10},{13,11},{18,20},{1... | collective-permute-start | bytes 884744 | tf_op jit(solution)/shard_map/ppermute | solution.py:522
  165.2 13.5 %collective-permute-start.30 = (f32[9,32,256]{2,1,0:T(8,128)S(1)}, f32[9,32,256]{2,1,0:T(8,128)S(1)}, u32[]{:S(2)}, u32[]{:S(2)}) collective-permute-start(f32[9,32,256]{2,1,0:T(8,128)S(1)} %relay.8), channel_id=1, source_target_pairs={{4,6},{5,7},{2,0},{3,1},{12,14},{13,15},{10,8},{11,9},{20,22},{21,... | collective-permute-start | bytes 884744 | tf_op jit(solution)/shard_map/ppermute | solution.py:522
  (22 other events, 162.3 us)

commit v2 on v1

--- a/solution.py
+++ b/solution.py
@@ -76,9 +76,9 @@
     return pl.BlockSpec(shape, lambda *_: (0,) * len(shape))
 
 
-def end_kernel(width, first_row, low_row, counts, *refs):
+def end_kernel(width, first_row, low_row, counts, extra, copies, *refs):
     guess, slope, kernel = refs[:3]
-    outs, (zs,) = refs[-1 - len(counts) : -1], refs[-1:]
+    outs, zs = refs[3 + extra : -1], refs[-1]
     lead = (first_row - (low_row - 1)) * width
     count = guess.shape[0]
     if lead:
@@ -89,12 +89,14 @@
         blank(zs, lead + count, rest)
     base = 0
     inside = (low_row - first_row) * width
-    for out in outs:
+    for out in outs[: len(counts)]:
         for start, size in tiles_of(out.shape[0]):
             moved = taps_at(zs, kernel, base + start, size, width)
             rows = pl.ds(inside + base + start, size)
             out[pl.ds(start, size), :] = guess[rows, :] + step_size * moved
         base += out.shape[0]
+    for source, out in zip(copies, outs[len(counts) :]):
+        out[...] = refs[source][...]
 
 
 def tiles_of(count):
@@ -102,26 +104,44 @@
     return [(start, tile) for start in range(0, count, tile)]
 
 
-def section_end_of(guess, slopes, kernels, image, cuts, width, after):
-    pixels, channels = guess.shape[2:]
+def in_hbm(x):
+    return pltpu.with_memory_space_constraint(x, pltpu.HBM)
+
+
+def section_end_of(guess, slopes, kernel, image, cuts, width, keep):
+    layers, _, pixels, channels = guess.shape
     height = pixels // width
     low, high = cuts[0], cuts[-1]
     first, last = max(low - 1, 0), min(high + 1, height)
     rows = window(((last - first) * width, channels), (0, image), first * width)
     shapes = [((b - a) * width, channels) for a, b in zip(cuts, cuts[1:])]
-    anywhere = [pl.BlockSpec(memory_space=pl.ANY)] * len(after)
+    taps = kernel.shape[-3:]
+    kernel_spec = whole(taps)
+    if kernel.ndim == 4:
+        kernel, kernel_spec = in_hbm(kernel), pl.BlockSpec((None, *taps), lambda *_: (0, 0, 0, 0))
+    args, in_specs = [in_hbm(guess), in_hbm(slopes), kernel], [rows, rows, kernel_spec]
+    out_shape = [jax.ShapeDtypeStruct(x, f32) for x in shapes]
+    copies = []
+    if keep:
+        args += [in_hbm(guess), in_hbm(slopes)]
+        in_specs += [window((pixels, channels), (layers - 1, image), 0)]
+        in_specs += [window((pixels, channels), (0, image), 0)]
+        out_shape += [jax.ShapeDtypeStruct((pixels, channels), t) for t in (f32, slopes.dtype)]
+        copies = [3, 4]
+        if kernel.ndim == 4:
+            out_shape.append(jax.ShapeDtypeStruct(taps, kernel.dtype))
+            copies.append(2)
     return pl.pallas_call(
-        functools.partial(end_kernel, width, first, low, shapes),
-        out_shape=[jax.ShapeDtypeStruct(s, f32) for s in shapes],
+        functools.partial(end_kernel, width, first, low, shapes, len(args) - 3, copies),
+        out_shape=out_shape,
         grid=(1,),
-        in_specs=[rows, rows, pl.BlockSpec((None, *kernels.shape[1:]), lambda *_: (0, 0, 0, 0))]
-        + anywhere,
-        out_specs=[whole(s) for s in shapes],
+        in_specs=in_specs,
+        out_specs=[whole(x.shape) for x in out_shape],
         scratch_shapes=[pltpu.VMEM((3, (high - low + 2) * width, channels), bf16)],
         cost_estimate=cost((high - low) * width, channels, 9, (high - low) * width * channels * 12),
-        compiler_params=limits(16) if after else None,
+        compiler_params=limits(24),
         name="section_end",
-    )(guess, slopes, kernels, *after)
+    )(*args)
 
 
 def stage_kernel(width, factor, first_row, low_row, has_tail, gives_tail, spans, owner, *refs):
@@ -160,9 +180,9 @@
             out[rows, :] = out[rows, :] + end[pl.ds(begin, size), :]
 
 
-def stage(place, owner, arrived, tail, guess, slopes, kernels, ends, image, factor, rows, width):
+def stage(place, owner, arrived, tail, guess, slope, kernel, ends, factor, rows, width):
     first, low, last, high, height = rows
-    layers, _, _, channels = guess.shape
+    channels = guess.shape[1]
     above = max(first - 1, 0)
     gives_tail = high < height
     count = (last - first) * width
@@ -177,9 +197,9 @@
     in_specs += [] if tail is None else [whole(tail.shape)]
     in_specs += [
         whole(arrived.shape),
-        window(arrived.shape, (layers - 1, image), low * width),
-        window(((high - above) * width, channels), (0, image), above * width),
-        pl.BlockSpec((None, *kernels.shape[1:]), lambda *_: (0, 0, 0, 0)),
+        window(arrived.shape, (), low * width),
+        window(((high - above) * width, channels), (), above * width),
+        whole(kernel.shape),
     ] + [whole(piece.shape) for piece in used]
     out_shape = [jax.ShapeDtypeStruct((count, channels), f32)]
     if gives_tail:
@@ -200,7 +220,7 @@
         cost_estimate=cost(count, channels, 9, count * channels * 20),
         compiler_params=limits(12),
         name="stage",
-    )(place, *(() if tail is None else (tail,)), arrived, guess, slopes, kernels, *used)
+    )(place, *(() if tail is None else (tail,)), arrived, guess, slope, kernel, *used)
     return results[0], (results[1] if gives_tail else None)
 
 
@@ -264,14 +284,14 @@
 
 
 def top_of(place, arrived, guess, slopes, states, before, after, image, width, scale, share):
-    layers, _, pixels, channels = guess.shape
+    layers, _, pixels, channels = slopes.shape
     final = before is not None
     grad = (9, channels, channels)
     split = (channels // share // 2, 9, share, channels)
     tile = window((pixels, channels), (layers - 1, image), 0)
     pieces = [p for hop in arrived for p in hop]
     in_specs = [pl.BlockSpec(memory_space=pltpu.SMEM)]
-    in_specs += [whole(p.shape) for p in pieces] + [tile, tile, tile]
+    in_specs += [whole(p.shape) for p in pieces] + [whole(guess.shape), tile, tile]
     out_shape = [jax.ShapeDtypeStruct((pixels, channels), f32)]
     scratch = [pltpu.VMEM((3, pixels + 2 * width, channels), bf16)]
     if final:
@@ -362,7 +382,7 @@
     )
 
 
-def lower_of(adjoint, slopes, kernels, image, images, into, width):
+def lower_of(adjoint, slope, kernel, image, images, into, width):
     pixels, channels = adjoint.shape
     return pl.pallas_call(
         functools.partial(lower_kernel, width),
@@ -370,8 +390,8 @@
         grid=(1,),
         in_specs=[
             whole((pixels, channels)),
-            window((pixels, channels), (0, image), 0),
-            pl.BlockSpec((None, *kernels.shape[1:]), lambda *_: (0, 0, 0, 0)),
+            whole((pixels, channels)),
+            whole(kernel.shape),
         ]
         + [pl.BlockSpec(memory_space=pl.ANY)] * len(into),
         out_specs=pl.BlockSpec((None, pixels, channels), lambda *_: (image, 0, 0)),
@@ -380,7 +400,7 @@
         cost_estimate=cost(pixels, channels, 9, pixels * channels * 12),
         compiler_params=limits(16),
         name="lower",
-    )(adjoint, slopes, kernels, *into)
+    )(adjoint, slope, kernel, *into)
 
 
 def cuts_of(height, hops):
@@ -391,10 +411,10 @@
     ]
 
 
-def chain(place, ends, cuts, guess, slopes, kernels, factor, width):
+def chain(place, ends, cuts, guess, slope, kernel, factor, width):
     sections = lax.axis_size("layer")
-    images, pixels = guess.shape[1:3]
-    height = pixels // width
+    images = len(ends)
+    height = guess[0].shape[0] // width
     hops = sections - 1
     payload = ends
     arrivals = [[] for _ in range(images)]
@@ -410,8 +430,8 @@
                     low, high = cuts[hop][k : k + 2]
                     first, last = cuts[hop + 1][k : k + 2]
                     passed, tail = stage(
-                        place, sections - 2 - hop, arrived, tail, guess, slopes, kernels,
-                        list(zip(cuts[0], ends[i])), i, factor,
+                        place, sections - 2 - hop, arrived, tail, guess[i], slope[i], kernel,
+                        list(zip(cuts[0], ends[i])), factor,
                         (first, low, last, high, height), width,
                     )
                     sent.append(passed)
@@ -542,11 +562,15 @@
     device = lax.axis_index("dp")
     place = jnp.stack([lax.axis_index("layer"), device % 2, device // 2]).astype(jnp.int32)
     cuts = cuts_of(height, sections - 1)
-    ends = [section_end_of(guess, slopes, kernels, 0, cuts[0][:2], width, ())]
-    ends[0] += section_end_of(guess, slopes, kernels, 0, cuts[0][1:], width, ends[0])
+    first = section_end_of(guess, slopes, kernels, 0, cuts[0][:2], width, False)
+    *rest, last, slope, kernel = section_end_of(guess, slopes, kernels, 0, cuts[0][1:], width, True)
+    ends, lasts, slopes_of = [[*first, *rest]], [last], [slope]
     for i in range(1, images):
-        ends.append(section_end_of(guess, slopes, kernels, i, cuts[0], width, ends[i - 1][-1:]))
-    arrivals = chain(place, ends, cuts, guess, slopes, kernels, step_size * layers, width)
+        *rest, last, slope = section_end_of(guess, slopes, kernel, i, cuts[0], width, True)
+        ends.append(rest)
+        lasts.append(last)
+        slopes_of.append(slope)
+    arrivals = chain(place, ends, cuts, lasts, slopes_of, kernel, step_size * layers, width)
     scale = step_size / (images * replicas)
     adjoints = [None] * images
     grads = [None] * layers
@@ -555,7 +579,7 @@
         for layer in range(layers - 1, -1, -1):
             if layer == layers - 1:
                 adjoints[i], *grads[layer] = top_of(
-                    place, arrivals[i], guess, slopes, states,
+                    place, arrivals[i], lasts[i], slopes, states,
                     grads[layer][0] if final else None, adjoints[i - 1] if final else None, i,
                     width, scale if final else 1.0, share,
                 )
@@ -567,7 +591,7 @@
                 )
     lower = ()
     for i in range(images):
-        lower = (lower_of(adjoints[i], slopes, kernels, i, images, lower, width),)
+        lower = (lower_of(adjoints[i], slopes_of[i], kernel, i, images, lower, width),)
     if replicas in (4, 8):
         gradients = ()
         for layer in range(layers - 1, -1, -1):

time: 181 us -> 179 us (0.989)
  Pallas kernels: 43.2 us -> 52.1 us
  local copies, waits for them, and re-layouts: 12.4 us -> 4.06 us
  waiting for transfers between devices: 75.1 us -> 72.1 us
    unnamed x32 -> x24, local copies, waits for them, and re-layouts: 12.4 us -> 4.06 us
    pallas_call x3, Pallas kernels: 5.73 us -> 10.5 us  [section_end_of(): pl.pallas_call(functools.partial(end_kernel, width, first, low, shapes, l...]
    pallas_call x16, Pallas kernels: 12 us -> 16.1 us  [stage(): pl.pallas_call(functools.partial(stage_kernel, width, factor, first, low,...]
    ppermute x24, waiting for transfers between devices: 58.6 us -> 55.5 us  [chain(): arrived = lax.ppermute(rows, 'layer', pairs)]
  transfers between devices with their start and end apart: 38 -> 38, of which waited for: 13 -> 13; matrix products, arithmetic and copies ran while one was open for 0% -> 0% of each run, Pallas kernels for 20% -> 25%
where the time goes in v2:
time: 179 us; the launch traced here: 177 us
  waiting for transfers between devices  72.1 us (40%)
  Pallas kernels  52.1 us (29%)
  starting transfers between devices  47.7 us (27%)
  local copies, waits for them, and re-layouts  4.06 us (2%)
    ppermute x24, waiting for transfers between devices, chain(): arrived = lax.ppermute(rows, 'layer', pairs)  55.5 us
    ppermute x24, starting transfers between devices, chain(): arrived = lax.ppermute(rows, 'layer', pairs)  24.6 us
    ppermute x12, starting transfers between devices, line_sum(): arrived[wave, item] = lax.ppermute(out, 'dp', pairs)  22.5 us
    ppermute x12, waiting for transfers between devices, line_sum(): arrived[wave, item] = lax.ppermute(out, 'dp', pairs)  16.6 us
    pallas_call x16, Pallas kernels, stage(): pl.pallas_call(functools.partial(stage_kernel, width, factor, first, low,...  16.1 us
    pallas_call x3, Pallas kernels, section_end_of(): pl.pallas_call(functools.partial(end_kernel, width, first, low, shapes, l...  10.5 us
    pallas_call x2, Pallas kernels, inner_of(): pl.pallas_call(functools.partial(inner_kernel, width, final, scale, share...  7.14 us
    pallas_call x2, Pallas kernels, top_of(): pl.pallas_call(functools.partial(top_kernel, width, [len(hop) for hop in...  5.96 us
  transfers between devices with their start and end apart: 38, of which 13 were waited for; matrix products, arithmetic and copies ran while one was open for 0% of the time, Pallas kernels for 25%

profile of v2, /device:TPU:0, one launch (start us, length us, event | category | flops | bytes accessed | tf_op | source)
XLA Modules:
  0.0 177.4 jit_solution(10997527251893768217)
XLA Ops:
  0.6 2.8 %section_end.5.refs_5_.refs_6_ = f32[320,256]{1,0:T(8,128)} custom-call(f32[2,2,1024,256]{3,2,1,0:T(8,128)} %bitcast.22, bf16[2,2,1024,256]{3,2,1,0:T(8,128)(2,1)} %bitcast.7, bf16[2,9,256,256]{3,2,1,0:T(8,128)(2,1)} %refs_5_.3), custom_call_target="tpu_custom_call" | custom-call | flops 377487360 | bytes 983040 | tf_op jit(solution)/shard_map/section_end/pallas_call | solution.py:134
  3.4 1.4 collective-permute-start.12
  4.8 4.0 %section_end.3 = (f32[256,256]{1,0:T(8,128)}, f32[256,256]{1,0:T(8,128)}, f32[192,256]{1,0:T(8,128)S(1)}, f32[1024,256]{1,0:T(8,128)S(1)}, bf16[1024,256]{1,0:T(...) custom-call(f32[2,2,1024,256]{3,2,1,0:T(8,128)} %bitcast.23, bf16[2,2,1024,256]{3,2,1,0:T(8,128)(2,1)} %bitcast.8, ...), custom_call_target="tpu_custom_call" | custom-call | flops 830472192 | bytes 2162688 | tf_op jit(solution)/shard_map/section_end/pallas_call | solution.py:134
  10.3 1.4 collective-permute-start.13
  11.7 1.4 collective-permute-start.14
  13.0 3.7 %section_end.4 = (f32[320,256]{1,0:T(8,128)}, f32[256,256]{1,0:T(8,128)}, f32[256,256]{1,0:T(8,128)S(1)}, f32[192,256]{1,0:T(8,128)S(1)}, f32[1024,256]{1,0:T(8,128)S(1)}, /*index=5*/bf16[1024,256]{1,0:T(8,128)(2,1)S(1)}) custom-call(f32[2,2,1024,256]{3,2,1,0:T(8,128)} %bitcast.25, bf16[2,2,1024,256]{3,2,1,0:T(8,128)(2,1)} %bitcast.10, ...), custom_call_target="tpu_custom_call" | custom-call | flops 1207959552 | bytes 3145728 | tf_op jit(solution)/shard_map/section_end/pallas_call | solution.py:134
  18.2 1.4 collective-permute-start
  19.5 1.3 collective-permute-start.1
  52.5 29.7 %collective-permute-done.22.refs_11_ = f32[256,256]{1,0:T(8,128)S(1)} collective-permute-done((f32[256,256]{1,0:T(8,128)S(1)}, f32[256,256]{1,0:T(8,128)S(1)}, u32[]{:S(2)}, u32[]{:S(2)}) %collective-permute-start.22) | collective-permute-done | bytes 262176 | tf_op jit(solution)/shard_map/ppermute | solution.py:427
  83.5 4.3 %collective-permute-done.23.refs_12_ = f32[256,256]{1,0:T(8,128)S(1)} collective-permute-done((f32[256,256]{1,0:T(8,128)S(1)}, f32[256,256]{1,0:T(8,128)S(1)}, u32[]{:S(2)}, u32[]{:S(2)}) %collective-permute-start.23) | collective-permute-done | bytes 262176 | tf_op jit(solution)/shard_map/ppermute | solution.py:427
  89.1 4.3 %collective-permute-done.21.refs_10_ = f32[256,256]{1,0:T(8,128)S(1)} collective-permute-done((f32[256,256]{1,0:T(8,128)S(1)}, f32[256,256]{1,0:T(8,128)S(1)}, u32[]{:S(2)}, u32[]{:S(2)}) %collective-permute-start.21) | collective-permute-done | bytes 262176 | tf_op jit(solution)/shard_map/ppermute | solution.py:427
  94.7 4.3 %collective-permute-done.20.refs_9_ = f32[256,256]{1,0:T(8,128)S(1)} collective-permute-done((f32[256,256]{1,0:T(8,128)S(1)}, f32[256,256]{1,0:T(8,128)S(1)}, u32[]{:S(2)}, u32[]{:S(2)}) %collective-permute-start.20) | collective-permute-done | bytes 262176 | tf_op jit(solution)/shard_map/ppermute | solution.py:427
  99.1 3.1 %top.2 = (f32[1024,256]{1,0:T(8,128)S(1)}, f32[9,256,256]{2,1,0:T(8,128)S(1)}) custom-call(s32[3]{0:T(128)S(1)} %pad_add_fusion.refs_0_.place, f32[320,256]{1,0:T(8,128)} %collective-permute-done.12.refs_1_, f32[256,256]{1,0:T(8,128)} %collective-permute-done.13.refs_2_, f32[256,256]{1,0:T(8,128)} %collective-permute-done.14.refs_2_.refs_3_, ...), custom_call_target="tpu_custom_call" | custom-call | flops 1207959552 | bytes 5242880 | tf_op jit(solution)/shard_map/top/pallas_call | solution.py:303
  102.2 3.5 %inner.2 = (f32[1024,256]{1,0:T(8,128)S(1)}, f32[9,256,256]{2,1,0:T(8,128)S(1)}) custom-call(s32[3]{0:T(128)S(1)} %pad_add_fusion.refs_0_.place, f32[1024,256]{1,0:T(8,128)S(1)} %get-tuple-element.93.refs_1_, bf16[2,2,1024,256]{3,2,1,0:T(8,128)(2,1)S(1)} %bitcast.13, bf16[2,2,1024,256]{3,2,1,0:T(8,128)(2,1)S(1)} %bitcast.14, ...), custom_call_target="tpu_custom_call" | custom-call | flops 2415919104 | bytes 5242880 | tf_op jit(solution)/shard_map/inner/pallas_call | solution.py:360
  105.7 4.6 %collective-permute-done.11.refs_12_ = f32[256,256]{1,0:T(8,128)S(1)} collective-permute-done((f32[256,256]{1,0:T(8,128)S(1)}, f32[256,256]{1,0:T(8,128)S(1)}, u32[]{:S(2)}, u32[]{:S(2)}) %collective-permute-start.11) | collective-permute-done | bytes 262176 | tf_op jit(solution)/shard_map/ppermute | solution.py:427
  110.3 5.4 %collective-permute-done.9.refs_10_ = f32[256,256]{1,0:T(8,128)S(1)} collective-permute-done((f32[256,256]{1,0:T(8,128)S(1)}, f32[256,256]{1,0:T(8,128)S(1)}, u32[]{:S(2)}, u32[]{:S(2)}) %collective-permute-start.9) | collective-permute-done | bytes 262176 | tf_op jit(solution)/shard_map/ppermute | solution.py:427
  115.7 2.8 %collective-permute-done.8.refs_9_ = f32[256,256]{1,0:T(8,128)S(1)} collective-permute-done((f32[256,256]{1,0:T(8,128)S(1)}, f32[256,256]{1,0:T(8,128)S(1)}, u32[]{:S(2)}, u32[]{:S(2)}) %collective-permute-start.8) | collective-permute-done | bytes 262176 | tf_op jit(solution)/shard_map/ppermute | solution.py:427
  118.5 2.9 %top.3 = (f32[1024,256]{1,0:T(8,128)S(1)}, f32[4,9,32,256]{3,2,1,0:T(8,128)S(1)}, f32[4,9,32,256]{3,2,1,0:T(8,128)S(1)}) custom-call(s32[3]{0:T(128)S(1)} %pad_add_fusion.refs_0_.place, f32[320,256]{1,0:T(8,128)} %collective-permute-done.refs_1_, f32[256,256]{1,0:T(8,128)} %collective-permute-done.1.refs_2_, ...), custom_call_target="tpu_custom_call" | custom-call | flops 1207959552 | bytes 5242880 | tf_op jit(solution)/shard_map/top/pallas_call | solution.py:303
  121.5 3.7 %inner.3 = (f32[1024,256]{1,0:T(8,128)S(1)}, f32[4,9,32,256]{3,2,1,0:T(8,128)S(1)}, f32[4,9,32,256]{3,2,1,0:T(8,128)S(1)}) custom-call(s32[3]{0:T(128)S(1)} %pad_add_fusion.refs_0_.place, f32[1024,256]{1,0:T(8,128)S(1)} %get-tuple-element.95.refs_1_, bf16[2,2,1024,256]{3,2,1,0:T(8,128)(2,1)S(1)} %bitcast.16, bf16[2,2,1024,256]{3,2,1,0:T(8,128)(2,1)S(1)} %bitcast.17, ...), custom_call_target="tpu_custom_call" | custom-call | flops 2415919104 | bytes 5242880 | tf_op jit(solution)/shard_map/inner/pallas_call | solution.py:360
  126.4 3.5 %collective-permute-start.35 = (f32[9,32,256]{2,1,0:T(8,128)S(1)}, f32[9,32,256]{2,1,0:T(8,128)S(1)}, u32[]{:S(2)}, u32[]{:S(2)}) collective-permute-start(f32[9,32,256]{2,1,0:T(8,128)S(1)} %get-tuple-element.109), channel_id=1, source_target_pairs={{0,2},{1,3},{6,4},{7,5},{8,10},{9,11},{14,12},{15,13},{16,18},{17,... | collective-permute-start | bytes 884744 | tf_op jit(solution)/shard_map/ppermute | solution.py:542
  130.6 1.7 collective-permute-start.28
  135.0 2.3 %collective-permute-done.35.arrived = f32[9,32,256]{2,1,0:T(8,128)S(1)} collective-permute-done((f32[9,32,256]{2,1,0:T(8,128)S(1)}, f32[9,32,256]{2,1,0:T(8,128)S(1)}, u32[]{:S(2)}, u32[]{:S(2)}) %collective-permute-start.35) | collective-permute-done | bytes 294944 | tf_op jit(solution)/shard_map/ppermute | solution.py:542
  138.5 5.1 %collective-permute-done.28.arrived = f32[9,32,256]{2,1,0:T(8,128)S(1)} collective-permute-done((f32[9,32,256]{2,1,0:T(8,128)S(1)}, f32[9,32,256]{2,1,0:T(8,128)S(1)}, u32[]{:S(2)}, u32[]{:S(2)}) %collective-permute-start.28) | collective-permute-done | bytes 294944 | tf_op jit(solution)/shard_map/ppermute | solution.py:542
  144.8 7.2 %collective-permute-start.32 = (f32[9,32,256]{2,1,0:T(8,128)S(1)}, f32[9,32,256]{2,1,0:T(8,128)S(1)}, u32[]{:S(2)}, u32[]{:S(2)}) collective-permute-start(f32[9,32,256]{2,1,0:T(8,128)S(1)} %get-tuple-element.107), channel_id=1, source_target_pairs={{0,2},{1,3},{6,4},{7,5},{8,10},{9,11},{14,12},{15,13},{16,18},{17,... | collective-permute-start | bytes 884744 | tf_op jit(solution)/shard_map/ppermute | solution.py:542
  152.1 2.2 %collective-permute-start.25 = (f32[9,32,256]{2,1,0:T(8,128)S(1)}, f32[9,32,256]{2,1,0:T(8,128)S(1)}, u32[]{:S(2)}, u32[]{:S(2)}) collective-permute-start(f32[9,32,256]{2,1,0:T(8,128)S(1)} %get-tuple-element.101), channel_id=1, source_target_pairs={{0,2},{1,3},{6,4},{7,5},{8,10},{9,11},{14,12},{15,13},{16,18},{17,... | collective-permute-start | bytes 884744 | tf_op jit(solution)/shard_map/ppermute | solution.py:542
  154.9 1.3 collective-permute-done.26.arrived
  160.6 1.9 %collective-permute-done.32.refs_0_ = f32[9,32,256]{2,1,0:T(8,128)S(1)} collective-permute-done((f32[9,32,256]{2,1,0:T(8,128)S(1)}, f32[9,32,256]{2,1,0:T(8,128)S(1)}, u32[]{:S(2)}, u32[]{:S(2)}) %collective-permute-start.32) | collective-permute-done | bytes 294944 | tf_op jit(solution)/shard_map/ppermute | solution.py:542
  163.8 2.4 %lower.2.refs_0_ = f32[2,1024,256]{2,1,0:T(8,128)} custom-call(f32[1024,256]{1,0:T(8,128)S(1)} %get-tuple-element.94.refs_17_.adjoint, bf16[1024,256]{1,0:T(8,128)(2,1)S(1)} %copy-done.3, bf16[9,256,256]{2,1,0:T(8,128)(2,1)S(1)} %get-tuple-element.56.refs_2_.refs_4_.refs_5_.kernel), custom_call_target="tpu_custom_call" | custom-call | flops 1207959552 | bytes 3145728 | tf_op jit(solution)/shard_map/lower/pallas_call | solution.py:387
  166.3 2.4 %lower.3 = f32[2,1024,256]{2,1,0:T(8,128)} custom-call(f32[1024,256]{1,0:T(8,128)S(1)} %get-tuple-element.97.adjoint, bf16[1024,256]{1,0:T(8,128)(2,1)S(1)} %copy-done.5, bf16[9,256,256]{2,1,0:T(8,128)(2,1)S(1)} %get-tuple-element.56.refs_2_.refs_4_.refs_5_.kernel, f32[2,1024,256]{2,1,0:T(8,128)} %lower.2.refs_0_), custom_call_target="tpu_custom_call", output_to_operand_aliasing={{}: (3, {})} | custom-call | flops 1207959552 | bytes 3145728 | tf_op jit(solution)/shard_map/lower/pallas_call | solution.py:387
  168.7 3.3 %collective-permute-done.37.refs_2_ = f32[9,32,256]{2,1,0:T(8,128)S(1)} collective-permute-done((f32[9,32,256]{2,1,0:T(8,128)S(1)}, f32[9,32,256]{2,1,0:T(8,128)S(1)}, u32[]{:S(2)}, u32[]{:S(2)}) %collective-permute-start.37) | collective-permute-done | bytes 294944 | tf_op jit(solution)/shard_map/ppermute | solution.py:542
  172.0 1.3 total.2.refs_3_
  173.4 2.7 %collective-permute-done.30.refs_2_ = f32[9,32,256]{2,1,0:T(8,128)S(1)} collective-permute-done((f32[9,32,256]{2,1,0:T(8,128)S(1)}, f32[9,32,256]{2,1,0:T(8,128)S(1)}, u32[]{:S(2)}, u32[]{:S(2)}) %collective-permute-start.30) | collective-permute-done | bytes 294944 | tf_op jit(solution)/shard_map/ppermute | solution.py:542
  (104 shorter events, 52.7 us)
Async XLA Ops:
  3.4 17.5 %collective-permute-start.12 = (f32[320,256]{1,0:T(8,128)}, f32[320,256]{1,0:T(8,128)}, u32[]{:S(2)}, u32[]{:S(2)}) collective-permute-start(f32[320,256]{1,0:T(8,128)} %section_end.5.refs_5_.refs_6_), channel_id=1, source_target_pairs={{24,16},{25,17},{26,18},{27,19},{28,20},{29,21},{30,22},{31,23}} | collective-permute-start | bytes 983048 | tf_op jit(solution)/shard_map/ppermute | solution.py:427
  10.3 13.5 %collective-permute-start.13 = (f32[256,256]{1,0:T(8,128)}, f32[256,256]{1,0:T(8,128)}, u32[]{:S(2)}, u32[]{:S(2)}) collective-permute-start(f32[256,256]{1,0:T(8,128)} %get-tuple-element.75.refs_7_.refs_6_), channel_id=1, source_target_pairs={{24,16},{25,17},{26,18},{27,19},{28,20},{29,21},{30,22},{31,23}} | collective-permute-start | bytes 786440 | tf_op jit(solution)/shard_map/ppermute | solution.py:427
  11.7 14.1 %collective-permute-start.14 = (f32[256,256]{1,0:T(8,128)}, f32[256,256]{1,0:T(8,128)}, u32[]{:S(2)}, u32[]{:S(2)}) collective-permute-start(f32[256,256]{1,0:T(8,128)} %get-tuple-element.76.refs_7_.refs_6_), channel_id=1, source_target_pairs={{24,16},{25,17},{26,18},{27,19},{28,20},{29,21},{30,22},{31,23}} | collective-permute-start | bytes 786440 | tf_op jit(solution)/shard_map/ppermute | solution.py:427
  18.2 10.2 %collective-permute-start = (f32[320,256]{1,0:T(8,128)}, f32[320,256]{1,0:T(8,128)}, u32[]{:S(2)}, u32[]{:S(2)}) collective-permute-start(f32[320,256]{1,0:T(8,128)} %get-tuple-element.57.refs_5_.refs_6_), channel_id=1, source_target_pairs={{24,16},{25,17},{26,18},{27,19},{28,20},{29,21},{30,22},{31,23}} | collective-permute-start | bytes 983048 | tf_op jit(solution)/shard_map/ppermute | solution.py:427
  19.5 8.1 %collective-permute-start.1 = (f32[256,256]{1,0:T(8,128)}, f32[256,256]{1,0:T(8,128)}, u32[]{:S(2)}, u32[]{:S(2)}) collective-permute-start(f32[256,256]{1,0:T(8,128)} %get-tuple-element.58.refs_7_.refs_6_), channel_id=1, source_target_pairs={{24,16},{25,17},{26,18},{27,19},{28,20},{29,21},{30,22},{31,23}} | collective-permute-start | bytes 786440 | tf_op jit(solution)/shard_map/ppermute | solution.py:427
  21.0 10.4 %collective-permute-start.2 = (f32[256,256]{1,0:T(8,128)S(1)}, f32[256,256]{1,0:T(8,128)S(1)}, u32[]{:S(2)}, u32[]{:S(2)}) collective-permute-start(f32[256,256]{1,0:T(8,128)S(1)} %get-tuple-element.59.refs_7_.refs_6_), channel_id=1, source_target_pairs={{24,16},{25,17},{26,18},{27,19},{28,20},{29,21},{30,22},{31,23}} | collective-permute-start | bytes 786440 | tf_op jit(solution)/shard_map/ppermute | solution.py:427
  25.1 8.6 %collective-permute-start.17 = (f32[256,256]{1,0:T(8,128)S(1)}, f32[256,256]{1,0:T(8,128)S(1)}, u32[]{:S(2)}, u32[]{:S(2)}) collective-permute-start(f32[256,256]{1,0:T(8,128)S(1)} %get-tuple-element.82), channel_id=1, source_target_pairs={{16,8},{17,9},{18,10},{19,11},{20,12},{21,13},{22,14},{23,15}} | collective-permute-start | bytes 786440 | tf_op jit(solution)/shard_map/ppermute | solution.py:427
  27.0 8.4 %collective-permute-start.18 = (f32[256,256]{1,0:T(8,128)S(1)}, f32[256,256]{1,0:T(8,128)S(1)}, u32[]{:S(2)}, u32[]{:S(2)}) collective-permute-start(f32[256,256]{1,0:T(8,128)S(1)} %get-tuple-element.84), channel_id=1, source_target_pairs={{16,8},{17,9},{18,10},{19,11},{20,12},{21,13},{22,14},{23,15}} | collective-permute-start | bytes 786440 | tf_op jit(solution)/shard_map/ppermute | solution.py:427
  27.7 8.4 %collective-permute-start.16 = (f32[288,256]{1,0:T(8,128)S(1)}, f32[288,256]{1,0:T(8,128)S(1)}, u32[]{:S(2)}, u32[]{:S(2)}) collective-permute-start(f32[288,256]{1,0:T(8,128)S(1)} %get-tuple-element.80), channel_id=1, source_target_pairs={{16,8},{17,9},{18,10},{19,11},{20,12},{21,13},{22,14},{23,15}} | collective-permute-start | bytes 884744 | tf_op jit(solution)/shard_map/ppermute | solution.py:427
  31.4 15.4 %collective-permute-start.4 = (f32[288,256]{1,0:T(8,128)S(1)}, f32[288,256]{1,0:T(8,128)S(1)}, u32[]{:S(2)}, u32[]{:S(2)}) collective-permute-start(f32[288,256]{1,0:T(8,128)S(1)} %get-tuple-element.63), channel_id=1, source_target_pairs={{16,8},{17,9},{18,10},{19,11},{20,12},{21,13},{22,14},{23,15}} | collective-permute-start | bytes 884744 | tf_op jit(solution)/shard_map/ppermute | solution.py:427
  33.0 10.5 %collective-permute-start.5 = (f32[256,256]{1,0:T(8,128)S(1)}, f32[256,256]{1,0:T(8,128)S(1)}, u32[]{:S(2)}, u32[]{:S(2)}) collective-permute-start(f32[256,256]{1,0:T(8,128)S(1)} %get-tuple-element.65), channel_id=1, source_target_pairs={{16,8},{17,9},{18,10},{19,11},{20,12},{21,13},{22,14},{23,15}} | collective-permute-start | bytes 786440 | tf_op jit(solution)/shard_map/ppermute | solution.py:427
  33.7 11.2 %collective-permute-start.6 = (f32[256,256]{1,0:T(8,128)S(1)}, f32[256,256]{1,0:T(8,128)S(1)}, u32[]{:S(2)}, u32[]{:S(2)}) collective-permute-start(f32[256,256]{1,0:T(8,128)S(1)} %get-tuple-element.67), channel_id=1, source_target_pairs={{16,8},{17,9},{18,10},{19,11},{20,12},{21,13},{22,14},{23,15}} | collective-permute-start | bytes 786440 | tf_op jit(solution)/shard_map/ppermute | solution.py:427
  40.0 42.2 %collective-permute-start.22 = (f32[256,256]{1,0:T(8,128)S(1)}, f32[256,256]{1,0:T(8,128)S(1)}, u32[]{:S(2)}, u32[]{:S(2)}) collective-permute-start(f32[256,256]{1,0:T(8,128)S(1)} %get-tuple-element.90), channel_id=1, source_target_pairs={{8,0},{9,1},{10,2},{11,3},{12,4},{13,5},{14,6},{15,7}} | collective-permute-start | bytes 786440 | tf_op jit(solution)/shard_map/ppermute | solution.py:427
  42.3 45.6 %collective-permute-start.23 = (f32[256,256]{1,0:T(8,128)S(1)}, f32[256,256]{1,0:T(8,128)S(1)}, u32[]{:S(2)}, u32[]{:S(2)}) collective-permute-start(f32[256,256]{1,0:T(8,128)S(1)} %stage.31), channel_id=1, source_target_pairs={{8,0},{9,1},{10,2},{11,3},{12,4},{13,5},{14,6},{15,7}} | collective-permute-start | bytes 786440 | tf_op jit(solution)/shard_map/ppermute | solution.py:427
  43.6 49.9 %collective-permute-start.21 = (f32[256,256]{1,0:T(8,128)S(1)}, f32[256,256]{1,0:T(8,128)S(1)}, u32[]{:S(2)}, u32[]{:S(2)}) collective-permute-start(f32[256,256]{1,0:T(8,128)S(1)} %get-tuple-element.88), channel_id=1, source_target_pairs={{8,0},{9,1},{10,2},{11,3},{12,4},{13,5},{14,6},{15,7}} | collective-permute-start | bytes 786440 | tf_op jit(solution)/shard_map/ppermute | solution.py:427
  44.9 54.2 %collective-permute-start.20 = (f32[256,256]{1,0:T(8,128)S(1)}, f32[256,256]{1,0:T(8,128)S(1)}, u32[]{:S(2)}, u32[]{:S(2)}) collective-permute-start(f32[256,256]{1,0:T(8,128)S(1)} %get-tuple-element.86), channel_id=1, source_target_pairs={{8,0},{9,1},{10,2},{11,3},{12,4},{13,5},{14,6},{15,7}} | collective-permute-start | bytes 786440 | tf_op jit(solution)/shard_map/ppermute | solution.py:427
  50.7 55.0 %collective-permute-start.10 = (f32[256,256]{1,0:T(8,128)S(1)}, f32[256,256]{1,0:T(8,128)S(1)}, u32[]{:S(2)}, u32[]{:S(2)}) collective-permute-start(f32[256,256]{1,0:T(8,128)S(1)} %get-tuple-element.73), channel_id=1, source_target_pairs={{8,0},{9,1},{10,2},{11,3},{12,4},{13,5},{14,6},{15,7}} | collective-permute-start | bytes 786440 | tf_op jit(solution)/shard_map/ppermute | solution.py:427
  82.2 28.1 %collective-permute-start.11 = (f32[256,256]{1,0:T(8,128)S(1)}, f32[256,256]{1,0:T(8,128)S(1)}, u32[]{:S(2)}, u32[]{:S(2)}) collective-permute-start(f32[256,256]{1,0:T(8,128)S(1)} %stage.23), channel_id=1, source_target_pairs={{8,0},{9,1},{10,2},{11,3},{12,4},{13,5},{14,6},{15,7}} | collective-permute-start | bytes 786440 | tf_op jit(solution)/shard_map/ppermute | solution.py:427
  87.8 27.8 %collective-permute-start.9 = (f32[256,256]{1,0:T(8,128)S(1)}, f32[256,256]{1,0:T(8,128)S(1)}, u32[]{:S(2)}, u32[]{:S(2)}) collective-permute-start(f32[256,256]{1,0:T(8,128)S(1)} %get-tuple-element.71), channel_id=1, source_target_pairs={{8,0},{9,1},{10,2},{11,3},{12,4},{13,5},{14,6},{15,7}} | collective-permute-start | bytes 786440 | tf_op jit(solution)/shard_map/ppermute | solution.py:427
  93.5 25.0 %collective-permute-start.8 = (f32[256,256]{1,0:T(8,128)S(1)}, f32[256,256]{1,0:T(8,128)S(1)}, u32[]{:S(2)}, u32[]{:S(2)}) collective-permute-start(f32[256,256]{1,0:T(8,128)S(1)} %get-tuple-element.69), channel_id=1, source_target_pairs={{8,0},{9,1},{10,2},{11,3},{12,4},{13,5},{14,6},{15,7}} | collective-permute-start | bytes 786440 | tf_op jit(solution)/shard_map/ppermute | solution.py:427
  126.4 10.8 %collective-permute-start.35 = (f32[9,32,256]{2,1,0:T(8,128)S(1)}, f32[9,32,256]{2,1,0:T(8,128)S(1)}, u32[]{:S(2)}, u32[]{:S(2)}) collective-permute-start(f32[9,32,256]{2,1,0:T(8,128)S(1)} %get-tuple-element.109), channel_id=1, source_target_pairs={{0,2},{1,3},{6,4},{7,5},{8,10},{9,11},{14,12},{15,13},{16,18},{17,... | collective-permute-start | bytes 884744 | tf_op jit(solution)/shard_map/ppermute | solution.py:542
  130.6 12.9 %collective-permute-start.28 = (f32[9,32,256]{2,1,0:T(8,128)S(1)}, f32[9,32,256]{2,1,0:T(8,128)S(1)}, u32[]{:S(2)}, u32[]{:S(2)}) collective-permute-start(f32[9,32,256]{2,1,0:T(8,128)S(1)} %get-tuple-element.103), channel_id=1, source_target_pairs={{0,2},{1,3},{6,4},{7,5},{8,10},{9,11},{14,12},{15,13},{16,18},{17,... | collective-permute-start | bytes 884744 | tf_op jit(solution)/shard_map/ppermute | solution.py:542
  132.4 19.7 %collective-permute-start.33 = (f32[9,32,256]{2,1,0:T(8,128)S(1)}, f32[9,32,256]{2,1,0:T(8,128)S(1)}, u32[]{:S(2)}, u32[]{:S(2)}) collective-permute-start(f32[9,32,256]{2,1,0:T(8,128)S(1)} %get-tuple-element.108), channel_id=1, source_target_pairs={{0,2},{1,3},{6,4},{7,5},{8,10},{9,11},{14,12},{15,13},{16,18},{17,... | collective-permute-start | bytes 884744 | tf_op jit(solution)/shard_map/ppermute | solution.py:542
  133.7 22.5 %collective-permute-start.26 = (f32[9,32,256]{2,1,0:T(8,128)S(1)}, f32[9,32,256]{2,1,0:T(8,128)S(1)}, u32[]{:S(2)}, u32[]{:S(2)}) collective-permute-start(f32[9,32,256]{2,1,0:T(8,128)S(1)} %get-tuple-element.102), channel_id=1, source_target_pairs={{0,2},{1,3},{6,4},{7,5},{8,10},{9,11},{14,12},{15,13},{16,18},{17,... | collective-permute-start | bytes 884744 | tf_op jit(solution)/shard_map/ppermute | solution.py:542
  137.8 19.6 %collective-permute-start.36 = (f32[9,32,256]{2,1,0:T(8,128)S(1)}, f32[9,32,256]{2,1,0:T(8,128)S(1)}, u32[]{:S(2)}, u32[]{:S(2)}) collective-permute-start(f32[9,32,256]{2,1,0:T(8,128)S(1)} %relay.10), channel_id=1, source_target_pairs={{2,4},{3,5},{4,2},{5,3},{10,12},{11,13},{12,10},{13,11},{18,20},{1... | collective-permute-start | bytes 884744 | tf_op jit(solution)/shard_map/ppermute | solution.py:542
  144.2 15.2 %collective-permute-start.29 = (f32[9,32,256]{2,1,0:T(8,128)S(1)}, f32[9,32,256]{2,1,0:T(8,128)S(1)}, u32[]{:S(2)}, u32[]{:S(2)}) collective-permute-start(f32[9,32,256]{2,1,0:T(8,128)S(1)} %relay.7), channel_id=1, source_target_pairs={{2,4},{3,5},{4,2},{5,3},{10,12},{11,13},{12,10},{13,11},{18,20},{1... | collective-permute-start | bytes 884744 | tf_op jit(solution)/shard_map/ppermute | solution.py:542
  144.8 17.7 %collective-permute-start.32 = (f32[9,32,256]{2,1,0:T(8,128)S(1)}, f32[9,32,256]{2,1,0:T(8,128)S(1)}, u32[]{:S(2)}, u32[]{:S(2)}) collective-permute-start(f32[9,32,256]{2,1,0:T(8,128)S(1)} %get-tuple-element.107), channel_id=1, source_target_pairs={{0,2},{1,3},{6,4},{7,5},{8,10},{9,11},{14,12},{15,13},{16,18},{17,... | collective-permute-start | bytes 884744 | tf_op jit(solution)/shard_map/ppermute | solution.py:542
  152.1 21.3 %collective-permute-start.25 = (f32[9,32,256]{2,1,0:T(8,128)S(1)}, f32[9,32,256]{2,1,0:T(8,128)S(1)}, u32[]{:S(2)}, u32[]{:S(2)}) collective-permute-start(f32[9,32,256]{2,1,0:T(8,128)S(1)} %get-tuple-element.101), channel_id=1, source_target_pairs={{0,2},{1,3},{6,4},{7,5},{8,10},{9,11},{14,12},{15,13},{16,18},{17,... | collective-permute-start | bytes 884744 | tf_op jit(solution)/shard_map/ppermute | solution.py:542
  156.2 12.5 %collective-permute-start.34 = (f32[9,32,256]{2,1,0:T(8,128)S(1)}, f32[9,32,256]{2,1,0:T(8,128)S(1)}, u32[]{:S(2)}, u32[]{:S(2)}) collective-permute-start(f32[9,32,256]{2,1,0:T(8,128)S(1)} %relay.9), channel_id=1, source_target_pairs={{2,4},{3,5},{4,2},{5,3},{10,12},{11,13},{12,10},{13,11},{18,20},{1... | collective-permute-start | bytes 884744 | tf_op jit(solution)/shard_map/ppermute | solution.py:542
  158.1 14.0 %collective-permute-start.37 = (f32[9,32,256]{2,1,0:T(8,128)S(1)}, f32[9,32,256]{2,1,0:T(8,128)S(1)}, u32[]{:S(2)}, u32[]{:S(2)}) collective-permute-start(f32[9,32,256]{2,1,0:T(8,128)S(1)} %relay.11), channel_id=1, source_target_pairs={{4,6},{5,7},{2,0},{3,1},{12,14},{13,15},{10,8},{11,9},{20,22},{21,... | collective-permute-start | bytes 884744 | tf_op jit(solution)/shard_map/ppermute | solution.py:542
  159.4 14.0 %collective-permute-start.27 = (f32[9,32,256]{2,1,0:T(8,128)S(1)}, f32[9,32,256]{2,1,0:T(8,128)S(1)}, u32[]{:S(2)}, u32[]{:S(2)}) collective-permute-start(f32[9,32,256]{2,1,0:T(8,128)S(1)} %relay.6), channel_id=1, source_target_pairs={{2,4},{3,5},{4,2},{5,3},{10,12},{11,13},{12,10},{13,11},{18,20},{1... | collective-permute-start | bytes 884744 | tf_op jit(solution)/shard_map/ppermute | solution.py:542
  162.5 13.5 %collective-permute-start.30 = (f32[9,32,256]{2,1,0:T(8,128)S(1)}, f32[9,32,256]{2,1,0:T(8,128)S(1)}, u32[]{:S(2)}, u32[]{:S(2)}) collective-permute-start(f32[9,32,256]{2,1,0:T(8,128)S(1)} %relay.8), channel_id=1, source_target_pairs={{4,6},{5,7},{2,0},{3,1},{12,14},{13,15},{10,8},{11,9},{20,22},{21,... | collective-permute-start | bytes 884744 | tf_op jit(solution)/shard_map/ppermute | solution.py:542
  (18 other events, 140.9 us)

commit v3 on v2

--- a/solution.py
+++ b/solution.py
@@ -108,7 +108,7 @@
     return pltpu.with_memory_space_constraint(x, pltpu.HBM)
 
 
-def section_end_of(guess, slopes, kernel, image, cuts, width, keep):
+def section_end_of(guess, slopes, kernel, image, cuts, width, keep, after=()):
     layers, _, pixels, channels = guess.shape
     height = pixels // width
     low, high = cuts[0], cuts[-1]
@@ -131,6 +131,8 @@
         if kernel.ndim == 4:
             out_shape.append(jax.ShapeDtypeStruct(taps, kernel.dtype))
             copies.append(2)
+    args += after
+    in_specs += [pl.BlockSpec(memory_space=pltpu.SMEM)] * len(after)
     return pl.pallas_call(
         functools.partial(end_kernel, width, first, low, shapes, len(args) - 3, copies),
         out_shape=out_shape,
@@ -238,13 +240,15 @@
             acc[3 * a + b] = term * scale if scale != 1.0 else term
 
 
-def hand_out(acc, side, mine, away, share):
-    for node in range(mine.shape[0]):
-        base = 2 * node * share
-        kept = pl.multiple_of(base + side * share, share)
-        sent = pl.multiple_of(base + (1 - side) * share, share)
-        mine[node] = acc[:, pl.ds(kept, share), :]
-        away[node] = acc[:, pl.ds(sent, share), :]
+def hand_out(acc, side, outs, share):
+    nodes = len(outs)
+    for group in range(nodes // 2):
+        for place, node in enumerate((group, nodes - 1 - group)):
+            base = 2 * node * share
+            kept = pl.multiple_of(base + side * share, share)
+            sent = pl.multiple_of(base + (1 - side) * share, share)
+            outs[2 * group][place] = acc[:, pl.ds(kept, share), :]
+            outs[2 * group + 1][place] = acc[:, pl.ds(sent, share), :]
 
 
 def top_kernel(width, hops, final, scale, share, *refs):
@@ -256,7 +260,7 @@
     guess, slope, states = refs[:3]
     refs = refs[3:]
     if final:
-        before, _, adjoint, mine, away, acc, zs = refs
+        before, _, adjoint, *outs, acc, zs = refs
     else:
         before = None
         adjoint, acc, zs = refs
@@ -280,14 +284,14 @@
     fill(zs, width, slope[...].astype(f32) * adjoint[...], width)
     grads_into(acc, zs, states, width, scale, before)
     if final:
-        hand_out(acc, place[1], mine, away, share)
+        hand_out(acc, place[1], outs, share)
 
 
 def top_of(place, arrived, guess, slopes, states, before, after, image, width, scale, share):
     layers, _, pixels, channels = slopes.shape
     final = before is not None
     grad = (9, channels, channels)
-    split = (channels // share // 2, 9, share, channels)
+    split = (2, 9, share, channels)
     tile = window((pixels, channels), (layers - 1, image), 0)
     pieces = [p for hop in arrived for p in hop]
     in_specs = [pl.BlockSpec(memory_space=pltpu.SMEM)]
@@ -295,8 +299,8 @@
     out_shape = [jax.ShapeDtypeStruct((pixels, channels), f32)]
     scratch = [pltpu.VMEM((3, pixels + 2 * width, channels), bf16)]
     if final:
-        in_specs += [whole(grad), pl.BlockSpec(memory_space=pl.ANY)]
-        out_shape += [jax.ShapeDtypeStruct(split, f32)] * 2
+        in_specs += [whole(grad), pl.BlockSpec(memory_space=pltpu.HBM)]
+        out_shape += [jax.ShapeDtypeStruct(split, f32)] * (channels // share // 2)
         scratch.insert(0, pltpu.VMEM(grad, f32))
     else:
         out_shape.append(jax.ShapeDtypeStruct(grad, f32))
@@ -308,9 +312,9 @@
         out_specs=[whole(s.shape) for s in out_shape],
         scratch_shapes=scratch,
         cost_estimate=cost(pixels, channels, 9, pixels * channels * 20),
-        compiler_params=limits(36),
+        compiler_params=limits(24),
         name="top",
-    )(place, *pieces, guess, slopes, states, *((before, after) if final else ()))
+    )(place, *pieces, guess, slopes, states, *((before, in_hbm(after)) if final else ()))
 
 
 def inner_kernel(width, final, scale, share, *refs):
@@ -318,7 +322,7 @@
     refs = list(refs[6:])
     before = refs.pop(0) if final else None
     if final:
-        below, mine, away, acc, zs, zs2 = refs
+        below, *outs, acc, zs, zs2 = refs
     else:
         below, acc, zs, zs2 = refs
     pixels = adjoint.shape[0]
@@ -333,14 +337,14 @@
     fill(zs2, width, slope[...].astype(f32) * below[...], width)
     grads_into(acc, zs2, states, width, scale, before)
     if final:
-        hand_out(acc, place[1], mine, away, share)
+        hand_out(acc, place[1], outs, share)
 
 
 def inner_of(place, adjoint, slopes, states, kernels, before, layer, image, width, scale, share):
     pixels, channels = adjoint.shape
     final = before is not None
     grad = (9, channels, channels)
-    split = (channels // share // 2, 9, share, channels)
+    split = (2, 9, share, channels)
     in_specs = [
         pl.BlockSpec(memory_space=pltpu.SMEM),
         whole((pixels, channels)),
@@ -353,7 +357,7 @@
     scratch = [pltpu.VMEM((3, pixels + 2 * width, channels), bf16)] * 2
     if final:
         in_specs.append(whole(grad))
-        out_shape += [jax.ShapeDtypeStruct(split, f32)] * 2
+        out_shape += [jax.ShapeDtypeStruct(split, f32)] * (channels // share // 2)
         scratch.insert(0, pltpu.VMEM(grad, f32))
     else:
         out_shape.append(jax.ShapeDtypeStruct(grad, f32))
@@ -365,7 +369,7 @@
         out_specs=[whole(s.shape) for s in out_shape],
         scratch_shapes=scratch,
         cost_estimate=cost(pixels, channels, 18, pixels * channels * 20),
-        compiler_params=limits(36),
+        compiler_params=limits(24),
         name="inner",
     )(place, adjoint, slopes, slopes, states, kernels, *((before,) if final else ()))
 
@@ -445,23 +449,29 @@
     return [(2 * a + side, 2 * b + side) for a, b in pairs for side in range(2)]
 
 
-def join_kernel(place, mine, got, held, *outs):
+def join_kernel(items, nodes, place, mine, got, held, *outs):
     held[...] = mine[...] + got[...]
-    last = held.shape[0] - 1
-    for item, out in enumerate(outs):
-        out[...] = held[jnp.where(place[2] == 0, last - item, item)]
-
-
-def join(place, mine, got):
-    nodes, *block = mine.shape
-    shapes = [mine.shape] + [tuple(block)] * (nodes - 1)
+    for item, out in zip(items, outs):
+        out[...] = held[which_of(item, nodes, place[2] == 0)]
+
+
+def which_of(item, nodes, upward):
+    high = jnp.where(upward, 1, 0)
+    return high if 2 * item < nodes else 1 - high
+
+
+def join(place, mine, got, items, nodes):
+    block = mine.shape[1:]
+    shapes = [mine.shape] + [block] * len(items)
     return pl.pallas_call(
-        join_kernel,
+        functools.partial(join_kernel, items, nodes),
         out_shape=[jax.ShapeDtypeStruct(x, f32) for x in shapes],
         grid=(1,),
         in_specs=[pl.BlockSpec(memory_space=pltpu.SMEM)] + [whole(mine.shape)] * 2,
         out_specs=[whole(x) for x in shapes],
-        cost_estimate=pl.CostEstimate(flops=mine.size, bytes_accessed=16 * mine.size, transcendentals=0),
+        cost_estimate=pl.CostEstimate(
+            flops=mine.size, bytes_accessed=16 * mine.size, transcendentals=0
+        ),
         compiler_params=limits(16),
         name="join",
     )(place, mine, got)
@@ -471,12 +481,11 @@
     out[...] = held[...] + arrived[...]
 
 
-def relay(place, held, arrived, wave, item):
-    last = held.shape[0] - 1
-    block = held.shape[1:]
+def relay(place, held, arrived, wave, item, nodes):
+    block = arrived.shape
 
     def which(_, place):
-        return (jnp.where(place[2] == wave - 1, last - item, item), 0, 0, 0)
+        return (which_of(item, nodes, place[2] == wave - 1), 0, 0, 0)
 
     return pl.pallas_call(
         relay_kernel,
@@ -495,58 +504,82 @@
     )(place, held, arrived)
 
 
-def total_kernel(nodes, place, held, *refs):
-    arrived, out = refs[: nodes - 1], refs[-1]
-    out[...] = held[...]
+def total_kernel(nodes, place, *refs):
+    held, arrived, out = refs[: nodes // 2], refs[nodes // 2 : nodes // 2 + nodes - 1], refs[-1]
+    node = place[2]
+    for group, block in enumerate(held):
+
+        @pl.when((node == group) | (node == nodes - 1 - group))
+        def _(block=block):
+            out[...] = block[...]
+
     for wave, piece in enumerate(arrived, 1):
 
-        @pl.when((place[2] == wave) | (place[2] == nodes - 1 - wave))
+        @pl.when((node == wave) | (node == nodes - 1 - wave))
         def _(piece=piece):
             out[...] = out[...] + piece[...]
 
 
 def total(place, held, arrived, layer, layers, into):
-    nodes, *block = held.shape
+    nodes = 2 * len(held)
+    block = held[0].shape[1:]
+
+    def which(_, place):
+        return (jnp.where(2 * place[2] < nodes, 0, 1), 0, 0, 0)
+
     return pl.pallas_call(
         functools.partial(total_kernel, nodes),
         out_shape=jax.ShapeDtypeStruct((layers, *block), f32),
         grid_spec=pltpu.PrefetchScalarGridSpec(
             num_scalar_prefetch=1,
             grid=(1,),
-            in_specs=[pl.BlockSpec((None, *block), lambda _, place: (place[2], 0, 0, 0))]
-            + [whole(tuple(block))] * len(arrived)
+            in_specs=[pl.BlockSpec((None, *block), which)] * len(held)
+            + [whole(block)] * len(arrived)
             + [pl.BlockSpec(memory_space=pl.ANY)] * len(into),
             out_specs=pl.BlockSpec((None, *block), lambda *_: (layer, 0, 0, 0)),
         ),
-        input_output_aliases={2 + len(arrived): 0} if into else {},
+        input_output_aliases={1 + len(held) + len(arrived): 0} if into else {},
         cost_estimate=pl.CostEstimate(
-            flops=held.size, bytes_accessed=4 * held.size, transcendentals=0
+            flops=nodes * arrived[0].size, bytes_accessed=12 * arrived[0].size, transcendentals=0
         ),
         compiler_params=limits(12),
         name="total",
-    )(place, held, *arrived, *into)
-
-
-def line_sum(place, mine, away, layer, layers, into):
+    )(place, *held, *arrived, *into)
+
+
+def line_sum(place, terms, layer, layers, into):
     replicas = lax.axis_size("dp")
     nodes = replicas // 2
-    got = lax.ppermute(away, "dp", [(i, i ^ 1) for i in range(replicas)])
-    held, *sends = join(place, mine, got)
+    got = []
+    for group in range(nodes // 2):
+        pairs = [(i, i ^ 1) for i in range(replicas)]
+        got.append(lax.ppermute(terms[2 * group + 1], "dp", pairs))
+    held, sends = [], {}
+    for group in range(nodes // 2):
+        items = [item for item in (group, nodes - 1 - group) if item < nodes - 1]
+        both, *outs = join(place, terms[2 * group], got[group], items, nodes)
+        held.append(both)
+        sends.update(zip(items, outs))
     arrived = {}
     for wave in range(1, nodes):
         pairs = both_sides([(wave - 1, wave), (nodes - wave, nodes - 1 - wave)])
         for item in range(nodes - wave):
             out = sends[item]
             if wave > 1:
-                out = relay(place, held, arrived[wave - 1, item], wave, item)
+                group = held[min(item, nodes - 1 - item)]
+                out = relay(place, group, arrived[wave - 1, item], wave, item, nodes)
             arrived[wave, item] = lax.ppermute(out, "dp", pairs)
     last = [arrived[wave, nodes - 1 - wave] for wave in range(1, nodes)]
     return total(place, held, last, layer, layers, into)
 
 
-def plain_sum(mine, away):
-    nodes, taps, share, channels = mine.shape
+def plain_sum(terms):
+    nodes = len(terms)
+    taps, share, channels = terms[0].shape[1:]
     side = lax.axis_index("dp") % 2
+    order = [(min(k, nodes - 1 - k), int(2 * k >= nodes)) for k in range(nodes)]
+    mine = jnp.stack([terms[2 * group][place] for group, place in order])
+    away = jnp.stack([terms[2 * group + 1][place] for group, place in order])
     first, second = jnp.where(side == 0, mine, away), jnp.where(side == 0, away, mine)
     terms = jnp.stack([first, second], axis=1).reshape(2 * nodes, taps, share, channels)
     return lax.psum_scatter(terms, "dp", scatter_dimension=0, tiled=False)
@@ -563,7 +596,9 @@
     place = jnp.stack([lax.axis_index("layer"), device % 2, device // 2]).astype(jnp.int32)
     cuts = cuts_of(height, sections - 1)
     first = section_end_of(guess, slopes, kernels, 0, cuts[0][:2], width, False)
-    *rest, last, slope, kernel = section_end_of(guess, slopes, kernels, 0, cuts[0][1:], width, True)
+    *rest, last, slope, kernel = section_end_of(
+        guess, slopes, kernels, 0, cuts[0][1:], width, True, [place]
+    )
     ends, lasts, slopes_of = [[*first, *rest]], [last], [slope]
     for i in range(1, images):
         *rest, last, slope = section_end_of(guess, slopes, kernel, i, cuts[0], width, True)
@@ -574,13 +609,14 @@
     scale = step_size / (images * replicas)
     adjoints = [None] * images
     grads = [None] * layers
+    lower = ()
     for i in range(images):
         final = i == images - 1
         for layer in range(layers - 1, -1, -1):
             if layer == layers - 1:
                 adjoints[i], *grads[layer] = top_of(
                     place, arrivals[i], lasts[i], slopes, states,
-                    grads[layer][0] if final else None, adjoints[i - 1] if final else None, i,
+                    grads[layer][0] if final else None, lower[0] if final else None, i,
                     width, scale if final else 1.0, share,
                 )
             else:
@@ -589,16 +625,14 @@
                     grads[layer][0] if final else None, layer, i, width,
                     scale if final else 1.0, share,
                 )
-    lower = ()
-    for i in range(images):
         lower = (lower_of(adjoints[i], slopes_of[i], kernel, i, images, lower, width),)
     if replicas in (4, 8):
         gradients = ()
         for layer in range(layers - 1, -1, -1):
-            gradients = (line_sum(place, *grads[layer], layer, layers, gradients),)
+            gradients = (line_sum(place, grads[layer], layer, layers, gradients),)
         gradients = gradients[0]
     else:
-        gradients = jnp.stack([plain_sum(*grads[layer]) for layer in range(layers)])
+        gradients = jnp.stack([plain_sum(grads[layer]) for layer in range(layers)])
     return lower[0].reshape(1, images, height, width, channels), gradients
 
 

time: 179 us -> 177 us (0.989)
  waiting for transfers between devices: 72.1 us -> 87.4 us
  Pallas kernels: 52.1 us -> 43.1 us
  local copies, waits for them, and re-layouts: 4.06 us -> 0.02 us
  starting transfers between devices: 47.7 us -> 44.6 us
    ppermute x24, waiting for transfers between devices: 55.5 us -> 69.1 us  [chain(): arrived = lax.ppermute(rows, 'layer', pairs)]
    pallas_call x16, Pallas kernels: 16.1 us -> 8.81 us  [stage(): pl.pallas_call(functools.partial(stage_kernel, width, factor, first, low,...]
    unnamed x24 -> x6, local copies, waits for them, and re-layouts: 4.06 us -> 0.02 us
    ppermute x24, starting transfers between devices: 24.6 us -> 21.3 us  [chain(): arrived = lax.ppermute(rows, 'layer', pairs)]
  transfers between devices with their start and end apart: 38 -> 40, of which waited for: 13 -> 13; matrix products, arithmetic and copies ran while one was open for 0% -> 0% of each run, Pallas kernels for 25% -> 21%
where the time goes in v3:
time: 177 us
  waiting for transfers between devices  87.4 us (49%)
  starting transfers between devices  44.6 us (25%)
  Pallas kernels  43.1 us (24%)
    ppermute x24, waiting for transfers between devices, chain(): arrived = lax.ppermute(rows, 'layer', pairs)  69.1 us
    ppermute x12, starting transfers between devices, line_sum(): arrived[wave, item] = lax.ppermute(out, 'dp', pairs)  22.1 us
    ppermute x24, starting transfers between devices, chain(): arrived = lax.ppermute(rows, 'layer', pairs)  21.3 us
    ppermute x12, waiting for transfers between devices, line_sum(): arrived[wave, item] = lax.ppermute(out, 'dp', pairs)  18.3 us
    pallas_call x3, Pallas kernels, section_end_of(): pl.pallas_call(functools.partial(end_kernel, width, first, low, shapes, l...  8.9 us
    pallas_call x16, Pallas kernels, stage(): pl.pallas_call(functools.partial(stage_kernel, width, factor, first, low,...  8.81 us
    pallas_call x2, Pallas kernels, inner_of(): pl.pallas_call(functools.partial(inner_kernel, width, final, scale, share...  7.16 us
    pallas_call x2, Pallas kernels, lower_of(): pl.pallas_call(functools.partial(lower_kernel, width), out_shape=jax.Shap...  4.89 us
  transfers between devices with their start and end apart: 40, of which 13 were waited for; matrix products, arithmetic and copies ran while one was open for 0% of the time, Pallas kernels for 21%

profile of v3, /device:TPU:0, one launch (start us, length us, event | category | flops | bytes accessed | tf_op | source)
XLA Modules:
  0.0 176.5 jit_solution(9086251237780364612)
XLA Ops:
  0.6 2.1 %section_end.5.refs_5_.refs_6_ = f32[320,256]{1,0:T(8,128)S(1)} custom-call(f32[2,2,1024,256]{3,2,1,0:T(8,128)} %bitcast.22, bf16[2,2,1024,256]{3,2,1,0:T(8,128)(2,1)} %bitcast.7, bf16[2,9,256,256]{3,2,1,0:T(8,128)(2,1)} %refs_5_.3), custom_call_target="tpu_custom_call" | custom-call | flops 377487360 | bytes 983040 | tf_op jit(solution)/shard_map/section_end/pallas_call | solution.py:136
  3.5 3.3 %section_end.3 = (f32[256,256]{1,0:T(8,128)S(1)}, f32[256,256]{1,0:T(8,128)S(1)}, f32[192,256]{1,0:T(8,128)S(1)}, f32[1024,256]{1,0:T(8,128)S(1)}, bf16[1024,256...) custom-call(f32[2,2,1024,256]{3,2,1,0:T(8,128)} %bitcast.23, bf16[2,2,1024,256]{3,2,1,0:T(8,128)(2,1)} %bitcast.8, ...), custom_call_target="tpu_custom_call" | custom-call | flops 830472192 | bytes 2162688 | tf_op jit(solution)/shard_map/section_end/pallas_call | solution.py:136
  8.2 3.5 %section_end.4 = (f32[320,256]{1,0:T(8,128)S(1)}, f32[256,256]{1,0:T(8,128)S(1)}, f32[256,256]{1,0:T(8,128)S(1)}, f32[192,256]{1,0:T(8,128)S(1)}, f32[1024,256]{...) custom-call(f32[2,2,1024,256]{3,2,1,0:T(8,128)} %bitcast.25, bf16[2,2,1024,256]{3,2,1,0:T(8,128)(2,1)} %bitcast.10, ...), custom_call_target="tpu_custom_call" | custom-call | flops 1207959552 | bytes 3145728 | tf_op jit(solution)/shard_map/section_end/pallas_call | solution.py:136
  30.1 1.3 collective-permute-start.20
  34.4 1.4 collective-permute-start.10
  36.4 44.3 %collective-permute-done.22.refs_11_ = f32[256,256]{1,0:T(8,128)S(1)} collective-permute-done((f32[256,256]{1,0:T(8,128)S(1)}, f32[256,256]{1,0:T(8,128)S(1)}, u32[]{:S(2)}, u32[]{:S(2)}) %collective-permute-start.22) | collective-permute-done | bytes 262176 | tf_op jit(solution)/shard_map/ppermute | solution.py:431
  82.0 4.3 %collective-permute-done.23.refs_12_ = f32[256,256]{1,0:T(8,128)S(1)} collective-permute-done((f32[256,256]{1,0:T(8,128)S(1)}, f32[256,256]{1,0:T(8,128)S(1)}, u32[]{:S(2)}, u32[]{:S(2)}) %collective-permute-start.23) | collective-permute-done | bytes 262176 | tf_op jit(solution)/shard_map/ppermute | solution.py:431
  87.6 4.3 %collective-permute-done.21.refs_10_ = f32[256,256]{1,0:T(8,128)S(1)} collective-permute-done((f32[256,256]{1,0:T(8,128)S(1)}, f32[256,256]{1,0:T(8,128)S(1)}, u32[]{:S(2)}, u32[]{:S(2)}) %collective-permute-start.21) | collective-permute-done | bytes 262176 | tf_op jit(solution)/shard_map/ppermute | solution.py:431
  93.2 4.3 %collective-permute-done.20.refs_9_ = f32[256,256]{1,0:T(8,128)S(1)} collective-permute-done((f32[256,256]{1,0:T(8,128)S(1)}, f32[256,256]{1,0:T(8,128)S(1)}, u32[]{:S(2)}, u32[]{:S(2)}) %collective-permute-start.20) | collective-permute-done | bytes 262176 | tf_op jit(solution)/shard_map/ppermute | solution.py:431
  97.6 2.4 %top.2 = (f32[1024,256]{1,0:T(8,128)S(1)}, f32[9,256,256]{2,1,0:T(8,128)S(1)}) custom-call(s32[3]{0:T(128)S(1)} %pad_add_fusion.refs_5_.refs_0_.place, f32[320,256]{1,0:T(8,128)S(1)} %collective-permute-done.12.refs_1_, f32[256,256]{1,0:T(8,128)S(1)} %collective-permute-done.13.refs_2_, f32[256,256]{1,0:T(8,128)S(1)} %collective-permute-done.14.refs_2_.refs_3_, ...), custom_call_target="tpu_custom_call" | custom-call | flops 1207959552 | bytes 5242880 | tf_op jit(solution)/shard_map/top/pallas_call | solution.py:307
  99.9 3.5 %inner.2 = (f32[1024,256]{1,0:T(8,128)S(1)}, f32[9,256,256]{2,1,0:T(8,128)S(1)}) custom-call(s32[3]{0:T(128)S(1)} %pad_add_fusion.refs_5_.refs_0_.place, f32[1024,256]{1,0:T(8,128)S(1)} %get-tuple-element.99.refs_1_, bf16[2,2,1024,256]{3,2,1,0:T(8,128)(2,1)S(1)} %bitcast.13, bf16[2,2,1024,256]{3,2,1,0:T(8,128)(2,1)S(1)} %bitcast.14, ...), custom_call_target="tpu_custom_call" | custom-call | flops 2415919104 | bytes 5242880 | tf_op jit(solution)/shard_map/inner/pallas_call | solution.py:364
  103.4 2.4 %lower.2.refs_17_.refs_0_ = f32[2,1024,256]{2,1,0:T(8,128)} custom-call(f32[1024,256]{1,0:T(8,128)S(1)} %get-tuple-element.100.adjoint, bf16[1024,256]{1,0:T(8,128)(2,1)S(1)} %get-tuple-element.85.refs_3_.refs_4_.slope, bf16[9,256,256]{2,1,0:T(8,128)(2,1)S(1)} %get-tuple-element.62.refs_2_.refs_4_.refs_5_.kernel), custom_call_target="tpu_custom_call" | custom-call | flops 1207959552 | bytes 3145728 | tf_op jit(solution)/shard_map/lower/pallas_call | solution.py:391
  105.9 2.9 %collective-permute-done.11.refs_12_ = f32[256,256]{1,0:T(8,128)S(1)} collective-permute-done((f32[256,256]{1,0:T(8,128)S(1)}, f32[256,256]{1,0:T(8,128)S(1)}, u32[]{:S(2)}, u32[]{:S(2)}) %collective-permute-start.11) | collective-permute-done | bytes 262176 | tf_op jit(solution)/shard_map/ppermute | solution.py:431
  108.8 5.6 %collective-permute-done.9.refs_10_ = f32[256,256]{1,0:T(8,128)S(1)} collective-permute-done((f32[256,256]{1,0:T(8,128)S(1)}, f32[256,256]{1,0:T(8,128)S(1)}, u32[]{:S(2)}, u32[]{:S(2)}) %collective-permute-start.9) | collective-permute-done | bytes 262176 | tf_op jit(solution)/shard_map/ppermute | solution.py:431
  114.4 3.2 %collective-permute-done.8.refs_9_ = f32[256,256]{1,0:T(8,128)S(1)} collective-permute-done((f32[256,256]{1,0:T(8,128)S(1)}, f32[256,256]{1,0:T(8,128)S(1)}, u32[]{:S(2)}, u32[]{:S(2)}) %collective-permute-start.8) | collective-permute-done | bytes 262176 | tf_op jit(solution)/shard_map/ppermute | solution.py:431
  117.6 2.3 %top.3 = (f32[1024,256]{1,0:T(8,128)S(1)}, f32[2,9,32,256]{3,2,1,0:T(8,128)S(1)}, f32[2,9,32,256]{3,2,1,0:T(8,128)S(1)}, f32[2,9,32,256]{3,2,1,0:T(8,128)S(1)}, f32[2,9,32,256]{3,2,1,0:T(8,128)S(1)}) custom-call(s32[3]{0:T(128)S(1)} %pad_add_fusion.refs_5_.refs_0_.place, f32[320,256]{1,0:T(8,128)S(1)} %collective-permute-done.refs_1_, ...), custom_call_target="tpu_custom_call" | custom-call | flops 1207959552 | bytes 5242880 | tf_op jit(solution)/shard_map/top/pallas_call | solution.py:307
  120.0 3.7 %inner.3 = (f32[1024,256]{1,0:T(8,128)S(1)}, f32[2,9,32,256]{3,2,1,0:T(8,128)S(1)}, f32[2,9,32,256]{3,2,1,0:T(8,128)S(1)}, f32[2,9,32,256]{3,2,1,0:T(8,128)S(1)}, f32[2,9,32,256]{3,2,1,0:T(8,128)S(1)}) custom-call(s32[3]{0:T(128)S(1)} %pad_add_fusion.refs_5_.refs_0_.place, f32[1024,256]{1,0:T(8,128)S(1)} %get-tuple-element.101.refs_1_, ...), custom_call_target="tpu_custom_call" | custom-call | flops 2415919104 | bytes 5242880 | tf_op jit(solution)/shard_map/inner/pallas_call | solution.py:364
  125.4 3.5 %collective-permute-start.37 = (f32[9,32,256]{2,1,0:T(8,128)S(1)}, f32[9,32,256]{2,1,0:T(8,128)S(1)}, u32[]{:S(2)}, u32[]{:S(2)}) collective-permute-start(f32[9,32,256]{2,1,0:T(8,128)S(1)} %get-tuple-element.121), channel_id=1, source_target_pairs={{0,2},{1,3},{6,4},{7,5},{8,10},{9,11},{14,12},{15,13},{16,18},{17,... | collective-permute-start | bytes 884744 | tf_op jit(solution)/shard_map/ppermute | solution.py:571
  129.6 1.3 collective-permute-start.29
  131.6 1.3 collective-permute-start.35
  133.5 1.3 collective-permute-start.27
  134.9 1.4 collective-permute-done.37.arrived
  137.6 5.1 %collective-permute-done.29.arrived = f32[9,32,256]{2,1,0:T(8,128)S(1)} collective-permute-done((f32[9,32,256]{2,1,0:T(8,128)S(1)}, f32[9,32,256]{2,1,0:T(8,128)S(1)}, u32[]{:S(2)}, u32[]{:S(2)}) %collective-permute-start.29) | collective-permute-done | bytes 294944 | tf_op jit(solution)/shard_map/ppermute | solution.py:571
  143.9 7.2 %collective-permute-start.34 = (f32[9,32,256]{2,1,0:T(8,128)S(1)}, f32[9,32,256]{2,1,0:T(8,128)S(1)}, u32[]{:S(2)}, u32[]{:S(2)}) collective-permute-start(f32[9,32,256]{2,1,0:T(8,128)S(1)} %get-tuple-element.119), channel_id=1, source_target_pairs={{0,2},{1,3},{6,4},{7,5},{8,10},{9,11},{14,12},{15,13},{16,18},{17,... | collective-permute-start | bytes 884744 | tf_op jit(solution)/shard_map/ppermute | solution.py:571
  151.1 2.2 %collective-permute-start.26 = (f32[9,32,256]{2,1,0:T(8,128)S(1)}, f32[9,32,256]{2,1,0:T(8,128)S(1)}, u32[]{:S(2)}, u32[]{:S(2)}) collective-permute-start(f32[9,32,256]{2,1,0:T(8,128)S(1)} %get-tuple-element.110), channel_id=1, source_target_pairs={{0,2},{1,3},{6,4},{7,5},{8,10},{9,11},{14,12},{15,13},{16,18},{17,... | collective-permute-start | bytes 884744 | tf_op jit(solution)/shard_map/ppermute | solution.py:571
  153.9 1.3 collective-permute-done.27.arrived
  159.7 1.9 %collective-permute-done.34.refs_2_ = f32[9,32,256]{2,1,0:T(8,128)S(1)} collective-permute-done((f32[9,32,256]{2,1,0:T(8,128)S(1)}, f32[9,32,256]{2,1,0:T(8,128)S(1)}, u32[]{:S(2)}, u32[]{:S(2)}) %collective-permute-start.34) | collective-permute-done | bytes 294944 | tf_op jit(solution)/shard_map/ppermute | solution.py:571
  162.9 2.4 %lower.3 = f32[2,1024,256]{2,1,0:T(8,128)} custom-call(f32[1024,256]{1,0:T(8,128)S(1)} %get-tuple-element.103.adjoint, bf16[1024,256]{1,0:T(8,128)(2,1)S(1)} %get-tuple-element.68.refs_3_.refs_4_.slope, bf16[9,256,256]{2,1,0:T(8,128)(2,1)S(1)} %get-tuple-element.62.refs_2_.refs_4_.refs_5_.kernel, ...), custom_call_target="tpu_custom_call", output_to_operand_aliasing={{}: (3, {})} | custom-call | flops 1207959552 | bytes 3145728 | tf_op jit(solution)/shard_map/lower/pallas_call | solution.py:391
  165.3 5.9 %collective-permute-done.39.refs_4_ = f32[9,32,256]{2,1,0:T(8,128)S(1)} collective-permute-done((f32[9,32,256]{2,1,0:T(8,128)S(1)}, f32[9,32,256]{2,1,0:T(8,128)S(1)}, u32[]{:S(2)}, u32[]{:S(2)}) %collective-permute-start.39) | collective-permute-done | bytes 294944 | tf_op jit(solution)/shard_map/ppermute | solution.py:571
  171.2 1.3 total.2.refs_5_
  172.5 2.7 %collective-permute-done.31.refs_4_ = f32[9,32,256]{2,1,0:T(8,128)S(1)} collective-permute-done((f32[9,32,256]{2,1,0:T(8,128)S(1)}, f32[9,32,256]{2,1,0:T(8,128)S(1)}, u32[]{:S(2)}, u32[]{:S(2)}) %collective-permute-start.31) | collective-permute-done | bytes 294944 | tf_op jit(solution)/shard_map/ppermute | solution.py:571
  175.2 1.3 total.3
  (92 shorter events, 40.0 us)
Async XLA Ops:
  2.7 10.4 %collective-permute-start.12 = (f32[320,256]{1,0:T(8,128)S(1)}, f32[320,256]{1,0:T(8,128)S(1)}, u32[]{:S(2)}, u32[]{:S(2)}) collective-permute-start(f32[320,256]{1,0:T(8,128)S(1)} %section_end.5.refs_5_.refs_6_), channel_id=1, source_target_pairs={{24,16},{25,17},{26,18},{27,19},{28,20},{29,21},{30,22},{31,23}} | collective-permute-start | bytes 983048 | tf_op jit(solution)/shard_map/ppermute | solution.py:431
  6.8 7.5 %collective-permute-start.13 = (f32[256,256]{1,0:T(8,128)S(1)}, f32[256,256]{1,0:T(8,128)S(1)}, u32[]{:S(2)}, u32[]{:S(2)}) collective-permute-start(f32[256,256]{1,0:T(8,128)S(1)} %get-tuple-element.81.refs_7_.refs_6_), channel_id=1, source_target_pairs={{24,16},{25,17},{26,18},{27,19},{28,20},{29,21},{30,22},{31,23}} | collective-permute-start | bytes 786440 | tf_op jit(solution)/shard_map/ppermute | solution.py:431
  7.5 8.1 %collective-permute-start.14 = (f32[256,256]{1,0:T(8,128)S(1)}, f32[256,256]{1,0:T(8,128)S(1)}, u32[]{:S(2)}, u32[]{:S(2)}) collective-permute-start(f32[256,256]{1,0:T(8,128)S(1)} %get-tuple-element.82.refs_7_.refs_6_), channel_id=1, source_target_pairs={{24,16},{25,17},{26,18},{27,19},{28,20},{29,21},{30,22},{31,23}} | collective-permute-start | bytes 786440 | tf_op jit(solution)/shard_map/ppermute | solution.py:431
  13.1 6.3 %collective-permute-start.2 = (f32[256,256]{1,0:T(8,128)S(1)}, f32[256,256]{1,0:T(8,128)S(1)}, u32[]{:S(2)}, u32[]{:S(2)}) collective-permute-start(f32[256,256]{1,0:T(8,128)S(1)} %get-tuple-element.65.refs_7_.refs_6_), channel_id=1, source_target_pairs={{24,16},{25,17},{26,18},{27,19},{28,20},{29,21},{30,22},{31,23}} | collective-permute-start | bytes 786440 | tf_op jit(solution)/shard_map/ppermute | solution.py:431
  14.9 6.4 %collective-permute-start.17 = (f32[256,256]{1,0:T(8,128)S(1)}, f32[256,256]{1,0:T(8,128)S(1)}, u32[]{:S(2)}, u32[]{:S(2)}) collective-permute-start(f32[256,256]{1,0:T(8,128)S(1)} %get-tuple-element.88), channel_id=1, source_target_pairs={{16,8},{17,9},{18,10},{19,11},{20,12},{21,13},{22,14},{23,15}} | collective-permute-start | bytes 786440 | tf_op jit(solution)/shard_map/ppermute | solution.py:431
  16.2 6.4 %collective-permute-start.18 = (f32[256,256]{1,0:T(8,128)S(1)}, f32[256,256]{1,0:T(8,128)S(1)}, u32[]{:S(2)}, u32[]{:S(2)}) collective-permute-start(f32[256,256]{1,0:T(8,128)S(1)} %get-tuple-element.90), channel_id=1, source_target_pairs={{16,8},{17,9},{18,10},{19,11},{20,12},{21,13},{22,14},{23,15}} | collective-permute-start | bytes 786440 | tf_op jit(solution)/shard_map/ppermute | solution.py:431
  16.9 6.4 %collective-permute-start.16 = (f32[288,256]{1,0:T(8,128)S(1)}, f32[288,256]{1,0:T(8,128)S(1)}, u32[]{:S(2)}, u32[]{:S(2)}) collective-permute-start(f32[288,256]{1,0:T(8,128)S(1)} %get-tuple-element.86), channel_id=1, source_target_pairs={{16,8},{17,9},{18,10},{19,11},{20,12},{21,13},{22,14},{23,15}} | collective-permute-start | bytes 884744 | tf_op jit(solution)/shard_map/ppermute | solution.py:431
  19.4 12.6 %collective-permute-start.4 = (f32[288,256]{1,0:T(8,128)S(1)}, f32[288,256]{1,0:T(8,128)S(1)}, u32[]{:S(2)}, u32[]{:S(2)}) collective-permute-start(f32[288,256]{1,0:T(8,128)S(1)} %get-tuple-element.69), channel_id=1, source_target_pairs={{16,8},{17,9},{18,10},{19,11},{20,12},{21,13},{22,14},{23,15}} | collective-permute-start | bytes 884744 | tf_op jit(solution)/shard_map/ppermute | solution.py:431
  20.6 8.2 %collective-permute-start.5 = (f32[256,256]{1,0:T(8,128)S(1)}, f32[256,256]{1,0:T(8,128)S(1)}, u32[]{:S(2)}, u32[]{:S(2)}) collective-permute-start(f32[256,256]{1,0:T(8,128)S(1)} %get-tuple-element.71), channel_id=1, source_target_pairs={{16,8},{17,9},{18,10},{19,11},{20,12},{21,13},{22,14},{23,15}} | collective-permute-start | bytes 786440 | tf_op jit(solution)/shard_map/ppermute | solution.py:431
  21.3 8.8 %collective-permute-start.6 = (f32[256,256]{1,0:T(8,128)S(1)}, f32[256,256]{1,0:T(8,128)S(1)}, u32[]{:S(2)}, u32[]{:S(2)}) collective-permute-start(f32[256,256]{1,0:T(8,128)S(1)} %get-tuple-element.73), channel_id=1, source_target_pairs={{16,8},{17,9},{18,10},{19,11},{20,12},{21,13},{22,14},{23,15}} | collective-permute-start | bytes 786440 | tf_op jit(solution)/shard_map/ppermute | solution.py:431
  25.6 55.1 %collective-permute-start.22 = (f32[256,256]{1,0:T(8,128)S(1)}, f32[256,256]{1,0:T(8,128)S(1)}, u32[]{:S(2)}, u32[]{:S(2)}) collective-permute-start(f32[256,256]{1,0:T(8,128)S(1)} %get-tuple-element.96), channel_id=1, source_target_pairs={{8,0},{9,1},{10,2},{11,3},{12,4},{13,5},{14,6},{15,7}} | collective-permute-start | bytes 786440 | tf_op jit(solution)/shard_map/ppermute | solution.py:431
  27.5 58.8 %collective-permute-start.23 = (f32[256,256]{1,0:T(8,128)S(1)}, f32[256,256]{1,0:T(8,128)S(1)}, u32[]{:S(2)}, u32[]{:S(2)}) collective-permute-start(f32[256,256]{1,0:T(8,128)S(1)} %stage.31), channel_id=1, source_target_pairs={{8,0},{9,1},{10,2},{11,3},{12,4},{13,5},{14,6},{15,7}} | collective-permute-start | bytes 786440 | tf_op jit(solution)/shard_map/ppermute | solution.py:431
  28.8 63.1 %collective-permute-start.21 = (f32[256,256]{1,0:T(8,128)S(1)}, f32[256,256]{1,0:T(8,128)S(1)}, u32[]{:S(2)}, u32[]{:S(2)}) collective-permute-start(f32[256,256]{1,0:T(8,128)S(1)} %get-tuple-element.94), channel_id=1, source_target_pairs={{8,0},{9,1},{10,2},{11,3},{12,4},{13,5},{14,6},{15,7}} | collective-permute-start | bytes 786440 | tf_op jit(solution)/shard_map/ppermute | solution.py:431
  30.1 67.4 %collective-permute-start.20 = (f32[256,256]{1,0:T(8,128)S(1)}, f32[256,256]{1,0:T(8,128)S(1)}, u32[]{:S(2)}, u32[]{:S(2)}) collective-permute-start(f32[256,256]{1,0:T(8,128)S(1)} %get-tuple-element.92), channel_id=1, source_target_pairs={{8,0},{9,1},{10,2},{11,3},{12,4},{13,5},{14,6},{15,7}} | collective-permute-start | bytes 786440 | tf_op jit(solution)/shard_map/ppermute | solution.py:431
  34.4 71.5 %collective-permute-start.10 = (f32[256,256]{1,0:T(8,128)S(1)}, f32[256,256]{1,0:T(8,128)S(1)}, u32[]{:S(2)}, u32[]{:S(2)}) collective-permute-start(f32[256,256]{1,0:T(8,128)S(1)} %get-tuple-element.79), channel_id=1, source_target_pairs={{8,0},{9,1},{10,2},{11,3},{12,4},{13,5},{14,6},{15,7}} | collective-permute-start | bytes 786440 | tf_op jit(solution)/shard_map/ppermute | solution.py:431
  80.7 28.1 %collective-permute-start.11 = (f32[256,256]{1,0:T(8,128)S(1)}, f32[256,256]{1,0:T(8,128)S(1)}, u32[]{:S(2)}, u32[]{:S(2)}) collective-permute-start(f32[256,256]{1,0:T(8,128)S(1)} %stage.23), channel_id=1, source_target_pairs={{8,0},{9,1},{10,2},{11,3},{12,4},{13,5},{14,6},{15,7}} | collective-permute-start | bytes 786440 | tf_op jit(solution)/shard_map/ppermute | solution.py:431
  86.3 28.1 %collective-permute-start.9 = (f32[256,256]{1,0:T(8,128)S(1)}, f32[256,256]{1,0:T(8,128)S(1)}, u32[]{:S(2)}, u32[]{:S(2)}) collective-permute-start(f32[256,256]{1,0:T(8,128)S(1)} %get-tuple-element.77), channel_id=1, source_target_pairs={{8,0},{9,1},{10,2},{11,3},{12,4},{13,5},{14,6},{15,7}} | collective-permute-start | bytes 786440 | tf_op jit(solution)/shard_map/ppermute | solution.py:431
  91.9 25.7 %collective-permute-start.8 = (f32[256,256]{1,0:T(8,128)S(1)}, f32[256,256]{1,0:T(8,128)S(1)}, u32[]{:S(2)}, u32[]{:S(2)}) collective-permute-start(f32[256,256]{1,0:T(8,128)S(1)} %get-tuple-element.75), channel_id=1, source_target_pairs={{8,0},{9,1},{10,2},{11,3},{12,4},{13,5},{14,6},{15,7}} | collective-permute-start | bytes 786440 | tf_op jit(solution)/shard_map/ppermute | solution.py:431
  124.3 6.6 %collective-permute-start.33 = (f32[2,9,32,256]{3,2,1,0:T(8,128)S(1)}, f32[2,9,32,256]{3,2,1,0:T(8,128)S(1)}, u32[]{:S(2)}, u32[]{:S(2)}) collective-permute-start(f32[2,9,32,256]{3,2,1,0:T(8,128)S(1)} %get-tuple-element.117), channel_id=1, source_target_pairs={{0,1},{1,0},{2,3},{3,2},{4,5},{5,4},{6,7},{7,6},{8,9},{9,8},{10,11... | collective-permute-start | bytes 1769480 | tf_op jit(solution)/shard_map/ppermute | solution.py:556
  124.4 8.5 %collective-permute-start.25 = (f32[2,9,32,256]{3,2,1,0:T(8,128)S(1)}, f32[2,9,32,256]{3,2,1,0:T(8,128)S(1)}, u32[]{:S(2)}, u32[]{:S(2)}) collective-permute-start(f32[2,9,32,256]{3,2,1,0:T(8,128)S(1)} %get-tuple-element.108), channel_id=1, source_target_pairs={{0,1},{1,0},{2,3},{3,2},{4,5},{5,4},{6,7},{7,6},{8,9},{9,8},{10,11... | collective-permute-start | bytes 1769480 | tf_op jit(solution)/shard_map/ppermute | solution.py:556
  125.4 10.9 %collective-permute-start.37 = (f32[9,32,256]{2,1,0:T(8,128)S(1)}, f32[9,32,256]{2,1,0:T(8,128)S(1)}, u32[]{:S(2)}, u32[]{:S(2)}) collective-permute-start(f32[9,32,256]{2,1,0:T(8,128)S(1)} %get-tuple-element.121), channel_id=1, source_target_pairs={{0,2},{1,3},{6,4},{7,5},{8,10},{9,11},{14,12},{15,13},{16,18},{17,... | collective-permute-start | bytes 884744 | tf_op jit(solution)/shard_map/ppermute | solution.py:571
  129.6 13.0 %collective-permute-start.29 = (f32[9,32,256]{2,1,0:T(8,128)S(1)}, f32[9,32,256]{2,1,0:T(8,128)S(1)}, u32[]{:S(2)}, u32[]{:S(2)}) collective-permute-start(f32[9,32,256]{2,1,0:T(8,128)S(1)} %get-tuple-element.112), channel_id=1, source_target_pairs={{0,2},{1,3},{6,4},{7,5},{8,10},{9,11},{14,12},{15,13},{16,18},{17,... | collective-permute-start | bytes 884744 | tf_op jit(solution)/shard_map/ppermute | solution.py:571
  131.6 19.5 %collective-permute-start.35 = (f32[9,32,256]{2,1,0:T(8,128)S(1)}, f32[9,32,256]{2,1,0:T(8,128)S(1)}, u32[]{:S(2)}, u32[]{:S(2)}) collective-permute-start(f32[9,32,256]{2,1,0:T(8,128)S(1)} %get-tuple-element.120), channel_id=1, source_target_pairs={{0,2},{1,3},{6,4},{7,5},{8,10},{9,11},{14,12},{15,13},{16,18},{17,... | collective-permute-start | bytes 884744 | tf_op jit(solution)/shard_map/ppermute | solution.py:571
  133.5 21.7 %collective-permute-start.27 = (f32[9,32,256]{2,1,0:T(8,128)S(1)}, f32[9,32,256]{2,1,0:T(8,128)S(1)}, u32[]{:S(2)}, u32[]{:S(2)}) collective-permute-start(f32[9,32,256]{2,1,0:T(8,128)S(1)} %get-tuple-element.111), channel_id=1, source_target_pairs={{0,2},{1,3},{6,4},{7,5},{8,10},{9,11},{14,12},{15,13},{16,18},{17,... | collective-permute-start | bytes 884744 | tf_op jit(solution)/shard_map/ppermute | solution.py:571
  136.9 19.6 %collective-permute-start.38 = (f32[9,32,256]{2,1,0:T(8,128)S(1)}, f32[9,32,256]{2,1,0:T(8,128)S(1)}, u32[]{:S(2)}, u32[]{:S(2)}) collective-permute-start(f32[9,32,256]{2,1,0:T(8,128)S(1)} %relay.10), channel_id=1, source_target_pairs={{2,4},{3,5},{4,2},{5,3},{10,12},{11,13},{12,10},{13,11},{18,20},{1... | collective-permute-start | bytes 884744 | tf_op jit(solution)/shard_map/ppermute | solution.py:571
  143.2 15.2 %collective-permute-start.30 = (f32[9,32,256]{2,1,0:T(8,128)S(1)}, f32[9,32,256]{2,1,0:T(8,128)S(1)}, u32[]{:S(2)}, u32[]{:S(2)}) collective-permute-start(f32[9,32,256]{2,1,0:T(8,128)S(1)} %relay.7), channel_id=1, source_target_pairs={{2,4},{3,5},{4,2},{5,3},{10,12},{11,13},{12,10},{13,11},{18,20},{1... | collective-permute-start | bytes 884744 | tf_op jit(solution)/shard_map/ppermute | solution.py:571
  143.9 17.7 %collective-permute-start.34 = (f32[9,32,256]{2,1,0:T(8,128)S(1)}, f32[9,32,256]{2,1,0:T(8,128)S(1)}, u32[]{:S(2)}, u32[]{:S(2)}) collective-permute-start(f32[9,32,256]{2,1,0:T(8,128)S(1)} %get-tuple-element.119), channel_id=1, source_target_pairs={{0,2},{1,3},{6,4},{7,5},{8,10},{9,11},{14,12},{15,13},{16,18},{17,... | collective-permute-start | bytes 884744 | tf_op jit(solution)/shard_map/ppermute | solution.py:571
  151.1 21.4 %collective-permute-start.26 = (f32[9,32,256]{2,1,0:T(8,128)S(1)}, f32[9,32,256]{2,1,0:T(8,128)S(1)}, u32[]{:S(2)}, u32[]{:S(2)}) collective-permute-start(f32[9,32,256]{2,1,0:T(8,128)S(1)} %get-tuple-element.110), channel_id=1, source_target_pairs={{0,2},{1,3},{6,4},{7,5},{8,10},{9,11},{14,12},{15,13},{16,18},{17,... | collective-permute-start | bytes 884744 | tf_op jit(solution)/shard_map/ppermute | solution.py:571
  155.3 10.1 %collective-permute-start.36 = (f32[9,32,256]{2,1,0:T(8,128)S(1)}, f32[9,32,256]{2,1,0:T(8,128)S(1)}, u32[]{:S(2)}, u32[]{:S(2)}) collective-permute-start(f32[9,32,256]{2,1,0:T(8,128)S(1)} %relay.9), channel_id=1, source_target_pairs={{2,4},{3,5},{4,2},{5,3},{10,12},{11,13},{12,10},{13,11},{18,20},{1... | collective-permute-start | bytes 884744 | tf_op jit(solution)/shard_map/ppermute | solution.py:571
  157.1 14.1 %collective-permute-start.39 = (f32[9,32,256]{2,1,0:T(8,128)S(1)}, f32[9,32,256]{2,1,0:T(8,128)S(1)}, u32[]{:S(2)}, u32[]{:S(2)}) collective-permute-start(f32[9,32,256]{2,1,0:T(8,128)S(1)} %relay.11), channel_id=1, source_target_pairs={{4,6},{5,7},{2,0},{3,1},{12,14},{13,15},{10,8},{11,9},{20,22},{21,... | collective-permute-start | bytes 884744 | tf_op jit(solution)/shard_map/ppermute | solution.py:571
  158.4 14.1 %collective-permute-start.28 = (f32[9,32,256]{2,1,0:T(8,128)S(1)}, f32[9,32,256]{2,1,0:T(8,128)S(1)}, u32[]{:S(2)}, u32[]{:S(2)}) collective-permute-start(f32[9,32,256]{2,1,0:T(8,128)S(1)} %relay.6), channel_id=1, source_target_pairs={{2,4},{3,5},{4,2},{5,3},{10,12},{11,13},{12,10},{13,11},{18,20},{1... | collective-permute-start | bytes 884744 | tf_op jit(solution)/shard_map/ppermute | solution.py:571
  161.6 13.6 %collective-permute-start.31 = (f32[9,32,256]{2,1,0:T(8,128)S(1)}, f32[9,32,256]{2,1,0:T(8,128)S(1)}, u32[]{:S(2)}, u32[]{:S(2)}) collective-permute-start(f32[9,32,256]{2,1,0:T(8,128)S(1)} %relay.8), channel_id=1, source_target_pairs={{4,6},{5,7},{2,0},{3,1},{12,14},{13,15},{10,8},{11,9},{20,22},{21,... | collective-permute-start | bytes 884744 | tf_op jit(solution)/shard_map/ppermute | solution.py:571
  (11 other events, 162.4 us)

commit v4 on v3

--- a/solution.py
+++ b/solution.py
@@ -408,11 +408,8 @@
 
 
 def cuts_of(height, hops):
-    piece = height // PIECES
-    return [
-        [0] + [min(height, piece * (k + 1) + hops - 1 - hop) for k in range(PIECES - 1)] + [height]
-        for hop in range(hops)
-    ]
+    ends = [height * k // PIECES - 1 for k in range(1, PIECES)]
+    return [[0] + [min(height, e + hops - 1 - hop) for e in ends] + [height] for hop in range(hops)]
 
 
 def chain(place, ends, cuts, guess, slope, kernel, factor, width):

time: 177 us -> 170 us (0.960)
  waiting for transfers between devices: 87.4 us -> 79.7 us
    ppermute x24, waiting for transfers between devices: 69.1 us -> 61.4 us  [chain(): arrived = lax.ppermute(rows, 'layer', pairs)]
  transfers between devices with their start and end apart: 40 -> 40, of which waited for: 13 -> 9; matrix products, arithmetic and copies ran while one was open for 0% -> 0% of each run, Pallas kernels for 21% -> 22%
where the time goes in v4:
time: 170 us; the launch traced here: 169 us
  waiting for transfers between devices  79.7 us (47%)
  starting transfers between devices  44.6 us (26%)
  Pallas kernels  43 us (25%)
    ppermute x24, waiting for transfers between devices, chain(): arrived = lax.ppermute(rows, 'layer', pairs)  61.4 us
    ppermute x12, starting transfers between devices, line_sum(): arrived[wave, item] = lax.ppermute(out, 'dp', pairs)  22.1 us
    ppermute x24, starting transfers between devices, chain(): arrived = lax.ppermute(rows, 'layer', pairs)  21.3 us
    ppermute x12, waiting for transfers between devices, line_sum(): arrived[wave, item] = lax.ppermute(out, 'dp', pairs)  18.3 us
    pallas_call x16, Pallas kernels, stage(): pl.pallas_call(functools.partial(stage_kernel, width, factor, first, low,...  8.81 us
    pallas_call x3, Pallas kernels, section_end_of(): pl.pallas_call(functools.partial(end_kernel, width, first, low, shapes, l...  8.79 us
    pallas_call x2, Pallas kernels, inner_of(): pl.pallas_call(functools.partial(inner_kernel, width, final, scale, share...  7.16 us
    pallas_call x2, Pallas kernels, lower_of(): pl.pallas_call(functools.partial(lower_kernel, width), out_shape=jax.Shap...  4.89 us
  transfers between devices with their start and end apart: 40, of which 9 were waited for; matrix products, arithmetic and copies ran while one was open for 0% of the time, Pallas kernels for 22%

profile of v4, /device:TPU:0, one launch (start us, length us, event | category | flops | bytes accessed | tf_op | source)
XLA Modules:
  0.0 168.8 jit_solution(2983879608868772406)
XLA Ops:
  0.6 2.0 %section_end.5.refs_5_.refs_6_ = f32[288,256]{1,0:T(8,128)S(1)} custom-call(f32[2,2,1024,256]{3,2,1,0:T(8,128)} %bitcast.22, bf16[2,2,1024,256]{3,2,1,0:T(8,128)(2,1)} %bitcast.7, bf16[2,9,256,256]{3,2,1,0:T(8,128)(2,1)} %refs_5_.3), custom_call_target="tpu_custom_call" | custom-call | flops 339738624 | bytes 884736 | tf_op jit(solution)/shard_map/section_end/pallas_call | solution.py:136
  3.4 3.3 %section_end.3 = (f32[256,256]{1,0:T(8,128)S(1)}, f32[256,256]{1,0:T(8,128)S(1)}, f32[224,256]{1,0:T(8,128)S(1)}, f32[1024,256]{1,0:T(8,128)S(1)}, bf16[1024,256...) custom-call(f32[2,2,1024,256]{3,2,1,0:T(8,128)} %bitcast.23, bf16[2,2,1024,256]{3,2,1,0:T(8,128)(2,1)} %bitcast.8, ...), custom_call_target="tpu_custom_call" | custom-call | flops 868220928 | bytes 2260992 | tf_op jit(solution)/shard_map/section_end/pallas_call | solution.py:136
  8.1 3.4 %section_end.4 = (f32[288,256]{1,0:T(8,128)S(1)}, f32[256,256]{1,0:T(8,128)S(1)}, f32[256,256]{1,0:T(8,128)S(1)}, f32[224,256]{1,0:T(8,128)S(1)}, f32[1024,256]{...) custom-call(f32[2,2,1024,256]{3,2,1,0:T(8,128)} %bitcast.25, bf16[2,2,1024,256]{3,2,1,0:T(8,128)(2,1)} %bitcast.10, ...), custom_call_target="tpu_custom_call" | custom-call | flops 1207959552 | bytes 3145728 | tf_op jit(solution)/shard_map/section_end/pallas_call | solution.py:136
  26.1 1.3 collective-permute-start.23
  28.6 1.3 collective-permute-start.22
  30.0 1.3 collective-permute-start.21
  31.3 1.3 collective-permute-start.20
  34.3 1.4 collective-permute-start.8
  36.3 54.2 %collective-permute-done.20.refs_9_ = f32[224,256]{1,0:T(8,128)S(1)} collective-permute-done((f32[224,256]{1,0:T(8,128)S(1)}, f32[224,256]{1,0:T(8,128)S(1)}, u32[]{:S(2)}, u32[]{:S(2)}) %collective-permute-start.20) | collective-permute-done | bytes 229408 | tf_op jit(solution)/shard_map/ppermute | solution.py:428
  91.8 1.3 collective-permute-start.9
  94.4 2.4 %top.2 = (f32[1024,256]{1,0:T(8,128)S(1)}, f32[9,256,256]{2,1,0:T(8,128)S(1)}) custom-call(s32[3]{0:T(128)S(1)} %pad_add_fusion.refs_5_.refs_0_.place, f32[288,256]{1,0:T(8,128)S(1)} %collective-permute-done.12.refs_1_, f32[256,256]{1,0:T(8,128)S(1)} %collective-permute-done.13.refs_2_, f32[256,256]{1,0:T(8,128)S(1)} %collective-permute-done.14.refs_2_.refs_3_, ...), custom_call_target="tpu_custom_call" | custom-call | flops 1207959552 | bytes 5242880 | tf_op jit(solution)/shard_map/top/pallas_call | solution.py:307
  96.8 3.5 %inner.2 = (f32[1024,256]{1,0:T(8,128)S(1)}, f32[9,256,256]{2,1,0:T(8,128)S(1)}) custom-call(s32[3]{0:T(128)S(1)} %pad_add_fusion.refs_5_.refs_0_.place, f32[1024,256]{1,0:T(8,128)S(1)} %get-tuple-element.99.refs_1_, bf16[2,2,1024,256]{3,2,1,0:T(8,128)(2,1)S(1)} %bitcast.13, bf16[2,2,1024,256]{3,2,1,0:T(8,128)(2,1)S(1)} %bitcast.14, ...), custom_call_target="tpu_custom_call" | custom-call | flops 2415919104 | bytes 5242880 | tf_op jit(solution)/shard_map/inner/pallas_call | solution.py:364
  100.3 2.4 %lower.2.refs_17_.refs_0_ = f32[2,1024,256]{2,1,0:T(8,128)} custom-call(f32[1024,256]{1,0:T(8,128)S(1)} %get-tuple-element.100.adjoint, bf16[1024,256]{1,0:T(8,128)(2,1)S(1)} %get-tuple-element.85.refs_3_.refs_4_.slope, bf16[9,256,256]{2,1,0:T(8,128)(2,1)S(1)} %get-tuple-element.62.refs_2_.refs_4_.refs_5_.kernel), custom_call_target="tpu_custom_call" | custom-call | flops 1207959552 | bytes 3145728 | tf_op jit(solution)/shard_map/lower/pallas_call | solution.py:391
  102.7 4.0 %collective-permute-done.9.refs_10_ = f32[256,256]{1,0:T(8,128)S(1)} collective-permute-done((f32[256,256]{1,0:T(8,128)S(1)}, f32[256,256]{1,0:T(8,128)S(1)}, u32[]{:S(2)}, u32[]{:S(2)}) %collective-permute-start.9) | collective-permute-done | bytes 262176 | tf_op jit(solution)/shard_map/ppermute | solution.py:428
  106.7 3.2 %collective-permute-done.11.refs_12_ = f32[288,256]{1,0:T(8,128)S(1)} collective-permute-done((f32[288,256]{1,0:T(8,128)S(1)}, f32[288,256]{1,0:T(8,128)S(1)}, u32[]{:S(2)}, u32[]{:S(2)}) %collective-permute-start.11) | collective-permute-done | bytes 294944 | tf_op jit(solution)/shard_map/ppermute | solution.py:428
  109.9 2.4 %top.3 = (f32[1024,256]{1,0:T(8,128)S(1)}, f32[2,9,32,256]{3,2,1,0:T(8,128)S(1)}, f32[2,9,32,256]{3,2,1,0:T(8,128)S(1)}, f32[2,9,32,256]{3,2,1,0:T(8,128)S(1)}, f32[2,9,32,256]{3,2,1,0:T(8,128)S(1)}) custom-call(s32[3]{0:T(128)S(1)} %pad_add_fusion.refs_5_.refs_0_.place, f32[288,256]{1,0:T(8,128)S(1)} %collective-permute-done.refs_1_, ...), custom_call_target="tpu_custom_call" | custom-call | flops 1207959552 | bytes 5242880 | tf_op jit(solution)/shard_map/top/pallas_call | solution.py:307
  112.3 3.7 %inner.3 = (f32[1024,256]{1,0:T(8,128)S(1)}, f32[2,9,32,256]{3,2,1,0:T(8,128)S(1)}, f32[2,9,32,256]{3,2,1,0:T(8,128)S(1)}, f32[2,9,32,256]{3,2,1,0:T(8,128)S(1)}, f32[2,9,32,256]{3,2,1,0:T(8,128)S(1)}) custom-call(s32[3]{0:T(128)S(1)} %pad_add_fusion.refs_5_.refs_0_.place, f32[1024,256]{1,0:T(8,128)S(1)} %get-tuple-element.101.refs_1_, ...), custom_call_target="tpu_custom_call" | custom-call | flops 2415919104 | bytes 5242880 | tf_op jit(solution)/shard_map/inner/pallas_call | solution.py:364
  117.7 3.5 %collective-permute-start.37 = (f32[9,32,256]{2,1,0:T(8,128)S(1)}, f32[9,32,256]{2,1,0:T(8,128)S(1)}, u32[]{:S(2)}, u32[]{:S(2)}) collective-permute-start(f32[9,32,256]{2,1,0:T(8,128)S(1)} %get-tuple-element.121), channel_id=1, source_target_pairs={{0,2},{1,3},{6,4},{7,5},{8,10},{9,11},{14,12},{15,13},{16,18},{17,... | collective-permute-start | bytes 884744 | tf_op jit(solution)/shard_map/ppermute | solution.py:568
  121.8 1.3 collective-permute-start.29
  123.8 1.3 collective-permute-start.35
  125.8 1.3 collective-permute-start.27
  127.1 1.5 collective-permute-done.37.arrived
  129.8 5.1 %collective-permute-done.29.arrived = f32[9,32,256]{2,1,0:T(8,128)S(1)} collective-permute-done((f32[9,32,256]{2,1,0:T(8,128)S(1)}, f32[9,32,256]{2,1,0:T(8,128)S(1)}, u32[]{:S(2)}, u32[]{:S(2)}) %collective-permute-start.29) | collective-permute-done | bytes 294944 | tf_op jit(solution)/shard_map/ppermute | solution.py:568
  136.1 7.2 %collective-permute-start.34 = (f32[9,32,256]{2,1,0:T(8,128)S(1)}, f32[9,32,256]{2,1,0:T(8,128)S(1)}, u32[]{:S(2)}, u32[]{:S(2)}) collective-permute-start(f32[9,32,256]{2,1,0:T(8,128)S(1)} %get-tuple-element.119), channel_id=1, source_target_pairs={{0,2},{1,3},{6,4},{7,5},{8,10},{9,11},{14,12},{15,13},{16,18},{17,... | collective-permute-start | bytes 884744 | tf_op jit(solution)/shard_map/ppermute | solution.py:568
  143.4 2.2 %collective-permute-start.26 = (f32[9,32,256]{2,1,0:T(8,128)S(1)}, f32[9,32,256]{2,1,0:T(8,128)S(1)}, u32[]{:S(2)}, u32[]{:S(2)}) collective-permute-start(f32[9,32,256]{2,1,0:T(8,128)S(1)} %get-tuple-element.110), channel_id=1, source_target_pairs={{0,2},{1,3},{6,4},{7,5},{8,10},{9,11},{14,12},{15,13},{16,18},{17,... | collective-permute-start | bytes 884744 | tf_op jit(solution)/shard_map/ppermute | solution.py:568
  146.2 1.3 collective-permute-done.27.arrived
  152.0 1.9 %collective-permute-done.34.refs_2_ = f32[9,32,256]{2,1,0:T(8,128)S(1)} collective-permute-done((f32[9,32,256]{2,1,0:T(8,128)S(1)}, f32[9,32,256]{2,1,0:T(8,128)S(1)}, u32[]{:S(2)}, u32[]{:S(2)}) %collective-permute-start.34) | collective-permute-done | bytes 294944 | tf_op jit(solution)/shard_map/ppermute | solution.py:568
  155.1 2.4 %lower.3 = f32[2,1024,256]{2,1,0:T(8,128)} custom-call(f32[1024,256]{1,0:T(8,128)S(1)} %get-tuple-element.103.adjoint, bf16[1024,256]{1,0:T(8,128)(2,1)S(1)} %get-tuple-element.68.refs_3_.refs_4_.slope, bf16[9,256,256]{2,1,0:T(8,128)(2,1)S(1)} %get-tuple-element.62.refs_2_.refs_4_.refs_5_.kernel, ...), custom_call_target="tpu_custom_call", output_to_operand_aliasing={{}: (3, {})} | custom-call | flops 1207959552 | bytes 3145728 | tf_op jit(solution)/shard_map/lower/pallas_call | solution.py:391
  157.6 5.9 %collective-permute-done.39.refs_4_ = f32[9,32,256]{2,1,0:T(8,128)S(1)} collective-permute-done((f32[9,32,256]{2,1,0:T(8,128)S(1)}, f32[9,32,256]{2,1,0:T(8,128)S(1)}, u32[]{:S(2)}, u32[]{:S(2)}) %collective-permute-start.39) | collective-permute-done | bytes 294944 | tf_op jit(solution)/shard_map/ppermute | solution.py:568
  163.5 1.3 total.2.refs_5_
  164.8 2.7 %collective-permute-done.31.refs_4_ = f32[9,32,256]{2,1,0:T(8,128)S(1)} collective-permute-done((f32[9,32,256]{2,1,0:T(8,128)S(1)}, f32[9,32,256]{2,1,0:T(8,128)S(1)}, u32[]{:S(2)}, u32[]{:S(2)}) %collective-permute-start.31) | collective-permute-done | bytes 294944 | tf_op jit(solution)/shard_map/ppermute | solution.py:568
  167.5 1.3 total.3
  (92 shorter events, 34.8 us)
Async XLA Ops:
  2.7 10.3 %collective-permute-start.12 = (f32[288,256]{1,0:T(8,128)S(1)}, f32[288,256]{1,0:T(8,128)S(1)}, u32[]{:S(2)}, u32[]{:S(2)}) collective-permute-start(f32[288,256]{1,0:T(8,128)S(1)} %section_end.5.refs_5_.refs_6_), channel_id=1, source_target_pairs={{24,16},{25,17},{26,18},{27,19},{28,20},{29,21},{30,22},{31,23}} | collective-permute-start | bytes 884744 | tf_op jit(solution)/shard_map/ppermute | solution.py:428
  6.8 7.5 %collective-permute-start.13 = (f32[256,256]{1,0:T(8,128)S(1)}, f32[256,256]{1,0:T(8,128)S(1)}, u32[]{:S(2)}, u32[]{:S(2)}) collective-permute-start(f32[256,256]{1,0:T(8,128)S(1)} %get-tuple-element.81.refs_7_.refs_6_), channel_id=1, source_target_pairs={{24,16},{25,17},{26,18},{27,19},{28,20},{29,21},{30,22},{31,23}} | collective-permute-start | bytes 786440 | tf_op jit(solution)/shard_map/ppermute | solution.py:428
  7.5 8.7 %collective-permute-start.14 = (f32[256,256]{1,0:T(8,128)S(1)}, f32[256,256]{1,0:T(8,128)S(1)}, u32[]{:S(2)}, u32[]{:S(2)}) collective-permute-start(f32[256,256]{1,0:T(8,128)S(1)} %get-tuple-element.82.refs_7_.refs_6_), channel_id=1, source_target_pairs={{24,16},{25,17},{26,18},{27,19},{28,20},{29,21},{30,22},{31,23}} | collective-permute-start | bytes 786440 | tf_op jit(solution)/shard_map/ppermute | solution.py:428
  11.6 5.8 %collective-permute-start.1 = (f32[256,256]{1,0:T(8,128)S(1)}, f32[256,256]{1,0:T(8,128)S(1)}, u32[]{:S(2)}, u32[]{:S(2)}) collective-permute-start(f32[256,256]{1,0:T(8,128)S(1)} %get-tuple-element.64.refs_7_.refs_6_), channel_id=1, source_target_pairs={{24,16},{25,17},{26,18},{27,19},{28,20},{29,21},{30,22},{31,23}} | collective-permute-start | bytes 786440 | tf_op jit(solution)/shard_map/ppermute | solution.py:428
  18.7 6.8 %collective-permute-start.19 = (f32[256,256]{1,0:T(8,128)S(1)}, f32[256,256]{1,0:T(8,128)S(1)}, u32[]{:S(2)}, u32[]{:S(2)}) collective-permute-start(f32[256,256]{1,0:T(8,128)S(1)} %stage.27), channel_id=1, source_target_pairs={{16,8},{17,9},{18,10},{19,11},{20,12},{21,13},{22,14},{23,15}} | collective-permute-start | bytes 786440 | tf_op jit(solution)/shard_map/ppermute | solution.py:428
  19.9 7.4 %collective-permute-start.3 = (f32[224,256]{1,0:T(8,128)S(1)}, f32[224,256]{1,0:T(8,128)S(1)}, u32[]{:S(2)}, u32[]{:S(2)}) collective-permute-start(f32[224,256]{1,0:T(8,128)S(1)} %get-tuple-element.66.refs_7_), channel_id=1, source_target_pairs={{24,16},{25,17},{26,18},{27,19},{28,20},{29,21},{30,22},{31,23}} | collective-permute-start | bytes 688136 | tf_op jit(solution)/shard_map/ppermute | solution.py:428
  21.2 7.4 %collective-permute-start.4 = (f32[256,256]{1,0:T(8,128)S(1)}, f32[256,256]{1,0:T(8,128)S(1)}, u32[]{:S(2)}, u32[]{:S(2)}) collective-permute-start(f32[256,256]{1,0:T(8,128)S(1)} %get-tuple-element.69), channel_id=1, source_target_pairs={{16,8},{17,9},{18,10},{19,11},{20,12},{21,13},{22,14},{23,15}} | collective-permute-start | bytes 786440 | tf_op jit(solution)/shard_map/ppermute | solution.py:428
  21.9 8.1 %collective-permute-start.5 = (f32[256,256]{1,0:T(8,128)S(1)}, f32[256,256]{1,0:T(8,128)S(1)}, u32[]{:S(2)}, u32[]{:S(2)}) collective-permute-start(f32[256,256]{1,0:T(8,128)S(1)} %get-tuple-element.71), channel_id=1, source_target_pairs={{16,8},{17,9},{18,10},{19,11},{20,12},{21,13},{22,14},{23,15}} | collective-permute-start | bytes 786440 | tf_op jit(solution)/shard_map/ppermute | solution.py:428
  23.2 8.1 %collective-permute-start.6 = (f32[256,256]{1,0:T(8,128)S(1)}, f32[256,256]{1,0:T(8,128)S(1)}, u32[]{:S(2)}, u32[]{:S(2)}) collective-permute-start(f32[256,256]{1,0:T(8,128)S(1)} %get-tuple-element.73), channel_id=1, source_target_pairs={{16,8},{17,9},{18,10},{19,11},{20,12},{21,13},{22,14},{23,15}} | collective-permute-start | bytes 786440 | tf_op jit(solution)/shard_map/ppermute | solution.py:428
  26.1 68.3 %collective-permute-start.23 = (f32[288,256]{1,0:T(8,128)S(1)}, f32[288,256]{1,0:T(8,128)S(1)}, u32[]{:S(2)}, u32[]{:S(2)}) collective-permute-start(f32[288,256]{1,0:T(8,128)S(1)} %stage.31), channel_id=1, source_target_pairs={{8,0},{9,1},{10,2},{11,3},{12,4},{13,5},{14,6},{15,7}} | collective-permute-start | bytes 884744 | tf_op jit(solution)/shard_map/ppermute | solution.py:428
  28.0 6.3 %collective-permute-start.7 = (f32[256,256]{1,0:T(8,128)S(1)}, f32[256,256]{1,0:T(8,128)S(1)}, u32[]{:S(2)}, u32[]{:S(2)}) collective-permute-start(f32[256,256]{1,0:T(8,128)S(1)} %stage.19), channel_id=1, source_target_pairs={{16,8},{17,9},{18,10},{19,11},{20,12},{21,13},{22,14},{23,15}} | collective-permute-start | bytes 786440 | tf_op jit(solution)/shard_map/ppermute | solution.py:428
  28.6 63.1 %collective-permute-start.22 = (f32[256,256]{1,0:T(8,128)S(1)}, f32[256,256]{1,0:T(8,128)S(1)}, u32[]{:S(2)}, u32[]{:S(2)}) collective-permute-start(f32[256,256]{1,0:T(8,128)S(1)} %get-tuple-element.96), channel_id=1, source_target_pairs={{8,0},{9,1},{10,2},{11,3},{12,4},{13,5},{14,6},{15,7}} | collective-permute-start | bytes 786440 | tf_op jit(solution)/shard_map/ppermute | solution.py:428
  30.0 63.1 %collective-permute-start.21 = (f32[256,256]{1,0:T(8,128)S(1)}, f32[256,256]{1,0:T(8,128)S(1)}, u32[]{:S(2)}, u32[]{:S(2)}) collective-permute-start(f32[256,256]{1,0:T(8,128)S(1)} %get-tuple-element.94), channel_id=1, source_target_pairs={{8,0},{9,1},{10,2},{11,3},{12,4},{13,5},{14,6},{15,7}} | collective-permute-start | bytes 786440 | tf_op jit(solution)/shard_map/ppermute | solution.py:428
  31.3 59.2 %collective-permute-start.20 = (f32[224,256]{1,0:T(8,128)S(1)}, f32[224,256]{1,0:T(8,128)S(1)}, u32[]{:S(2)}, u32[]{:S(2)}) collective-permute-start(f32[224,256]{1,0:T(8,128)S(1)} %get-tuple-element.92), channel_id=1, source_target_pairs={{8,0},{9,1},{10,2},{11,3},{12,4},{13,5},{14,6},{15,7}} | collective-permute-start | bytes 688136 | tf_op jit(solution)/shard_map/ppermute | solution.py:428
  34.3 68.4 %collective-permute-start.8 = (f32[224,256]{1,0:T(8,128)S(1)}, f32[224,256]{1,0:T(8,128)S(1)}, u32[]{:S(2)}, u32[]{:S(2)}) collective-permute-start(f32[224,256]{1,0:T(8,128)S(1)} %get-tuple-element.75), channel_id=1, source_target_pairs={{8,0},{9,1},{10,2},{11,3},{12,4},{13,5},{14,6},{15,7}} | collective-permute-start | bytes 688136 | tf_op jit(solution)/shard_map/ppermute | solution.py:428
  90.5 12.3 %collective-permute-start.10 = (f32[256,256]{1,0:T(8,128)S(1)}, f32[256,256]{1,0:T(8,128)S(1)}, u32[]{:S(2)}, u32[]{:S(2)}) collective-permute-start(f32[256,256]{1,0:T(8,128)S(1)} %get-tuple-element.79), channel_id=1, source_target_pairs={{8,0},{9,1},{10,2},{11,3},{12,4},{13,5},{14,6},{15,7}} | collective-permute-start | bytes 786440 | tf_op jit(solution)/shard_map/ppermute | solution.py:428
  91.8 14.9 %collective-permute-start.9 = (f32[256,256]{1,0:T(8,128)S(1)}, f32[256,256]{1,0:T(8,128)S(1)}, u32[]{:S(2)}, u32[]{:S(2)}) collective-permute-start(f32[256,256]{1,0:T(8,128)S(1)} %get-tuple-element.77), channel_id=1, source_target_pairs={{8,0},{9,1},{10,2},{11,3},{12,4},{13,5},{14,6},{15,7}} | collective-permute-start | bytes 786440 | tf_op jit(solution)/shard_map/ppermute | solution.py:428
  93.1 16.8 %collective-permute-start.11 = (f32[288,256]{1,0:T(8,128)S(1)}, f32[288,256]{1,0:T(8,128)S(1)}, u32[]{:S(2)}, u32[]{:S(2)}) collective-permute-start(f32[288,256]{1,0:T(8,128)S(1)} %stage.23), channel_id=1, source_target_pairs={{8,0},{9,1},{10,2},{11,3},{12,4},{13,5},{14,6},{15,7}} | collective-permute-start | bytes 884744 | tf_op jit(solution)/shard_map/ppermute | solution.py:428
  116.6 6.6 %collective-permute-start.33 = (f32[2,9,32,256]{3,2,1,0:T(8,128)S(1)}, f32[2,9,32,256]{3,2,1,0:T(8,128)S(1)}, u32[]{:S(2)}, u32[]{:S(2)}) collective-permute-start(f32[2,9,32,256]{3,2,1,0:T(8,128)S(1)} %get-tuple-element.117), channel_id=1, source_target_pairs={{0,1},{1,0},{2,3},{3,2},{4,5},{5,4},{6,7},{7,6},{8,9},{9,8},{10,11... | collective-permute-start | bytes 1769480 | tf_op jit(solution)/shard_map/ppermute | solution.py:553
  116.6 8.5 %collective-permute-start.25 = (f32[2,9,32,256]{3,2,1,0:T(8,128)S(1)}, f32[2,9,32,256]{3,2,1,0:T(8,128)S(1)}, u32[]{:S(2)}, u32[]{:S(2)}) collective-permute-start(f32[2,9,32,256]{3,2,1,0:T(8,128)S(1)} %get-tuple-element.108), channel_id=1, source_target_pairs={{0,1},{1,0},{2,3},{3,2},{4,5},{5,4},{6,7},{7,6},{8,9},{9,8},{10,11... | collective-permute-start | bytes 1769480 | tf_op jit(solution)/shard_map/ppermute | solution.py:553
  117.7 10.9 %collective-permute-start.37 = (f32[9,32,256]{2,1,0:T(8,128)S(1)}, f32[9,32,256]{2,1,0:T(8,128)S(1)}, u32[]{:S(2)}, u32[]{:S(2)}) collective-permute-start(f32[9,32,256]{2,1,0:T(8,128)S(1)} %get-tuple-element.121), channel_id=1, source_target_pairs={{0,2},{1,3},{6,4},{7,5},{8,10},{9,11},{14,12},{15,13},{16,18},{17,... | collective-permute-start | bytes 884744 | tf_op jit(solution)/shard_map/ppermute | solution.py:568
  121.8 13.0 %collective-permute-start.29 = (f32[9,32,256]{2,1,0:T(8,128)S(1)}, f32[9,32,256]{2,1,0:T(8,128)S(1)}, u32[]{:S(2)}, u32[]{:S(2)}) collective-permute-start(f32[9,32,256]{2,1,0:T(8,128)S(1)} %get-tuple-element.112), channel_id=1, source_target_pairs={{0,2},{1,3},{6,4},{7,5},{8,10},{9,11},{14,12},{15,13},{16,18},{17,... | collective-permute-start | bytes 884744 | tf_op jit(solution)/shard_map/ppermute | solution.py:568
  123.8 19.6 %collective-permute-start.35 = (f32[9,32,256]{2,1,0:T(8,128)S(1)}, f32[9,32,256]{2,1,0:T(8,128)S(1)}, u32[]{:S(2)}, u32[]{:S(2)}) collective-permute-start(f32[9,32,256]{2,1,0:T(8,128)S(1)} %get-tuple-element.120), channel_id=1, source_target_pairs={{0,2},{1,3},{6,4},{7,5},{8,10},{9,11},{14,12},{15,13},{16,18},{17,... | collective-permute-start | bytes 884744 | tf_op jit(solution)/shard_map/ppermute | solution.py:568
  125.8 21.7 %collective-permute-start.27 = (f32[9,32,256]{2,1,0:T(8,128)S(1)}, f32[9,32,256]{2,1,0:T(8,128)S(1)}, u32[]{:S(2)}, u32[]{:S(2)}) collective-permute-start(f32[9,32,256]{2,1,0:T(8,128)S(1)} %get-tuple-element.111), channel_id=1, source_target_pairs={{0,2},{1,3},{6,4},{7,5},{8,10},{9,11},{14,12},{15,13},{16,18},{17,... | collective-permute-start | bytes 884744 | tf_op jit(solution)/shard_map/ppermute | solution.py:568
  129.1 19.6 %collective-permute-start.38 = (f32[9,32,256]{2,1,0:T(8,128)S(1)}, f32[9,32,256]{2,1,0:T(8,128)S(1)}, u32[]{:S(2)}, u32[]{:S(2)}) collective-permute-start(f32[9,32,256]{2,1,0:T(8,128)S(1)} %relay.10), channel_id=1, source_target_pairs={{2,4},{3,5},{4,2},{5,3},{10,12},{11,13},{12,10},{13,11},{18,20},{1... | collective-permute-start | bytes 884744 | tf_op jit(solution)/shard_map/ppermute | solution.py:568
  135.5 15.2 %collective-permute-start.30 = (f32[9,32,256]{2,1,0:T(8,128)S(1)}, f32[9,32,256]{2,1,0:T(8,128)S(1)}, u32[]{:S(2)}, u32[]{:S(2)}) collective-permute-start(f32[9,32,256]{2,1,0:T(8,128)S(1)} %relay.7), channel_id=1, source_target_pairs={{2,4},{3,5},{4,2},{5,3},{10,12},{11,13},{12,10},{13,11},{18,20},{1... | collective-permute-start | bytes 884744 | tf_op jit(solution)/shard_map/ppermute | solution.py:568
  136.1 17.7 %collective-permute-start.34 = (f32[9,32,256]{2,1,0:T(8,128)S(1)}, f32[9,32,256]{2,1,0:T(8,128)S(1)}, u32[]{:S(2)}, u32[]{:S(2)}) collective-permute-start(f32[9,32,256]{2,1,0:T(8,128)S(1)} %get-tuple-element.119), channel_id=1, source_target_pairs={{0,2},{1,3},{6,4},{7,5},{8,10},{9,11},{14,12},{15,13},{16,18},{17,... | collective-permute-start | bytes 884744 | tf_op jit(solution)/shard_map/ppermute | solution.py:568
  143.4 21.4 %collective-permute-start.26 = (f32[9,32,256]{2,1,0:T(8,128)S(1)}, f32[9,32,256]{2,1,0:T(8,128)S(1)}, u32[]{:S(2)}, u32[]{:S(2)}) collective-permute-start(f32[9,32,256]{2,1,0:T(8,128)S(1)} %get-tuple-element.110), channel_id=1, source_target_pairs={{0,2},{1,3},{6,4},{7,5},{8,10},{9,11},{14,12},{15,13},{16,18},{17,... | collective-permute-start | bytes 884744 | tf_op jit(solution)/shard_map/ppermute | solution.py:568
  147.5 10.1 %collective-permute-start.36 = (f32[9,32,256]{2,1,0:T(8,128)S(1)}, f32[9,32,256]{2,1,0:T(8,128)S(1)}, u32[]{:S(2)}, u32[]{:S(2)}) collective-permute-start(f32[9,32,256]{2,1,0:T(8,128)S(1)} %relay.9), channel_id=1, source_target_pairs={{2,4},{3,5},{4,2},{5,3},{10,12},{11,13},{12,10},{13,11},{18,20},{1... | collective-permute-start | bytes 884744 | tf_op jit(solution)/shard_map/ppermute | solution.py:568
  149.4 14.1 %collective-permute-start.39 = (f32[9,32,256]{2,1,0:T(8,128)S(1)}, f32[9,32,256]{2,1,0:T(8,128)S(1)}, u32[]{:S(2)}, u32[]{:S(2)}) collective-permute-start(f32[9,32,256]{2,1,0:T(8,128)S(1)} %relay.11), channel_id=1, source_target_pairs={{4,6},{5,7},{2,0},{3,1},{12,14},{13,15},{10,8},{11,9},{20,22},{21,... | collective-permute-start | bytes 884744 | tf_op jit(solution)/shard_map/ppermute | solution.py:568
  150.7 14.2 %collective-permute-start.28 = (f32[9,32,256]{2,1,0:T(8,128)S(1)}, f32[9,32,256]{2,1,0:T(8,128)S(1)}, u32[]{:S(2)}, u32[]{:S(2)}) collective-permute-start(f32[9,32,256]{2,1,0:T(8,128)S(1)} %relay.6), channel_id=1, source_target_pairs={{2,4},{3,5},{4,2},{5,3},{10,12},{11,13},{12,10},{13,11},{18,20},{1... | collective-permute-start | bytes 884744 | tf_op jit(solution)/shard_map/ppermute | solution.py:568
  153.8 13.7 %collective-permute-start.31 = (f32[9,32,256]{2,1,0:T(8,128)S(1)}, f32[9,32,256]{2,1,0:T(8,128)S(1)}, u32[]{:S(2)}, u32[]{:S(2)}) collective-permute-start(f32[9,32,256]{2,1,0:T(8,128)S(1)} %relay.8), channel_id=1, source_target_pairs={{4,6},{5,7},{2,0},{3,1},{12,14},{13,15},{10,8},{11,9},{20,22},{21,... | collective-permute-start | bytes 884744 | tf_op jit(solution)/shard_map/ppermute | solution.py:568
  (11 other events, 165.0 us)
